TPU v7x, 32 devices: a whole 2x2x4 slice. The times are simulated.
32 devices in a mesh: ctx: 4 (over y, x), shard: 8 (over z, core).
Axes of the slice: x: 2, y: 2, z: 4, core: 2. Of those that a mesh axis runs over, the one named last changes fastest.
Arguments:
- hidden_in: bfloat16 [8, 512, 2048], P('shard', 'ctx'), may hold values from -6 to 6
- out_cot: bfloat16 [8, 512, 2048], P('shard', 'ctx'), may hold values from -6 to 6
- routes: int32 [8, 512, 8], P('shard', 'ctx'), may hold values from 0 to 31, all different within a row; in each aligned block of 128 rows (0 to 127, 128 to 255, ..., all dimensions but the last counted through in order) at most 34 rows name the same one
- block_pairs: int32 [4], replicated, may hold values from 0 to 3, each once
- norm_attn: bfloat16 [2048], P('shard'), may hold values from 0.099609375 to 1.8984375
- norm_moe: bfloat16 [2048], P('shard'), may hold values from 0.099609375 to 1.8984375
- q_gain: bfloat16 [128], P('shard'), may hold values from 0.25 to 1.75
- k_gain: bfloat16 [128], P('shard'), may hold values from 0.25 to 1.75
- w_query: bfloat16 [2048, 4096], P('shard'), may hold values from -0.125 to 0.125
- key_weight_matrix: bfloat16 [2048, 512], P('shard'), may hold values from -0.125 to 0.125
- value_weight_matrix: bfloat16 [2048, 512], P('shard'), may hold values from -0.125 to 0.125
- w_out: bfloat16 [4096, 2048], P('shard'), may hold values from -1.5 to 1.5
- w_router: bfloat16 [2048, 32], P('shard'), may hold values from -0.03125 to 0.03125
- expert_gate: bfloat16 [32, 2048, 768], P(('ctx', 'shard')), may hold values from -0.125 to 0.125
- expert_up: bfloat16 [32, 2048, 768], P(('ctx', 'shard')), may hold values from -0.125 to 0.125
- expert_down: bfloat16 [32, 768, 2048], P(('ctx', 'shard')), may hold values from -0.4375 to 0.4375
Outputs:
- block_out: bfloat16 [8, 512, 2048], P('shard', 'ctx')
- grad_in: float32 [8, 512, 2048], P('shard', 'ctx')
- grad_query: float32 [2048, 4096], P('shard')
- grad_key: float32 [2048, 512], P('shard')
- grad_value: float32 [2048, 512], P('shard')
- grad_out: float32 [4096, 2048], P('shard')
- grad_router: float32 [2048, 32], P('shard')
- grad_norm_attn: float32 [2048], P('shard')
- grad_norm_moe: float32 [2048], P('shard')
- grad_q_gain: float32 [128], P('shard')
- grad_k_gain: float32 [128], P('shard')
- grad_expert_gate: float32 [32, 2048, 768], P(('ctx', 'shard'))
- grad_expert_up: float32 [32, 2048, 768], P(('ctx', 'shard'))
- grad_expert_down: float32 [32, 768, 2048], P(('ctx', 'shard'))
Inputs may be any that keep to these rules, and one draw needn't show every extreme that they name: `routes`: each row names 8 different experts; within the 128 rows of one device no expert is named by more than 34 rows, a bound that some block reaches. A permutation: ctx index c holds causal blocks p and 7 - p of its sequence, p = block_pairs[c].
All inputs are finite; a program needn't handle non-finite values.
Results may differ from a plain program's by a relative error of at most 0.023.
Values may be sent and summed in bfloat16 or wider, within the bound.
No kernel may reach another device: no remote copies, remote signals or barrier semaphores. Data moves between devices by JAX's collectives and lax.ppermute only.
A program may use at most 256 MiB of HBM per device.

v0:
```python
import math

import jax
import jax.numpy as jnp
from jax import lax
from jax.sharding import PartitionSpec as P

MODEL_WIDTH = 2048
QUERY_HEADS = 32
KEY_VALUE_HEADS = 4
HEAD_SIZE = 128
FF = 768
TOP = 8


EPS = 1e-06
THETA = 1000000.0
MASKED = -1e30


def root_mean_square_norm(values_in, gain_vec):
    return (
        values_in
        * lax.rsqrt(jnp.mean(values_in * values_in, axis=-1, keepdims=True) + EPS)
        * gain_vec
    )


def rotary_embed(values_in, cosine_lookup, sine_lookup):
    half_width = values_in.shape[-1] // 2
    first_half = values_in[..., :half_width]
    second_half = values_in[..., half_width:]
    return jnp.concatenate(
        [
            first_half * cosine_lookup - second_half * sine_lookup,
            second_half * cosine_lookup + first_half * sine_lookup,
        ],
        axis=-1,
    )


def place_rows(pair_value, row_count, pair_count):
    row_ids = jnp.arange(row_count, dtype=jnp.int32)
    half_rows = row_count // 2
    block_ids = jnp.where(row_ids >= half_rows, 2 * pair_count - 1 - pair_value, pair_value)
    return block_ids * half_rows + row_ids % half_rows


def angles(positions, head_width):
    frequency = THETA ** (-(jnp.arange(head_width // 2, dtype=jnp.float32) * 2.0) / head_width)
    phase_angle = positions.astype(jnp.float32)[:, None] * frequency[None, :]
    return (jnp.cos(phase_angle)[:, None, :], jnp.sin(phase_angle)[:, None, :])


def slot_rows(route_block, expert_count):
    flat_ids = route_block.reshape(-1)
    expert_hits = (flat_ids[:, None] == jnp.arange(expert_count, dtype=jnp.int32)[None, :]).astype(
        jnp.int32
    )
    before = jnp.cumsum(expert_hits, axis=0) - expert_hits
    return (flat_ids, jnp.sum(before * expert_hits, axis=1))


def body(
    hidden_in,
    out_cot,
    routes,
    block_pairs,
    norm_attn,
    norm_moe,
    q_gain,
    k_gain,
    w_query,
    key_weight_matrix,
    value_weight_matrix,
    w_out,
    w_router,
    expert_gate,
    expert_up,
    expert_down,
):
    ctx_count = lax.axis_size("ctx")
    shard_count = lax.axis_size("shard")
    local_rows = hidden_in.shape[1]
    token_length = local_rows * ctx_count
    query_groups = QUERY_HEADS // KEY_VALUE_HEADS
    score_scale = 1.0 / math.sqrt(HEAD_SIZE)
    local_experts = expert_gate.shape[0]
    experts = local_experts * ctx_count * shard_count
    capacity = max(2, (17 * local_rows * TOP + 16 * experts - 1) // (16 * experts))
    gathered = (
        lax.all_gather(w_query, "shard", axis=0, tiled=True),
        lax.all_gather(key_weight_matrix, "shard", axis=0, tiled=True),
        lax.all_gather(value_weight_matrix, "shard", axis=0, tiled=True),
        lax.all_gather(w_out, "shard", axis=0, tiled=True),
        lax.all_gather(w_router, "shard", axis=0, tiled=True),
        lax.all_gather(norm_attn, "shard", axis=0, tiled=True),
        lax.all_gather(norm_moe, "shard", axis=0, tiled=True),
        lax.all_gather(q_gain, "shard", axis=0, tiled=True),
        lax.all_gather(k_gain, "shard", axis=0, tiled=True),
    )
    full_query, full_key, full_value, full_out, full_router = (
        gathered[0],
        gathered[1],
        gathered[2],
        gathered[3],
        gathered[4],
    )
    gain_attn = gathered[5].astype(jnp.float32)
    gain_moe = gathered[6].astype(jnp.float32)
    gain_query = gathered[7].astype(jnp.float32)
    key_gain_vector = gathered[8].astype(jnp.float32)
    inputs = hidden_in[0].astype(jnp.float32)
    pair_here = block_pairs[lax.axis_index("ctx")]
    pos_here = place_rows(pair_here, local_rows, ctx_count)
    pos_all = jax.vmap(lambda pair_value: place_rows(pair_value, local_rows, ctx_count))(
        block_pairs
    ).reshape(token_length)
    cosine_lookup, sine_lookup = angles(pos_here, HEAD_SIZE)
    allowed = pos_here[:, None] >= pos_all[None, :]
    normed_one_float, norm_one_back = jax.vjp(root_mean_square_norm, inputs, gain_attn)
    normed_one = normed_one_float.astype(jnp.bfloat16)
    query_pre = jnp.dot(normed_one, full_query, preferred_element_type=jnp.float32)
    key_projected = jnp.dot(normed_one, full_key, preferred_element_type=jnp.float32)
    value_rows = jnp.dot(normed_one, full_value, preferred_element_type=jnp.float32).astype(
        jnp.bfloat16
    )

    def shape_heads(query_in, key_input, gain_q, key_norm_gain):
        query_rotated = rotary_embed(
            root_mean_square_norm(query_in.reshape(local_rows, QUERY_HEADS, HEAD_SIZE), gain_q),
            cosine_lookup,
            sine_lookup,
        )
        key_rotated = rotary_embed(
            root_mean_square_norm(
                key_input.reshape(local_rows, KEY_VALUE_HEADS, HEAD_SIZE), key_norm_gain
            ),
            cosine_lookup,
            sine_lookup,
        )
        return (
            query_rotated.reshape(local_rows, QUERY_HEADS * HEAD_SIZE),
            key_rotated.reshape(local_rows, KEY_VALUE_HEADS * HEAD_SIZE),
        )

    (query_float, key_float), heads_back = jax.vjp(
        shape_heads, query_pre, key_projected, gain_query, key_gain_vector
    )
    query_rows = query_float.astype(jnp.bfloat16)
    keys_here = key_float.astype(jnp.bfloat16)
    key_rows_total, value_rows_total = (
        lax.all_gather(keys_here, "ctx", axis=0, tiled=True),
        lax.all_gather(value_rows, "ctx", axis=0, tiled=True),
    )
    query_head_split = query_rows.reshape(
        local_rows, KEY_VALUE_HEADS, query_groups, HEAD_SIZE
    ).transpose(1, 2, 0, 3)
    key_head_split = key_rows_total.reshape(token_length, KEY_VALUE_HEADS, HEAD_SIZE).transpose(
        1, 0, 2
    )
    value_head_split = value_rows_total.reshape(token_length, KEY_VALUE_HEADS, HEAD_SIZE).transpose(
        1, 0, 2
    )

    def head_scores(query_block, key_block):
        score = (
            jnp.einsum("gtd,ld->gtl", query_block, key_block, preferred_element_type=jnp.float32)
            * score_scale
        )
        return jnp.where(allowed[None], score, MASKED)

    def causal_attention(parts):
        query_block, key_block, value_block = parts
        score = head_scores(query_block, key_block)
        row_peak = jnp.max(score, axis=-1, keepdims=True)
        exponent = jnp.exp(score - row_peak)
        row_total = jnp.sum(exponent, axis=-1, keepdims=True)
        prob_low = (exponent / row_total).astype(jnp.bfloat16)
        mixed_block = jnp.einsum(
            "gtl,ld->gtd", prob_low, value_block, preferred_element_type=jnp.float32
        )
        return (mixed_block, (row_peak + jnp.log(row_total))[..., 0])

    mixed_heads, log_totals = lax.map(
        causal_attention, (query_head_split, key_head_split, value_head_split)
    )
    mixed_output_rows = (
        mixed_heads.transpose(2, 0, 1, 3)
        .reshape(local_rows, QUERY_HEADS * HEAD_SIZE)
        .astype(jnp.bfloat16)
    )
    residual = inputs + jnp.dot(mixed_output_rows, full_out, preferred_element_type=jnp.float32)
    normed_two_float, norm_two_back = jax.vjp(root_mean_square_norm, residual, gain_moe)
    normed_two = normed_two_float.astype(jnp.bfloat16)
    logits = jnp.dot(normed_two, full_router, preferred_element_type=jnp.float32)
    route_ids = routes[0]
    route_hits = route_ids[:, :, None] == jnp.arange(experts, dtype=jnp.int32)[None, None, :]
    chosen = jnp.sum(jnp.where(route_hits, logits[:, None, :], 0.0), axis=-1)
    chosen_peak = jnp.max(chosen, axis=-1, keepdims=True)
    chosen_exp = jnp.exp(chosen - chosen_peak)
    gate_weights = chosen_exp / jnp.sum(chosen_exp, axis=-1, keepdims=True)
    flat_ids, slot_index = slot_rows(route_ids, experts)
    target = flat_ids * capacity + slot_index
    copies = jnp.repeat(normed_two, TOP, axis=0)
    outgoing = (
        jnp.zeros((experts * capacity, MODEL_WIDTH), jnp.bfloat16)
        .at[target]
        .set(copies)
        .reshape(experts, capacity, MODEL_WIDTH)
    )
    exchanged = lax.all_to_all(outgoing, ("ctx", "shard"), split_axis=0, concat_axis=0, tiled=True)
    slot_count = exchanged.shape[1]
    grouped_queries = exchanged.reshape(-1, local_experts, slot_count, MODEL_WIDTH)
    gate_pre = jnp.einsum(
        "secd,edf->secf", grouped_queries, expert_gate, preferred_element_type=jnp.float32
    )
    up_pre = jnp.einsum(
        "secd,edf->secf", grouped_queries, expert_up, preferred_element_type=jnp.float32
    )
    hidden_act = (gate_pre * jax.nn.sigmoid(gate_pre) * up_pre).astype(jnp.bfloat16)
    result = jnp.einsum(
        "secf,efd->secd", hidden_act, expert_down, preferred_element_type=jnp.float32
    ).astype(jnp.bfloat16)
    returned = lax.all_to_all(
        result.reshape(exchanged.shape), ("ctx", "shard"), split_axis=0, concat_axis=0, tiled=True
    )
    kept_gate = gate_pre.reshape(-1, slot_count, FF)
    kept_up = up_pre.reshape(-1, slot_count, FF)
    picked = returned.reshape(experts * capacity, MODEL_WIDTH)[target].reshape(
        local_rows, TOP, MODEL_WIDTH
    )
    mixture = jnp.einsum("tk,tkd->td", gate_weights, picked, preferred_element_type=jnp.float32)
    block_out = (residual + mixture).astype(jnp.bfloat16)[None]
    upstream = out_cot[0].astype(jnp.float32)
    gate_grads = jnp.einsum("td,tkd->tk", upstream, picked, preferred_element_type=jnp.float32)
    slot_grads = (
        (gate_weights[:, :, None] * upstream[:, None, :])
        .astype(jnp.bfloat16)
        .reshape(local_rows * TOP, MODEL_WIDTH)
    )
    grad_buffer = (
        jnp.zeros((experts * capacity, MODEL_WIDTH), jnp.bfloat16)
        .at[target]
        .set(slot_grads)
        .reshape(experts, capacity, MODEL_WIDTH)
    )
    arrived = lax.all_to_all(grad_buffer, ("ctx", "shard"), split_axis=0, concat_axis=0, tiled=True)
    grouped_grad = arrived.reshape(-1, local_experts, capacity, MODEL_WIDTH)
    grouped_in = exchanged.reshape(-1, local_experts, capacity, MODEL_WIDTH)
    gate_pre = kept_gate.reshape(-1, local_experts, capacity, FF)
    up_pre = kept_up.reshape(-1, local_experts, capacity, FF)
    sigmoid_gate = jax.nn.sigmoid(gate_pre)
    silu_gate = gate_pre * sigmoid_gate
    hidden_act = (silu_gate * up_pre).astype(jnp.bfloat16)
    grad_down = jnp.einsum(
        "secf,secd->efd", hidden_act, grouped_grad, preferred_element_type=jnp.float32
    )
    grad_hidden = jnp.einsum(
        "secd,efd->secf", grouped_grad, expert_down, preferred_element_type=jnp.float32
    )
    grad_gate_pre = (
        grad_hidden * up_pre * sigmoid_gate * (1.0 + gate_pre * (1.0 - sigmoid_gate))
    ).astype(jnp.bfloat16)
    grad_up_pre = (grad_hidden * silu_gate).astype(jnp.bfloat16)
    grad_gate = jnp.einsum(
        "secd,secf->edf", grouped_in, grad_gate_pre, preferred_element_type=jnp.float32
    )
    grad_up = jnp.einsum(
        "secd,secf->edf", grouped_in, grad_up_pre, preferred_element_type=jnp.float32
    )
    grad_inputs = jnp.einsum(
        "secf,edf->secd", grad_gate_pre, expert_gate, preferred_element_type=jnp.float32
    )
    grad_inputs = grad_inputs + jnp.einsum(
        "secf,edf->secd", grad_up_pre, expert_up, preferred_element_type=jnp.float32
    )
    returned_grads = lax.all_to_all(
        grad_inputs.astype(jnp.bfloat16).reshape(arrived.shape),
        ("ctx", "shard"),
        split_axis=0,
        concat_axis=0,
        tiled=True,
    )
    row_grads = returned_grads.reshape(experts * capacity, MODEL_WIDTH)[target].reshape(
        local_rows, TOP, MODEL_WIDTH
    )
    mean_term = jnp.sum(gate_weights * gate_grads, axis=-1, keepdims=True)
    chosen_grads = gate_weights * (gate_grads - mean_term)
    logit_grads = jnp.sum(jnp.where(route_hits, chosen_grads[:, :, None], 0.0), axis=1).astype(
        jnp.bfloat16
    )
    normed_two_grad = jnp.sum(row_grads.astype(jnp.float32), axis=1) + jnp.dot(
        logit_grads, full_router.T, preferred_element_type=jnp.float32
    )
    residual_norm_grad, grad_gain_moe = norm_two_back(normed_two_grad)
    residual_grad = upstream + residual_norm_grad
    attn_grad = residual_grad.astype(jnp.bfloat16)
    mixed_gradient = jnp.dot(attn_grad, full_out.T, preferred_element_type=jnp.float32).astype(
        jnp.bfloat16
    )
    mixed_gradient_heads = mixed_gradient.reshape(
        local_rows, KEY_VALUE_HEADS, query_groups, HEAD_SIZE
    ).transpose(1, 2, 0, 3)

    def attend_back(parts):
        query_block, key_block, value_block, grad_block, log_block = parts
        score = head_scores(query_block, key_block)
        prob_rows = jnp.exp(score - log_block[..., None])
        prob_grads = jnp.einsum(
            "gtd,ld->gtl", grad_block, value_block, preferred_element_type=jnp.float32
        )
        centre = jnp.sum(prob_rows * prob_grads, axis=-1, keepdims=True)
        score_grads = (prob_rows * (prob_grads - centre)).astype(jnp.bfloat16)
        query_grads = (
            jnp.einsum("gtl,ld->gtd", score_grads, key_block, preferred_element_type=jnp.float32)
            * score_scale
        )
        key_grads = (
            jnp.einsum("gtl,gtd->ld", score_grads, query_block, preferred_element_type=jnp.float32)
            * score_scale
        )
        value_grads = jnp.einsum(
            "gtl,gtd->ld",
            prob_rows.astype(jnp.bfloat16),
            grad_block,
            preferred_element_type=jnp.float32,
        )
        return (query_grads, key_grads, value_grads)

    query_grad_heads, key_gradient_heads, value_gradient_heads = lax.map(
        attend_back,
        (query_head_split, key_head_split, value_head_split, mixed_gradient_heads, log_totals),
    )
    query_grad = query_grad_heads.transpose(2, 0, 1, 3).reshape(local_rows, QUERY_HEADS * HEAD_SIZE)
    key_gradient_total = key_gradient_heads.transpose(1, 0, 2).reshape(
        token_length, KEY_VALUE_HEADS * HEAD_SIZE
    )
    value_gradient_total = value_gradient_heads.transpose(1, 0, 2).reshape(
        token_length, KEY_VALUE_HEADS * HEAD_SIZE
    )
    key_grad, value_grad = (
        lax.psum_scatter(
            key_gradient_total.astype(jnp.bfloat16), "ctx", scatter_dimension=0, tiled=True
        ).astype(jnp.float32),
        lax.psum_scatter(
            value_gradient_total.astype(jnp.bfloat16), "ctx", scatter_dimension=0, tiled=True
        ).astype(jnp.float32),
    )
    query_pre_grad, key_pre_grad, grad_gain_query, grad_gain_key = heads_back(
        (query_grad, key_grad)
    )
    query_pre_grad = query_pre_grad.astype(jnp.bfloat16)
    key_pre_grad = key_pre_grad.astype(jnp.bfloat16)
    value_pre_grad = value_grad.astype(jnp.bfloat16)
    normed_one_grad = jnp.dot(query_pre_grad, full_query.T, preferred_element_type=jnp.float32)
    normed_one_grad = normed_one_grad + jnp.dot(
        key_pre_grad, full_key.T, preferred_element_type=jnp.float32
    )
    normed_one_grad = normed_one_grad + jnp.dot(
        value_pre_grad, full_value.T, preferred_element_type=jnp.float32
    )
    input_norm_grad, grad_gain_attn = norm_one_back(normed_one_grad)
    grad_in = (residual_grad + input_norm_grad)[None]
    grad_query = jnp.dot(normed_one.T, query_pre_grad, preferred_element_type=jnp.float32)
    grad_key = jnp.dot(normed_one.T, key_pre_grad, preferred_element_type=jnp.float32)
    grad_value = jnp.dot(normed_one.T, value_pre_grad, preferred_element_type=jnp.float32)
    grad_out = jnp.dot(mixed_output_rows.T, attn_grad, preferred_element_type=jnp.float32)
    grad_router = jnp.dot(normed_two.T, logit_grads, preferred_element_type=jnp.float32)
    summed = (
        lax.psum_scatter(
            grad_query.astype(jnp.bfloat16), "shard", scatter_dimension=0, tiled=True
        ).astype(jnp.float32),
        lax.psum_scatter(
            grad_key.astype(jnp.bfloat16), "shard", scatter_dimension=0, tiled=True
        ).astype(jnp.float32),
        lax.psum_scatter(
            grad_value.astype(jnp.bfloat16), "shard", scatter_dimension=0, tiled=True
        ).astype(jnp.float32),
        lax.psum_scatter(
            grad_out.astype(jnp.bfloat16), "shard", scatter_dimension=0, tiled=True
        ).astype(jnp.float32),
        lax.psum_scatter(
            grad_router.astype(jnp.bfloat16), "shard", scatter_dimension=0, tiled=True
        ).astype(jnp.float32),
        lax.psum_scatter(
            grad_gain_attn.astype(jnp.bfloat16), "shard", scatter_dimension=0, tiled=True
        ).astype(jnp.float32),
        lax.psum_scatter(
            grad_gain_moe.astype(jnp.bfloat16), "shard", scatter_dimension=0, tiled=True
        ).astype(jnp.float32),
        lax.psum_scatter(
            grad_gain_query.astype(jnp.bfloat16), "shard", scatter_dimension=0, tiled=True
        ).astype(jnp.float32),
        lax.psum_scatter(
            grad_gain_key.astype(jnp.bfloat16), "shard", scatter_dimension=0, tiled=True
        ).astype(jnp.float32),
    )
    owned = (
        lax.psum(summed[0].astype(jnp.bfloat16), "ctx").astype(jnp.float32),
        lax.psum(summed[1].astype(jnp.bfloat16), "ctx").astype(jnp.float32),
        lax.psum(summed[2].astype(jnp.bfloat16), "ctx").astype(jnp.float32),
        lax.psum(summed[3].astype(jnp.bfloat16), "ctx").astype(jnp.float32),
        lax.psum(summed[4].astype(jnp.bfloat16), "ctx").astype(jnp.float32),
        lax.psum(summed[5].astype(jnp.bfloat16), "ctx").astype(jnp.float32),
        lax.psum(summed[6].astype(jnp.bfloat16), "ctx").astype(jnp.float32),
        lax.psum(summed[7].astype(jnp.bfloat16), "ctx").astype(jnp.float32),
        lax.psum(summed[8].astype(jnp.bfloat16), "ctx").astype(jnp.float32),
    )
    return (
        block_out,
        grad_in,
        owned[0],
        owned[1],
        owned[2],
        owned[3],
        owned[4],
        owned[5],
        owned[6],
        owned[7],
        owned[8],
        grad_gate,
        grad_up,
        grad_down,
    )


def solution(mesh):
    placed = (
        P("shard", "ctx", None),
        P("shard", "ctx", None),
        P("shard", "ctx", None),
        P(),
        P("shard"),
        P("shard"),
        P("shard"),
        P("shard"),
        P("shard", None),
        P("shard", None),
        P("shard", None),
        P("shard", None),
        P("shard", None),
        P(("ctx", "shard"), None, None),
        P(("ctx", "shard"), None, None),
        P(("ctx", "shard"), None, None),
    )
    return jax.shard_map(
        body,
        mesh=mesh,
        in_specs=placed,
        out_specs=(
            P("shard", "ctx", None),
            P("shard", "ctx", None),
            P("shard", None),
            P("shard", None),
            P("shard", None),
            P("shard", None),
            P("shard", None),
            P("shard"),
            P("shard"),
            P("shard"),
            P("shard"),
            P(("ctx", "shard"), None, None),
            P(("ctx", "shard"), None, None),
            P(("ctx", "shard"), None, None),
        ),
        check_vma=False,
    )
```

profile of v0, /device:TPU:0, one launch (start us, length us, event | category | flops | bytes accessed | tf_op | source)
XLA Modules:
  0.0 1687.6 jit_solution(4547270104600597098)
XLA Ops:
  10.4 13.5 all-gather
  25.7 14.9 all-reduce.11
  70.2 11.7 all_gather.38
  96.9 127.3 %all-gather.7.cloned.1.call-done = bf16[2048,4096]{1,0:T(8,128)(2,1)} async-done(((bf16[256,4096]{1,0:T(8,128)(2,1)}), bf16[2048,4096]{1,0:T(8,128)(2,1)}) %all-gather.7.cloned.1.call-update) | async-done | bytes 16777232 | tf_op jit(solution)/shard_map/all_gather | solution.py:92
  224.2 22.0 %copy.82 = bf16[4096,2048]{1,0:T(8,128)(2,1)} copy(bf16[4096,2048]{0,1:T(8,128)(2,1)} %bitcast.386) | data formatting | bytes 33554432 | tf_op jit(solution)/shard_map/dot_general | solution.py:123
  259.4 19.1 %while.28 = (s32[]{:T(128)}, bf16[4,8,128,128]{2,3,1,0:T(8,128)(2,1)}, f32[4,8,128]{2,1,0:T(8,128)S(1)}, bf16[4,8,128,128]{3,2,1,0:T(8,128)(2,1)}, bf16[4,512,12...) while((s32[]{:T(128)}, ...), condition=%wide.region_6.7_spmd.clone, body=%wide.region_3.6_spmd.clone.sunk | while | flops 274791424 | bytes 7639649 | solution.py:185
  278.5 96.5 %all-gather.13.cloned.1.call-done = bf16[4096,2048]{1,0:T(8,128)(2,1)} async-done(((bf16[512,2048]{1,0:T(8,128)(2,1)}), bf16[4096,2048]{1,0:T(8,128)(2,1)}) %all-gather.13.cloned.1.call-update) | async-done | bytes 16777232 | tf_op jit(solution)/shard_map/all_gather | solution.py:95
  402.6 120.5 %all_to_all.20 = bf16[32,34,2048]{2,1,0:T(8,128)(2,1)S(1)} all-to-all(bf16[32,34,2048]{2,1,0:T(8,128)(2,1)} %reshape.506), channel_id=1, replica_groups=mesh['ctx'=4,'shard'=8] {'ctx','shard'}, dimensions={0} | all-to-all | bytes 8912896 | tf_op jit(solution)/shard_map/all_to_all | solution.py:212
  545.1 122.3 %all_gather.43 = bf16[2048,32]{0,1:T(8,128)(2,1)S(1)} all-gather(bf16[256,32]{0,1:T(8,128)(2,1)S(1)} %copy-done.45), channel_id=1, replica_groups=mesh['ctx'=4,'shard'=8] {'shard'}, dimensions={0}, use_global_device_ids=true | all-gather | bytes 147456 | tf_op jit(solution)/shard_map/all_gather | solution.py:96
  678.2 11.6 gather_fusion
  712.5 122.4 %all_to_all.21 = bf16[32,34,2048]{2,1,0:T(8,128)(2,1)S(1)} all-to-all(bf16[32,34,2048]{2,1,0:T(8,128)(2,1)} %reshape.513), channel_id=1, replica_groups=mesh['ctx'=4,'shard'=8] {'ctx','shard'}, dimensions={0} | all-to-all | bytes 8912896 | tf_op jit(solution)/shard_map/all_to_all | solution.py:248
  864.9 112.5 %all-to-all-done.3 = bf16[32,34,2048]{2,1,0:T(8,128)(2,1)} async-done(((bf16[32,34,2048]{2,1,0:T(8,128)(2,1)}), bf16[32,34,2048]{2,1,0:T(8,128)(2,1)}, u32[]{:S(2)}, u32[]{:S(2)}) %all-to-all-start.3) | async-done | bytes 4456480 | tf_op jit(solution)/shard_map/all_to_all | solution.py:278
  984.7 11.6 gather_fusion.1
  1003.7 11.8 fusion.86
  1017.2 40.4 %while.29 = (s32[]{:T(128)}, f32[4,8,128,128]{3,2,1,0:T(8,128)}, bf16[4,512,128]{1,2,0:T(8,128)(2,1)}, bf16[4,512,128]{1,2,0:T(8,128)(2,1)}, bf16[4,8,128,128]{3...) while((s32[]{:T(128)}, f32[4,8,128,128]{3,2,1,0:T(8,128)}, ...), condition=%wide.region_22.23_spmd.clone, body=%wide.region_20.22_spmd.clone.sunk | while | flops 676133888 | bytes 18771576 | solution.py:331
  1062.0 20.6 %reduce-scatter.22.cloned.1.call-done = bf16[128,512]{1,0:T(8,128)(2,1)} async-done(((bf16[512,512]{1,0:T(8,128)(2,1)}), bf16[128,512]{1,0:T(8,128)(2,1)}) %reduce-scatter.22.cloned.1.call-update) | async-done | bytes 131088
  1086.3 24.7 %reduce-scatter.24.cloned.1.call-done = bf16[128,512]{1,0:T(8,128)(2,1)} async-done(((bf16[512,512]{1,0:T(8,128)(2,1)}), bf16[128,512]{1,0:T(8,128)(2,1)}) %reduce-scatter.24.cloned.1.call-update) | async-done | bytes 131088
  1161.6 25.1 %reduce-scatter.16.cloned.1.call-done = bf16[256,512]{1,0:T(8,128)(2,1)} async-done(((bf16[2048,512]{1,0:T(8,128)(2,1)}), bf16[256,512]{1,0:T(8,128)(2,1)}) %reduce-scatter.16.cloned.1.call-update) | async-done | bytes 262160 | tf_op jit(solution)/shard_map/reduce_scatter | solution.py:377
  1186.7 169.3 %reduce-scatter.18.cloned.1.call-done = bf16[512,2048]{1,0:T(8,128)(2,1)} async-done(((bf16[4096,2048]{1,0:T(8,128)(2,1)}), bf16[512,2048]{1,0:T(8,128)(2,1)}) %reduce-scatter.18.cloned.1.call-update) | async-done | bytes 2097168 | tf_op jit(solution)/shard_map/reduce_scatter | solution.py:380
  1356.0 168.9 %reduce-scatter.12.cloned.1.call-done = bf16[256,4096]{1,0:T(8,128)(2,1)} async-done(((bf16[2048,4096]{1,0:T(8,128)(2,1)}), bf16[256,4096]{1,0:T(8,128)(2,1)}) %reduce-scatter.12.cloned.1.call-update) | async-done | bytes 2097168 | tf_op jit(solution)/shard_map/reduce_scatter | solution.py:371
  1535.1 11.5 fusion.140
  1550.3 14.2 all-reduce.10
  1564.8 17.8 %all-reduce.12 = (bf16[256,32]{0,1:T(8,128)(2,1)S(1)}, bf16[256]{0:T(256)(128)(2,1)S(1)}, bf16[256]{0:T(256)(128)(2,1)S(1)}, bf16[16]{0:T(256)(128)(2,1)S(1)}, bf16[16]{0:T(256)(128)(2,1)S(1)}) all-reduce(bf16[256,32]{0,1:T(8,128)(2,1)} %reduce-scatter.20.cloned.1.call-done, ...), channel_id=1, replica_groups=mesh['ctx'=4,'shard'=8] {'ctx'}, use_global_device_ids=true, to_apply=%region_37.38 | all-reduce | flops 8736 | bytes 34944 | tf_op jit(solution)/shard_map/psum | solution.py:404
  1586.6 85.3 %all-reduce.16.cloned.1.call-done = (bf16[256,4096]{1,0:T(8,128)(2,1)}, bf16[256,512]{1,0:T(8,128)(2,1)}, bf16[256,512]{1,0:T(8,128)(2,1)}, bf16[512,2048]{1,0:T(8,128)(2,1)}) async-done(((bf16[256,4096]{1,0:T(8,128)(2,1)}, bf16[256,512]{1,0:T(8,128)(2,1)}, bf16[256,512]{1,0:T(8,128)(2,1)}, bf16[512,2048]{1,0:T(8,128)(2,1)}), (bf16[256,4096]{1,0:T(8,128)(2,1)}, bf16[256,512]{1,0:T(8,128)(2,1)}, ...) | async-done | bytes 4718608 | tf_op jit(solution)/shard_map/psum | solution.py:400
  (359 shorter events, 332.6 us)
Async XLA Ops:
  7.2 528.2 %copy-start = (bf16[1,768,2048]{2,1,0:T(8,128)(2,1)S(1)}, bf16[1,768,2048]{2,1,0:T(8,128)(2,1)}, u32[]{:S(2)}) copy-start(bf16[1,768,2048]{2,1,0:T(8,128)(2,1)} %param.35) | copy-start | bytes 9437188
  7.3 51.4 %copy-start.55 = (s32[4]{0:T(128)S(1)}, s32[4]{0:T(128)}, u32[]{:S(2)}) copy-start(s32[4]{0:T(128)} %param.23) | copy-start | bytes 52
  7.3 55.6 %all-gather.9.cloned.1.call-start = ((), (), s32[]{:S(2)}) async-start(), calls=%async_computation.12 | async-start | bytes 2359296 | tf_op jit(solution)/shard_map/all_gather | solution.py:93
  8.0 76.1 %all-gather.11.cloned.1.call-start = ((), (), s32[]{:S(2)}) async-start(), calls=%async_computation.13 | async-start | bytes 2359296 | tf_op jit(solution)/shard_map/all_gather | solution.py:94
  8.8 215.5 %all-gather.7.cloned.1.call-start = ((), (), s32[]{:S(2)}) async-start(), calls=%async_computation.11 | async-start | bytes 18874368 | tf_op jit(solution)/shard_map/all_gather | solution.py:92
  9.5 365.5 %all-gather.13.cloned.1.call-start = ((), (), s32[]{:S(2)}) async-start(), calls=%async_computation.14 | async-start | bytes 18874368 | tf_op jit(solution)/shard_map/all_gather | solution.py:95
  23.9 222.3 %copy-start.31 = (f32[8,1,256]{2,1,0:T(1,128)}, f32[8,1,256]{2,1,0:T(1,128)S(1)}, u32[]{:S(2)}) copy-start(f32[8,1,256]{2,1,0:T(1,128)S(1)} %convert_element_type.303) | copy-start | bytes 24580
  40.6 214.2 %copy-start.50 = (f32[128]{0:T(128)}, f32[128]{0:T(128)S(1)}, u32[]{:S(2)}) copy-start(f32[128]{0:T(128)S(1)} %convert_element_type.246) | copy-start | bytes 1540
  62.0 184.2 %copy-start.43 = (f32[128]{0:T(128)}, f32[128]{0:T(128)S(1)}, u32[]{:S(2)}) copy-start(f32[128]{0:T(128)S(1)} %fusion.128) | copy-start | bytes 1540
  62.8 192.4 %copy-start.27 = (f32[128,64]{0,1:T(8,128)}, f32[128,64]{0,1:T(8,128)S(1)}, u32[]{:S(2)}) copy-start(f32[128,64]{0,1:T(8,128)S(1)} %get-tuple-element.295) | copy-start | bytes 98308
  62.8 192.4 %copy-start.29 = (f32[128,64]{0,1:T(8,128)}, f32[128,64]{0,1:T(8,128)S(1)}, u32[]{:S(2)}) copy-start(f32[128,64]{0,1:T(8,128)S(1)} %get-tuple-element.296) | copy-start | bytes 98308
  402.6 120.5 %copy-start.58 = (bf16[1,2048,768]{2,1,0:T(8,128)(2,1)S(1)}, bf16[1,2048,768]{2,1,0:T(8,128)(2,1)}, u32[]{:S(2)}) copy-start(bf16[1,2048,768]{2,1,0:T(8,128)(2,1)} %param.34) | copy-start | bytes 9437188
  541.3 129.5 %all-to-all-start.1 = ((bf16[32,34,2048]{2,1,0:T(8,128)(2,1)}), bf16[32,34,2048]{2,1,0:T(8,128)(2,1)}, u32[]{:S(2)}, u32[]{:S(2)}) async-start(bf16[32,34,2048]{2,1,0:T(8,128)(2,1)} %convolution_convert_fusion.3), calls=%async_computation.1 | async-start | bytes 10485760 | tf_op jit(solution)/shard_map/all_to_all | solution.py:225
  712.4 122.4 %copy-start.16 = (f32[32,34,768]{2,1,0:T(8,128)S(1)}, f32[32,34,768]{2,1,0:T(8,128)}, u32[]{:S(2)}) copy-start(f32[32,34,768]{2,1,0:T(8,128)} %copy-done.15) | copy-start | bytes 10027012
  712.4 122.4 %copy-start.18 = (f32[32,34,768]{2,1,0:T(8,128)S(1)}, f32[32,34,768]{2,1,0:T(8,128)}, u32[]{:S(2)}) copy-start(f32[32,34,768]{2,1,0:T(8,128)} %copy-done.17) | copy-start | bytes 10027012
  856.4 121.0 %all-to-all-start.3 = ((bf16[32,34,2048]{2,1,0:T(8,128)(2,1)}), bf16[32,34,2048]{2,1,0:T(8,128)(2,1)}, u32[]{:S(2)}, u32[]{:S(2)}) async-start(bf16[32,34,2048]{2,1,0:T(8,128)(2,1)} %add_convert_fusion), calls=%async_computation.3 | async-start | bytes 10485760 | tf_op jit(solution)/shard_map/all_to_all | solution.py:278
  860.0 222.7 %reduce-scatter.22.cloned.1.call-start = ((), (), s32[]{:S(2)}) async-start(), calls=%async_computation.20 | async-start | bytes 655360
  1059.8 51.2 %reduce-scatter.24.cloned.1.call-start = ((), (), s32[]{:S(2)}) async-start(), calls=%async_computation.21 | async-start | bytes 655360
  1061.9 99.6 %reduce-scatter.14.cloned.1.call-start = ((), (), s32[]{:S(2)}) async-start(), calls=%async_computation.16 | async-start | bytes 2359296 | tf_op jit(solution)/shard_map/reduce_scatter | solution.py:374
  1086.3 100.4 %reduce-scatter.16.cloned.1.call-start = ((), (), s32[]{:S(2)}) async-start(), calls=%async_computation.17 | async-start | bytes 2359296 | tf_op jit(solution)/shard_map/reduce_scatter | solution.py:377
  1114.1 241.9 %reduce-scatter.18.cloned.1.call-start = ((), (), s32[]{:S(2)}) async-start(), calls=%async_computation.18 | async-start | bytes 18874368 | tf_op jit(solution)/shard_map/reduce_scatter | solution.py:380
  1123.6 401.3 %reduce-scatter.12.cloned.1.call-start = ((), (), s32[]{:S(2)}) async-start(), calls=%async_computation.15 | async-start | bytes 18874368 | tf_op jit(solution)/shard_map/reduce_scatter | solution.py:371
  1141.5 423.3 %reduce-scatter.20.cloned.1.call-start = ((), (), s32[]{:S(2)}) async-start(), calls=%async_computation.19 | async-start | bytes 147456 | tf_op jit(solution)/shard_map/reduce_scatter | solution.py:383
  1143.9 528.0 %all-reduce.16.cloned.1.call-start = ((), (), s32[]{:S(2)}) async-start(), calls=%async_computation.22 | async-start | bytes 9437184 | tf_op jit(solution)/shard_map/psum | solution.py:400
  (57 other events, 651.4 us)
Sparse Core Ops, SparseCore 0:
  9.7 32.1 all-gather.8
  43.4 28.6 all-gather.10
  73.7 150.5 all-gather.6
  225.7 149.2 all-gather.12
  1059.9 22.6 reduce-scatter.21
  1085.9 25.0 reduce-scatter.23
  1113.9 35.8 reduce-scatter.13
  1152.1 34.5 reduce-scatter.15
  1189.0 166.8 reduce-scatter.17
  1358.2 166.6 reduce-scatter.11
  1527.7 29.0 reduce-scatter.19
  1560.4 111.5 all-reduce.15
where the time goes:
time: 1690 us
  waiting for transfers between devices  833 us (49%)
  blocking collectives  455 us (27%)
  matrix products  201 us (12%)
  local copies, waits for them, and re-layouts  115 us (7%)
  other arithmetic  56.5 us (3%)
  between operations  18.3 us (1%)
    reduce_scatter x1, waiting for transfers between devices, body(): lax.psum_scatter(grad_out.astype(jnp.bfloat16), 'shard', scatter_dimensio...  169 us
    reduce_scatter x1, waiting for transfers between devices, body(): lax.psum_scatter(grad_query.astype(jnp.bfloat16), 'shard', scatter_dimens...  169 us
    all_gather x1, waiting for transfers between devices, body(): lax.all_gather(w_query, 'shard', axis=0, tiled=True)  127 us
    all_to_all x1, blocking collectives, body(): lax.all_to_all(grad_buffer, ('ctx', 'shard'), split_axis=0, concat_axis=0...  122 us
    all_gather x1, blocking collectives, body(): lax.all_gather(w_router, 'shard', axis=0, tiled=True)  122 us
    all_to_all x1, blocking collectives, body(): lax.all_to_all(outgoing, ('ctx', 'shard'), split_axis=0, concat_axis=0, t...  120 us
    all_to_all x1, waiting for transfers between devices, body(): lax.all_to_all(grad_inputs.astype(jnp.bfloat16).reshape(arrived.shape), (...  113 us
    all_gather x1, waiting for transfers between devices, body(): lax.all_gather(w_out, 'shard', axis=0, tiled=True)  96.5 us
  transfers between devices with their start and end apart: 14, of which 9 were waited for; matrix products, arithmetic and copies ran while one was open for 10% of the time, Pallas kernels for 0%

commit v1 on v0

v1 whole, which is shorter than its diff:
```python
import math

import jax
import jax.numpy as jnp
from jax import lax
from jax.experimental import pallas as pl
from jax.experimental.pallas import tpu as pltpu
from jax.sharding import PartitionSpec as P


QUERY_HEADS = 32
KEY_VALUE_HEADS = 4
HEAD_SIZE = 128
TOP = 8

EPS = 1e-06
THETA = 1000000.0
MASKED = -1e30
LANES = 128
VMEM_LIMIT = 58 * 1024 * 1024
F32 = jnp.float32
BF16 = jnp.bfloat16


def dot(a, b, ca=1, cb=0):
    return lax.dot_general(a, b, (((ca,), (cb,)), ((), ())), preferred_element_type=F32)


def params(**kw):
    return pltpu.CompilerParams(vmem_limit_bytes=VMEM_LIMIT, **kw)


def inverse_rms(v):
    return lax.rsqrt(jnp.mean(v * v, axis=-1, keepdims=True) + EPS)


def turn(v, cosine, sine):
    return v * cosine + pltpu.roll(v, HEAD_SIZE // 2, 1) * sine


def head(pre, gain, cosine, sine):
    return turn(pre * inverse_rms(pre) * gain, cosine, sine).astype(BF16)


def head_back(grad, pre, gain, cosine, sine):
    g = turn(grad, cosine, -sine)
    r = inverse_rms(pre)
    n = pre * r
    scaled = g * gain
    back = r * (scaled - n * jnp.mean(n * scaled, axis=-1, keepdims=True))
    return back.astype(BF16), jnp.sum(g * n, axis=0, keepdims=True)


def attend_forward(qkv, heads, gains, cosine, sine, pos_col, pos_row):
    n = qkv.shape[0]
    hs = HEAD_SIZE
    factor = math.log2(math.e) / math.sqrt(HEAD_SIZE)

    def kernel(q_ref, k_ref, v_ref, gain_ref, cos_ref, sin_ref, pc_ref, pr_ref, out_ref, tot_ref, key_s, val_s, bias_s):
        h = pl.program_id(0)

        @pl.when(h == 0)
        def _():
            key_s[...] = head(k_ref[...], gain_ref[1:2, :], cos_ref[...], sin_ref[...])
            val_s[:, :hs] = v_ref[...].astype(BF16)
            val_s[:, hs:] = jnp.ones((n, hs), BF16)
            bias_s[...] = jnp.where(pc_ref[...] >= pr_ref[...], 0.0, MASKED)
            tot_ref[...] = jnp.zeros_like(tot_ref)

        q = head(q_ref[...], gain_ref[0:1, :], cos_ref[...], sin_ref[...])
        e = jnp.exp2(dot(q, key_s[...], 1, 1) * factor + bias_s[...]).astype(BF16)
        both = dot(e, val_s[...])
        inverse = 1.0 / both[:, hs:]
        out_ref[...] = (both[:, :hs] * inverse).astype(BF16)
        lane = lax.broadcasted_iota(jnp.int32, (n, hs), 1)
        tot_ref[...] = jnp.where(lane == h, inverse, tot_ref[...])

    full = lambda a: pl.BlockSpec(a.shape, lambda h: (0, 0))
    return pl.pallas_call(
        kernel,
        grid=(heads,),
        in_specs=[
            pl.BlockSpec((n, hs), lambda h: (0, h)),
            pl.BlockSpec((n, hs), lambda h: (0, heads)),
            pl.BlockSpec((n, hs), lambda h: (0, heads + 1)),
            full(gains),
            full(cosine),
            full(sine),
            full(pos_col),
            full(pos_row),
        ],
        out_specs=[pl.BlockSpec((n, hs), lambda h: (0, h)), pl.BlockSpec((n, hs), lambda h: (0, 0))],
        out_shape=[
            jax.ShapeDtypeStruct((n, heads * hs), BF16),
            jax.ShapeDtypeStruct((n, hs), F32),
        ],
        scratch_shapes=[pltpu.VMEM((n, hs), BF16), pltpu.VMEM((n, 2 * hs), BF16), pltpu.VMEM((n, n), F32)],
        compiler_params=params(),
        name="attend_forward",
    )(qkv, qkv, qkv, gains, cosine, sine, pos_col, pos_row)


def attend_backward(qkv, d_mix, mix, totals, heads, gains, cosine, sine, pos_col, pos_row):
    n = qkv.shape[0]
    hs = HEAD_SIZE
    scale = 1.0 / math.sqrt(HEAD_SIZE)
    factor = math.log2(math.e) / math.sqrt(HEAD_SIZE)

    def kernel(q_ref, k_ref, v_ref, dm_ref, mix_ref, tot_ref, gain_ref, cos_ref, sin_ref, pc_ref, pr_ref, dq_ref, dkv_ref, gg_ref, key_s, val_s, dk_s, dv_s, bias_s):
        h = pl.program_id(0)

        @pl.when(h == 0)
        def _():
            key_s[...] = head(k_ref[...], gain_ref[1:2, :], cos_ref[...], sin_ref[...])
            val_s[...] = v_ref[...].astype(BF16)
            bias_s[...] = jnp.where(pc_ref[...] >= pr_ref[...], 0.0, MASKED)
            dk_s[...] = jnp.zeros_like(dk_s)
            dv_s[...] = jnp.zeros_like(dv_s)
            gg_ref[...] = jnp.zeros_like(gg_ref)

        pre = q_ref[...]
        q = head(pre, gain_ref[0:1, :], cos_ref[...], sin_ref[...])
        dm = dm_ref[...]
        lane = lax.broadcasted_iota(jnp.int32, (n, hs), 1)
        inverse = jnp.sum(jnp.where(lane == h, tot_ref[...], 0.0), axis=-1, keepdims=True)
        centre = jnp.sum(dm.astype(F32) * mix_ref[...].astype(F32), axis=-1, keepdims=True)
        p = jnp.exp2(dot(q, key_s[...], 1, 1) * factor + bias_s[...]) * inverse
        dp = dot(dm, val_s[...], 1, 1)
        ds = (p * (dp - centre)).astype(BF16)
        dq = dot(ds, key_s[...]) * scale
        dk_s[...] += dot(ds, q, 0, 0)
        dv_s[...] += dot(p.astype(BF16), dm, 0, 0)
        back, gg = head_back(dq, pre, gain_ref[0:1, :], cos_ref[...], sin_ref[...])
        dq_ref[...] = back
        gg_ref[0:1, :] += gg

        @pl.when(h == heads - 1)
        def _():
            back, gg = head_back(
                dk_s[...] * scale, k_ref[...], gain_ref[1:2, :], cos_ref[...], sin_ref[...]
            )
            dkv_ref[:, :hs] = back
            dkv_ref[:, hs:] = dv_s[...].astype(BF16)
            gg_ref[1:2, :] = gg

    full = lambda a: pl.BlockSpec(a.shape, lambda h: (0, 0))
    col = pl.BlockSpec((n, hs), lambda h: (0, h))
    return pl.pallas_call(
        kernel,
        grid=(heads,),
        in_specs=[
            col,
            pl.BlockSpec((n, hs), lambda h: (0, heads)),
            pl.BlockSpec((n, hs), lambda h: (0, heads + 1)),
            col,
            col,
            full(totals),
            full(gains),
            full(cosine),
            full(sine),
            full(pos_col),
            full(pos_row),
        ],
        out_specs=[col, pl.BlockSpec((n, 2 * hs), lambda h: (0, 0)), pl.BlockSpec((8, hs), lambda h: (0, 0))],
        out_shape=[
            jax.ShapeDtypeStruct((n, heads * hs), BF16),
            jax.ShapeDtypeStruct((n, 2 * hs), BF16),
            jax.ShapeDtypeStruct((8, hs), F32),
        ],
        scratch_shapes=[
            pltpu.VMEM((n, hs), BF16),
            pltpu.VMEM((n, hs), BF16),
            pltpu.VMEM((n, hs), F32),
            pltpu.VMEM((n, hs), F32),
            pltpu.VMEM((n, n), F32),
        ],
        compiler_params=params(),
        name="attend_backward",
    )(qkv, qkv, qkv, d_mix, mix, totals, gains, cosine, sine, pos_col, pos_row)


def expert_piece(x, cot, router, wg, wu, wd, me, experts, back_extra):
    r, d = x.shape
    f = wg.shape[1]
    extra = cot.shape[1] - d

    def kernel(me_ref, x_ref, cot_ref, router_ref, wg_ref, wu_ref, wd_ref,
               mixed_ref, back_ref, hid_ref, deo_ref, dg_ref, du_ref):
        own = me_ref[0]
        xv = x_ref[...]
        lane = lax.broadcasted_iota(jnp.int32, (r, extra), 1)
        mask = (cot_ref[:, d:].astype(F32) > 0.5) & (lane < experts)
        kept = jnp.where(mask, dot(xv, router_ref[...]), MASKED)
        e = jnp.where(mask, jnp.exp(kept - jnp.max(kept, axis=-1, keepdims=True)), 0.0)
        total = jnp.sum(e, axis=-1, keepdims=True)
        gate = jnp.sum(jnp.where(lane == own, e, 0.0), axis=-1, keepdims=True) / jnp.where(total > 0.0, total, 1.0)
        gp = dot(xv, wg_ref[...])
        up = dot(xv, wu_ref[...])
        sig = jax.nn.sigmoid(gp)
        silu = gp * sig
        hid = (silu * up).astype(BF16)
        hid_ref[...] = hid
        eo = dot(hid, wd_ref[...]).astype(BF16).astype(F32)
        dout = cot_ref[:, :d].astype(F32)
        dgr = jnp.sum(dout * eo, axis=-1, keepdims=True)
        mixed_ref[...] = (gate * eo).astype(BF16)
        deo = (gate * dout).astype(BF16)
        deo_ref[...] = deo
        dh = dot(deo, wd_ref[...], 1, 1)
        dg = (dh * up * sig * (1.0 + gp * (1.0 - sig))).astype(BF16)
        du = (dh * silu).astype(BF16)
        dg_ref[...] = dg
        du_ref[...] = du
        back_ref[:, :d] = (dot(dg, wg_ref[...], 1, 1) + dot(du, wu_ref[...], 1, 1)).astype(BF16)
        lane = lax.broadcasted_iota(jnp.int32, (r, back_extra), 1)
        high = dgr.astype(BF16).astype(F32)
        low = dgr - high
        back_ref[:, d:] = jnp.where(lane == own, high, jnp.where(lane == own + experts, low, 0.0)).astype(BF16)

    vm = pl.BlockSpec(memory_space=pltpu.VMEM)
    return pl.pallas_call(
        kernel,
        in_specs=[pl.BlockSpec(memory_space=pltpu.SMEM)] + [vm] * 6,
        out_specs=[vm] * 6,
        out_shape=[
            jax.ShapeDtypeStruct((r, d), BF16),
            jax.ShapeDtypeStruct((r, d + back_extra), BF16),
            jax.ShapeDtypeStruct((r, f), BF16),
            jax.ShapeDtypeStruct((r, d), BF16),
            jax.ShapeDtypeStruct((r, f), BF16),
            jax.ShapeDtypeStruct((r, f), BF16),
        ],
        compiler_params=params(),
        name="expert_piece",
    )(me, x, cot, router, wg, wu, wd)


def expert_grads(xs, dgs, dus, hids, deos, block=256):
    n = len(xs)
    r, d = xs[0].shape
    f = dgs[0].shape[1]

    def kernel(*refs):
        x, dg, du, hid, deo = (refs[i * n : (i + 1) * n] for i in range(5))
        gg_ref, gu_ref, gd_ref, x_s, deo_s, dg_s, du_s, hid_s = refs[5 * n :]

        @pl.when(pl.program_id(0) == 0)
        def _():
            for i in range(n):
                dg_s[i * r : (i + 1) * r, :] = dg[i][...]
                du_s[i * r : (i + 1) * r, :] = du[i][...]
                x_s[i * r : (i + 1) * r, :] = hid[i][:, :block]
            for j in range(f // block):
                if j:
                    for i in range(n):
                        x_s[i * r : (i + 1) * r, :] = hid[i][:, j * block : (j + 1) * block]
                hid_s[j * block : (j + 1) * block, :] = x_s[...].T

        for i in range(n):
            x_s[i * r : (i + 1) * r, :] = x[i][...]
            deo_s[i * r : (i + 1) * r, :] = deo[i][...]
        xt = x_s[...].T
        gg_ref[...] = dot(xt, dg_s[...])
        gu_ref[...] = dot(xt, du_s[...])
        gd_ref[...] = dot(hid_s[...], deo_s[...])

    part = pl.BlockSpec((r, block), lambda j: (0, j))
    whole = pl.BlockSpec((r, f), lambda j: (0, 0))
    return pl.pallas_call(
        kernel,
        grid=(d // block,),
        in_specs=[part] * n + [whole] * (3 * n) + [part] * n,
        out_specs=[pl.BlockSpec((block, f), lambda j: (j, 0))] * 2
        + [pl.BlockSpec((f, block), lambda j: (0, j))],
        out_shape=[jax.ShapeDtypeStruct((d, f), F32)] * 2
        + [jax.ShapeDtypeStruct((f, d), F32)],
        scratch_shapes=[
            pltpu.VMEM((n * r, block), BF16),
            pltpu.VMEM((n * r, block), BF16),
            pltpu.VMEM((n * r, f), BF16),
            pltpu.VMEM((n * r, f), BF16),
            pltpu.VMEM((f, n * r), BF16),
        ],
        compiler_params=params(),
        name="expert_grads",
    )(*xs, *dgs, *dus, *hids, *deos)


def combine(place, parts):
    n = len(parts)
    m = place.shape[0]
    r, d = parts[0].shape
    block = 256

    def kernel(place_ref, *refs):
        v, out_ref, v_s = refs[:n], refs[n], refs[n + 1]
        for i in range(n):
            v_s[i * r : (i + 1) * r, :] = v[i][...]
        out_ref[...] = dot(place_ref[...], v_s[...]).astype(BF16)

    return pl.pallas_call(
        kernel,
        grid=(pl.cdiv(d, block),),
        in_specs=[pl.BlockSpec(place.shape, lambda j: (0, 0))]
        + [pl.BlockSpec((r, block), lambda j: (0, j))] * n,
        out_specs=pl.BlockSpec((m, block), lambda j: (0, j)),
        out_shape=jax.ShapeDtypeStruct((m, d), BF16),
        scratch_shapes=[pltpu.VMEM((n * r, block), BF16)],
        compiler_params=params(),
    )(place, *parts)


def assemble(parts, c, qc, share):
    n = len(parts)
    rows = parts[0].shape[0]
    hs = HEAD_SIZE
    kw = n // share * hs

    def kernel(c_ref, *refs):
        v = refs[:n]
        q_ref, k_ref, v_ref, small_ref = refs[n:]
        small_ref[...] = sum(v[d][:, qc + 2 * hs :].astype(F32) for d in range(n))
        if share > 1:
            k_ref[...] = jnp.zeros_like(k_ref)
            v_ref[...] = jnp.zeros_like(v_ref)
        for d in range(n):
            at = c_ref[0] ^ d
            q_ref[:, pl.ds(pl.multiple_of(at * qc, qc), qc)] = v[d][:, :qc].astype(F32)
            to = pl.ds(pl.multiple_of(at // share * hs, hs), hs)
            key = v[d][:, qc : qc + hs].astype(F32)
            val = v[d][:, qc + hs : qc + 2 * hs].astype(F32)
            if share > 1:
                k_ref[:, to] += key
                v_ref[:, to] += val
            else:
                k_ref[:, to] = key
                v_ref[:, to] = val

    vm = pl.BlockSpec(memory_space=pltpu.VMEM)
    return pl.pallas_call(
        kernel,
        in_specs=[pl.BlockSpec(memory_space=pltpu.SMEM)] + [vm] * n,
        out_specs=[vm] * 4,
        out_shape=[
            jax.ShapeDtypeStruct((rows, n * qc), F32),
            jax.ShapeDtypeStruct((rows, kw), F32),
            jax.ShapeDtypeStruct((rows, kw), F32),
            jax.ShapeDtypeStruct((rows, parts[0].shape[1] - qc - 2 * hs), F32),
        ],
        compiler_params=params(),
        name="assemble",
    )(c, *parts)


def weight_grads(h1, d_q, d_kv, small, block=256):
    n, d = h1.shape
    qc, kc, sc = d_q.shape[1], d_kv.shape[1], small.shape[1]

    def kernel(h_ref, q_ref, kv_ref, small_ref, out_ref):
        h = h_ref[...].T
        out_ref[:, :qc] = dot(h, q_ref[...], 1, 0).astype(BF16)
        out_ref[:, qc : qc + kc] = dot(h, kv_ref[...], 1, 0).astype(BF16)
        out_ref[:, qc + kc :] = small_ref[...]

    return pl.pallas_call(
        kernel,
        grid=(d // block,),
        in_specs=[
            pl.BlockSpec((n, block), lambda j: (0, j)),
            pl.BlockSpec((n, qc), lambda j: (0, 0)),
            pl.BlockSpec((n, kc), lambda j: (0, 0)),
            pl.BlockSpec((block, sc), lambda j: (j, 0)),
        ],
        out_specs=pl.BlockSpec((block, qc + kc + sc), lambda j: (j, 0)),
        out_shape=jax.ShapeDtypeStruct((d, qc + kc + sc), BF16),
        compiler_params=params(),
        name="weight_grads",
    )(h1, d_q, d_kv, small)


def assemble_columns(parts, c):
    n = len(parts)
    rows, w = parts[0].shape

    def kernel(c_ref, *refs):
        for d in range(n):
            at = pl.multiple_of((c_ref[0] ^ d) * w, w)
            refs[n][:, pl.ds(at, w)] = refs[d][...].astype(F32)

    vm = pl.BlockSpec(memory_space=pltpu.VMEM)
    return pl.pallas_call(
        kernel,
        in_specs=[pl.BlockSpec(memory_space=pltpu.SMEM)] + [vm] * n,
        out_specs=vm,
        out_shape=jax.ShapeDtypeStruct((rows, n * w), F32),
        compiler_params=params(),
        name="assemble_columns",
    )(c, *parts)


def plan(targets, rows, block=LANES):
    n, m = targets.shape

    def kernel(row_ref, col_ref, *outs):
        ids = lax.broadcasted_iota(jnp.int32, (rows, block), 0)
        for d in range(n):
            outs[d][...] = jnp.where(row_ref[d : d + 1, :] == ids, 1.0, 0.0).astype(BF16)
        ids = lax.broadcasted_iota(jnp.int32, (block, n * rows), 1)
        hot = col_ref[:, 0:1] == ids
        for d in range(1, n):
            hot = hot | (col_ref[:, d : d + 1] + d * rows == ids)
        outs[n][...] = jnp.where(hot, 1.0, 0.0).astype(BF16)

    return pl.pallas_call(
        kernel,
        grid=(m // block,),
        in_specs=[
            pl.BlockSpec((n, block), lambda j: (0, j)),
            pl.BlockSpec((block, n), lambda j: (j, 0)),
        ],
        out_specs=[pl.BlockSpec((rows, block), lambda j: (0, j))] * n
        + [pl.BlockSpec((block, n * rows), lambda j: (j, 0))],
        out_shape=[jax.ShapeDtypeStruct((rows, m), BF16)] * n
        + [jax.ShapeDtypeStruct((m, n * rows), BF16)],
        compiler_params=params(),
        name="plan",
    )(targets, targets.T)


def norm_rows(parts, gain):
    n = len(parts)
    t, d = parts[0].shape

    def kernel(gain_ref, *refs):
        for i in range(n):
            v = refs[i][...].astype(F32)
            refs[n][i * t : (i + 1) * t, :] = (v * inverse_rms(v) * gain_ref[...]).astype(BF16)

    vm = pl.BlockSpec(memory_space=pltpu.VMEM)
    return pl.pallas_call(
        kernel,
        in_specs=[vm] * (n + 1),
        out_specs=vm,
        out_shape=jax.ShapeDtypeStruct((n * t, d), BF16),
        compiler_params=params(),
        name="norm_rows",
    )(gain, *parts)


def out_proj(parts, w_cols, c):
    n = len(parts)
    t, k = parts[0].shape
    w = w_cols.shape[1]

    def kernel(c_ref, *refs):
        w_ref, out_ref, acc_ref = refs[n:]
        d = pl.program_id(0)
        for i in range(n):

            @pl.when(d == i)
            def _():
                part = dot(refs[i][...], w_ref[...])
                for b in range(n):
                    to, of = b * (t // n), (b ^ i) * (t // n)
                    block = part[of : of + t // n, :]
                    if i == 0:
                        acc_ref[to : to + t // n, :] = block
                    elif i < n - 1:
                        acc_ref[to : to + t // n, :] += block
                    else:
                        total = acc_ref[to : to + t // n, :] + block
                        out_ref[to : to + t // n, :] = total.astype(BF16)

    return pl.pallas_call(
        kernel,
        grid_spec=pltpu.PrefetchScalarGridSpec(
            num_scalar_prefetch=1,
            grid=(n,),
            in_specs=[pl.BlockSpec((t, k), lambda d, c_ref: (0, 0))] * n
            + [pl.BlockSpec((k, w), lambda d, c_ref: (c_ref[0] ^ d, 0))],
            out_specs=pl.BlockSpec((t, w), lambda d, c_ref: (0, 0)),
            scratch_shapes=[pltpu.VMEM((t, w), F32)],
        ),
        out_shape=jax.ShapeDtypeStruct((t, w), BF16),
        compiler_params=params(),
        name="out_proj",
    )(c, *parts, w_cols)


def out_grads(mixes, d_parts, c, block=256):
    n = len(mixes)
    t, k = mixes[0].shape
    rows, d_model = d_parts[0].shape
    w = d_model // n
    nb = k // block

    def kernel(c_ref, *refs):
        mix, dp, out_ref, d_s = refs[:n], refs[n : 2 * n], refs[2 * n], refs[2 * n + 1]
        i, j = pl.program_id(0), pl.program_id(1)

        @pl.when((i == 0) & (j == 0))
        def _():
            for e in range(n):
                for b in range(n):
                    d_s[e, b * rows : (b + 1) * rows, :] = dp[b ^ e][...]

        for e in range(n):

            @pl.when(i == e)
            def _():
                m = mix[e][:, pl.ds(pl.multiple_of(j * block, block), block)]
                out_ref[...] = dot(m.T, d_s[e]).astype(BF16)

    return pl.pallas_call(
        kernel,
        grid_spec=pltpu.PrefetchScalarGridSpec(
            num_scalar_prefetch=1,
            grid=(n, nb),
            in_specs=[pl.BlockSpec((t, k), lambda i, j, c_ref: (0, 0))] * n
            + [pl.BlockSpec((rows, w), lambda i, j, c_ref: (0, c_ref[0]))] * n,
            out_specs=pl.BlockSpec((block, w), lambda i, j, c_ref: ((c_ref[0] ^ i) * nb + j, 0)),
            scratch_shapes=[pltpu.VMEM((n, t, w), BF16)],
        ),
        out_shape=jax.ShapeDtypeStruct((n * k, w), BF16),
        compiler_params=params(),
        name="out_grads",
    )(c, *mixes, *d_parts)


def residual(x, parts, gain, c):
    n = len(parts)
    w = parts[0].shape[1]

    def kernel(c_ref, x_ref, gain_ref, *refs):
        r1_ref, h2_ref = refs[n:]
        for i in range(n):
            at = pl.ds(pl.multiple_of((c_ref[0] ^ i) * w, w), w)
            r1_ref[:, at] = x_ref[:, at].astype(F32) + refs[i][...].astype(F32)
        v = r1_ref[...]
        h2_ref[...] = (v * inverse_rms(v) * gain_ref[...]).astype(BF16)

    vm = pl.BlockSpec(memory_space=pltpu.VMEM)
    return pl.pallas_call(
        kernel,
        in_specs=[pl.BlockSpec(memory_space=pltpu.SMEM)] + [vm] * (n + 2),
        out_specs=[vm] * 2,
        out_shape=[jax.ShapeDtypeStruct(x.shape, F32), jax.ShapeDtypeStruct(x.shape, BF16)],
        compiler_params=params(),
        name="residual",
    )(c, x, gain, *parts)


def masked_softmax(logits, mask):
    kept = jnp.where(mask, logits, MASKED)
    e = jnp.where(mask, jnp.exp(kept - jnp.max(kept, axis=-1, keepdims=True)), 0.0)
    total = jnp.sum(e, axis=-1, keepdims=True)
    return e / jnp.where(total > 0.0, total, 1.0)


def norm_back(v, gain, grad):
    r = inverse_rms(v)
    n = v * r
    scaled = grad * gain
    back = r * (scaled - n * jnp.mean(n * scaled, axis=-1, keepdims=True))
    return back, grad * n


def turn_back(back_sum, r1, h2, cot, hits, router, gain, experts):
    t, d = r1.shape
    extra = hits.shape[1]

    def kernel(back_ref, r1_ref, h2_ref, cot_ref, hit_ref, router_ref, gain_ref, dr_ref, da_ref, gr_ref, gn_ref):
        gates = masked_softmax(
            dot(h2_ref[...], router_ref[...]), hit_ref[...].astype(F32) > 0.5
        )
        high = back_ref[:, d : d + extra].astype(F32)
        if experts % LANES:
            d_gates = high + pltpu.roll(high, extra - experts, 1)
        else:
            d_gates = high + back_ref[:, d + experts : d + experts + extra].astype(F32)
        centre = jnp.sum(gates * d_gates, axis=-1, keepdims=True)
        d_logits = (gates * (d_gates - centre)).astype(BF16)
        gr_ref[...] = dot(h2_ref[...], d_logits, 0, 0)
        d_h2 = back_ref[:, :d].astype(F32) + dot(d_logits, router_ref[...], 1, 1)
        back, gain_rows = norm_back(r1_ref[...], gain_ref[...], d_h2)
        gn_ref[...] = jnp.sum(gain_rows, axis=0, keepdims=True)
        total = cot_ref[...].astype(F32) + back
        dr_ref[...] = total
        da_ref[...] = total.astype(BF16)

    vm = pl.BlockSpec(memory_space=pltpu.VMEM)
    return pl.pallas_call(
        kernel,
        in_specs=[vm] * 7,
        out_specs=[vm] * 4,
        out_shape=[
            jax.ShapeDtypeStruct((t, d), F32),
            jax.ShapeDtypeStruct((t, d), BF16),
            jax.ShapeDtypeStruct((d, extra), F32),
            jax.ShapeDtypeStruct((1, d), F32),
        ],
        compiler_params=params(),
        name="turn_back",
    )(back_sum, r1, h2, cot, hits, router, gain)


def input_back(x, parts, d_r1, gain):
    n = len(parts)

    def kernel(x_ref, dr_ref, gain_ref, *refs):
        grad = refs[0][...].astype(F32)
        for i in range(1, n):
            grad = grad + refs[i][...].astype(F32)
        back, _ = norm_back(x_ref[...].astype(F32), gain_ref[...], grad)
        refs[n][...] = dr_ref[...] + back

    vm = pl.BlockSpec(memory_space=pltpu.VMEM)
    return pl.pallas_call(
        kernel,
        in_specs=[vm] * (n + 3),
        out_specs=vm,
        out_shape=jax.ShapeDtypeStruct(x.shape, F32),
        compiler_params=params(),
        name="input_back",
    )(x, d_r1, gain, *parts)


def round_up(n, m):
    return (n + m - 1) // m * m


def rows_of_pair(pair_value, row_count, pair_count):
    row_ids = jnp.arange(row_count, dtype=jnp.int32)
    half = row_count // 2
    block = jnp.where(row_ids >= half, 2 * pair_count - 1 - pair_value, pair_value)
    return block * half + row_ids % half


def layer(
    hidden_in,
    out_cot,
    routes,
    block_pairs,
    norm_attn,
    norm_moe,
    q_gain,
    k_gain,
    w_query,
    w_key,
    w_value,
    w_out,
    w_router,
    expert_gate,
    expert_up,
    expert_down,
):
    C = lax.axis_size("ctx")
    S = lax.axis_size("shard")
    T = hidden_in.shape[1]
    D = hidden_in.shape[2]
    E = C * S
    M = S * T
    QW = QUERY_HEADS * HEAD_SIZE
    qc = QW // C
    share = C // KEY_VALUE_HEADS
    hc = qc // HEAD_SIZE
    cap = max(2, (17 * T * TOP + 16 * E - 1) // (16 * E))
    rows = S * cap
    ws = w_query.shape[0]
    gs = q_gain.shape[0]
    po = QW // E
    c = lax.axis_index("ctx")
    s = lax.axis_index("shard")
    me = c * S + s
    c_vec = c.astype(jnp.int32).reshape(1)

    def exchange_ctx(parts):
        out = [parts[0]]
        for d in range(1, C):
            out.append(lax.ppermute(parts[d], "ctx", [(i, i ^ d) for i in range(C)]))
        return out

    def gather_ctx(v):
        return exchange_ctx([v] * C)

    def gather_shard(v):
        return lax.all_gather(v, "shard", axis=0, tiled=True)

    def sum_shard(v):
        return lax.psum_scatter(v, "shard", scatter_dimension=0, tiled=True)

    kv = c // share
    packed = jnp.concatenate(
        [
            lax.dynamic_slice_in_dim(w_query, c * qc, qc, 1),
            lax.dynamic_slice_in_dim(w_key, kv * HEAD_SIZE, HEAD_SIZE, 1),
            lax.dynamic_slice_in_dim(w_value, kv * HEAD_SIZE, HEAD_SIZE, 1),
        ],
        axis=1,
    )
    w_qkv = gather_shard(packed)
    hits = (
        (routes[0][:, :, None] == jnp.arange(E, dtype=jnp.int32)[None, None, :])
        .any(axis=1)
        .astype(BF16)
    )
    rw = ws * E // T
    nw = ws // T
    small_parts = [
        hits,
        w_router.reshape(T, rw),
        norm_moe.reshape(T, nw),
        norm_attn.reshape(T, nw),
        jnp.pad(jnp.concatenate([q_gain, k_gain]), (0, T - 2 * gs)).reshape(T, 1),
    ]
    small_width = round_up(E + rw + 2 * nw + 1, LANES)
    small_parts.append(jnp.zeros((T, small_width - E - rw - 2 * nw - 1), BF16))
    table = gather_shard(jnp.concatenate(small_parts, axis=1))
    x_own = hidden_in[0]
    x_parts = gather_ctx(x_own)
    hits_column = table[:, :E]
    router = table[:, E : E + rw].reshape(D, E)
    gain_moe = table[:, E + rw : E + rw + nw].reshape(D).astype(F32)
    gain_attn = table[:, E + rw + nw : E + rw + 2 * nw].reshape(D).astype(F32)
    head_gains = table[:, E + rw + 2 * nw].reshape(S, T).astype(F32)
    head_gains = jnp.concatenate(
        [
            head_gains[:, :gs].reshape(1, -1),
            head_gains[:, gs : 2 * gs].reshape(1, -1),
            jnp.zeros((6, HEAD_SIZE), F32),
        ],
        axis=0,
    )

    spread = [((p % C) * S + p // C, p) for p in range(E)]
    piece = lax.ppermute(lax.dynamic_slice_in_dim(w_out, c * po, po, 0), ("ctx", "shard"), spread)
    w_out_rows = gather_shard(piece)
    dc = D // C
    w_out_cols = gather_shard(lax.dynamic_slice_in_dim(w_out, c * dc, dc, 1))

    extra = round_up(E, LANES)
    hits_wide = jnp.pad(hits, ((0, 0), (0, extra - E)))
    cot_own = jnp.concatenate([out_cot[0], hits_wide], axis=1)
    cot_column = gather_shard(cot_own)
    router_wide = jnp.pad(router, ((0, 0), (0, extra - E)))

    pairs_here = jnp.stack([block_pairs[c ^ d] for d in range(C)])
    positions = jax.vmap(lambda p: rows_of_pair(p, T, C))(pairs_here).reshape(-1)
    frequency = THETA ** (-(jnp.arange(HEAD_SIZE // 2, dtype=F32) * 2.0) / HEAD_SIZE)
    phase = positions.astype(F32)[:, None] * frequency[None, :]
    cosine, sine = jnp.cos(phase), jnp.sin(phase)
    cosine = jnp.concatenate([cosine, cosine], axis=1)
    sine = jnp.concatenate([-sine, sine], axis=1)
    pos_col, pos_row = positions[:, None], positions[None, :]

    own_experts = (
        jnp.arange(E, dtype=jnp.int32)[None, :]
        == ((c ^ jnp.arange(C, dtype=jnp.int32)) * S + s)[:, None]
    ).astype(BF16)
    hit = dot(own_experts, hits_column, 1, 1).reshape(C, S, T)
    slot = (jnp.cumsum(hit, axis=2) - hit).astype(jnp.int32)
    target = jnp.where(
        hit > 0.5, jnp.arange(S, dtype=jnp.int32)[None, :, None] * cap + slot, -E * cap
    )
    *picks, place = plan(target.reshape(C, M), rows)

    h1 = norm_rows(x_parts, gain_attn.reshape(1, D))
    qkv = dot(h1, w_qkv, 1, 0)
    mix, totals = attend_forward(qkv, hc, head_gains, cosine, sine, pos_col, pos_row)
    mixes = gather_ctx(mix)
    attn_cols = out_proj(mixes, w_out_cols, c_vec).reshape(C, T, dc)
    attn_out = exchange_ctx([attn_cols[d] for d in range(C)])
    r1, h2 = residual(x_own, attn_out, gain_moe.reshape(1, D), c_vec)

    h2_column = gather_shard(h2)

    def dispatch(v):
        sent = [None] * C
        for d in [C - 1] + list(range(1, C - 1)) + [0]:
            sent[d] = dot(picks[d], v, 1, 0).astype(BF16)
        return exchange_ctx(sent)

    cot_in = dispatch(cot_column)
    expert_in = dispatch(h2_column)

    wg, wu, wd = expert_gate[0], expert_up[0], expert_down[0]
    me_vec = me.astype(jnp.int32).reshape(1)
    back_extra = round_up(2 * E, LANES)
    done = [None] * C
    for d in [0, C - 1] + list(range(1, C - 1)):
        done[d] = expert_piece(
            expert_in[d], cot_in[d], router_wide, wg, wu, wd, me_vec, E, back_extra
        )
    mixed_rows, back_rows, hidden, d_expert_out, d_gate, d_up = (list(v) for v in zip(*done))
    back_in = exchange_ctx(back_rows)
    back_sum = sum_shard(combine(place, back_in))
    mixed_in = exchange_ctx(mixed_rows)
    grad_gate, grad_up, grad_down = expert_grads(expert_in, d_gate, d_up, hidden, d_expert_out)

    d_r1, d_attn_own, grad_router, grad_norm_moe = turn_back(
        back_sum, r1, h2, out_cot[0], hits_wide, router_wide, gain_moe.reshape(1, D), E
    )
    d_attn_parts = gather_ctx(d_attn_own)
    grad_out_piece = sum_shard(out_grads(mixes, d_attn_parts, c_vec))
    d_attn = jnp.concatenate(d_attn_parts, axis=0)
    d_mix = dot(d_attn, w_out_rows, 1, 1).astype(BF16)
    d_q, d_kv, gain_grads = attend_backward(
        qkv, d_mix, mix, totals, hc, head_gains, cosine, sine, pos_col, pos_row
    )
    d_qkv = jnp.concatenate([d_q, d_kv], axis=1)

    x_seq = jnp.concatenate(x_parts, axis=0).astype(F32)
    d_h1_partial = dot(d_qkv, w_qkv, 1, 1)
    grad_norm_attn = jnp.sum(d_h1_partial * (x_seq * inverse_rms(x_seq)), axis=0)

    def shard_column(v):
        return jnp.pad(v.reshape(S, gs), ((0, 0), (0, ws - gs))).reshape(-1)

    wide = round_up(E + 4, LANES)
    lane = jnp.arange(wide, dtype=jnp.int32)[None, :]
    small = jnp.pad(grad_router[:, :E], ((0, 0), (0, wide - E)))
    columns = (
        grad_norm_attn,
        grad_norm_moe.reshape(D),
        shard_column(gain_grads[0]),
        shard_column(gain_grads[1]),
    )
    for i, v in enumerate(columns):
        small = small + jnp.where(lane == E + i, v[:, None], 0.0)
    owned_partial = weight_grads(h1, d_q, d_kv, small.astype(BF16))
    owned = sum_shard(owned_partial)

    d_h1_parts = d_h1_partial.astype(BF16).reshape(C, T, D)
    d_h1_in = exchange_ctx([d_h1_parts[d] for d in range(C)])
    grad_in = input_back(x_own, d_h1_in, d_r1, gain_attn.reshape(1, D))[None]

    mixture = sum_shard(combine(place, mixed_in)).astype(F32)
    block_out = (r1 + mixture).astype(BF16)[None]

    out_parts = gather_ctx(grad_out_piece)
    owned_parts = gather_ctx(owned)
    grad_query, grad_key, grad_value, mine = assemble(owned_parts, c_vec, qc, share)
    grad_out = assemble_columns(out_parts, c_vec)
    return (
        block_out,
        grad_in,
        grad_query,
        grad_key,
        grad_value,
        grad_out,
        mine[:, :E],
        mine[:, E],
        mine[:, E + 1],
        mine[:gs, E + 2],
        mine[:gs, E + 3],
        grad_gate[None],
        grad_up[None],
        grad_down[None],
    )


def solution(mesh):
    token = P("shard", "ctx", None)
    row = P("shard", None)
    vector = P("shard")
    expert = P(("ctx", "shard"), None, None)
    return jax.shard_map(
        layer,
        mesh=mesh,
        in_specs=(token, token, token, P())
        + (vector,) * 4
        + (row,) * 5
        + (expert,) * 3,
        out_specs=(token, token) + (row,) * 5 + (vector,) * 4 + (expert,) * 3,
        check_vma=False,
    )
```

time: 1690 us -> 689 us (0.41)
  waiting for transfers between devices: 833 us -> 328 us
  blocking collectives: 455 us -> 16 us
  Pallas kernels: 0 us -> 179 us
  matrix products: 201 us -> 47.8 us
  local copies, waits for them, and re-layouts: 115 us -> 33.4 us
  other arithmetic: 56.5 us -> 17.1 us
  starting transfers between devices: 7.99 us -> 42.7 us
    reduce_scatter x5 -> x4, waiting for transfers between devices: 363 us -> 65.8 us  [sum_shard(): return lax.psum_scatter(v, 'shard', scatter_dimension=0, tiled=True)]
    all_to_all x2 -> x0, blocking collectives: 243 us -> none  [the longest x1 122 us: body(): lax.all_to_all(grad_buffer, ('ctx', 'shard'), split_axis=0, concat_axis=0...]
    ppermute x0 -> x34, waiting for transfers between devices: none -> 182 us  [the longest x33 182 us: exchange_ctx(): out.append(lax.ppermute(parts[d], 'ctx', [(i, i ^ d) for i in range(C)]))]
    pallas_call x0 -> x19, Pallas kernels: none -> 179 us  [the longest x4 50 us: expert_piece(): pl.pallas_call(kernel, in_specs=[pl.BlockSpec(memory_space=pltpu.SMEM)] +...]
    dot_general x54 -> x12, matrix products: 201 us -> 47.8 us  [dot(): lax.dot_general(a, b, (((ca,), (cb,)), ((), ())), preferred_element_type=...]
    all_gather x5 -> x1, blocking collectives: 165 us -> 16 us  [gather_shard(): return lax.all_gather(v, 'shard', axis=0, tiled=True)]
    all_gather x4 -> x5, waiting for transfers between devices: 224 us -> 79.9 us  [gather_shard(): return lax.all_gather(v, 'shard', axis=0, tiled=True)]
    all_to_all x2 -> x0, waiting for transfers between devices: 113 us -> none  [the longest x1 113 us: body(): lax.all_to_all(grad_inputs.astype(jnp.bfloat16).reshape(arrived.shape), (...]
  transfers between devices with their start and end apart: 14 -> 43, of which waited for: 9 -> 23; matrix products, arithmetic and copies ran while one was open for 10% -> 12% of each run, Pallas kernels for 0% -> 24%
where the time goes in v1:
time: 689 us; the launch traced here: 678 us
  waiting for transfers between devices  328 us (48%)
  Pallas kernels  179 us (26%)
  matrix products  47.8 us (7%)
  starting transfers between devices  42.7 us (6%)
  local copies, waits for them, and re-layouts  33.4 us (5%)
  other arithmetic  17.1 us (2%)
  blocking collectives  16 us (2%)
  between operations  14.6 us (2%)
    ppermute x33, waiting for transfers between devices, exchange_ctx(): out.append(lax.ppermute(parts[d], 'ctx', [(i, i ^ d) for i in range(C)]))  182 us
    all_gather x5, waiting for transfers between devices, gather_shard(): return lax.all_gather(v, 'shard', axis=0, tiled=True)  79.9 us
    reduce_scatter x4, waiting for transfers between devices, sum_shard(): return lax.psum_scatter(v, 'shard', scatter_dimension=0, tiled=True)  65.8 us
    pallas_call x4, Pallas kernels, expert_piece(): pl.pallas_call(kernel, in_specs=[pl.BlockSpec(memory_space=pltpu.SMEM)] +...  50 us
    dot_general x12, matrix products, dot(): lax.dot_general(a, b, (((ca,), (cb,)), ((), ())), preferred_element_type=...  47.8 us
    ppermute x33, starting transfers between devices, exchange_ctx(): out.append(lax.ppermute(parts[d], 'ctx', [(i, i ^ d) for i in range(C)]))  41 us
    pallas_call x2, Pallas kernels, combine(): pl.pallas_call(kernel, grid=(pl.cdiv(d, block),), in_specs=[pl.BlockSpec(...  23.2 us
    pallas_call x1, Pallas kernels, expert_grads(): pl.pallas_call(kernel, grid=(d // block,), in_specs=[part] * n + [whole]...  19.1 us
  transfers between devices with their start and end apart: 43, of which 23 were waited for; matrix products, arithmetic and copies ran while one was open for 12% of the time, Pallas kernels for 24%

profile of v1, /device:TPU:0, one launch (start us, length us, event | category | flops | bytes accessed | tf_op | source)
XLA Modules:
  0.0 678.4 jit_solution(8423718851715461762)
XLA Ops:
  18.6 16.0 %all_gather.18 = bf16[1024,128]{1,0:T(8,128)(2,1)S(1)} all-gather(bf16[128,128]{1,0:T(8,128)(2,1)S(1)} %concatenate.31), channel_id=1, replica_groups=mesh['ctx'=4,'shard'=8] {'shard'}, dimensions={0}, use_global_device_ids=true | all-gather | bytes 294912 | tf_op jit(solution)/shard_map/all_gather | solution.py:687
  48.8 22.1 %all-gather.6.cloned.1.call-done = bf16[2048,1280]{1,0:T(8,128)(2,1)} async-done(((bf16[256,1280]{1,0:T(8,128)(2,1)}), bf16[2048,1280]{1,0:T(8,128)(2,1)}) %all-gather.6.cloned.1.call-update) | async-done | bytes 5242896 | tf_op jit(solution)/shard_map/all_gather | solution.py:687
  78.4 12.0 %attend_forward.1 = (bf16[512,1024]{1,0:T(8,128)(2,1)}, f32[512,128]{1,0:T(8,128)}) custom-call(f32[512,1280]{1,0:T(8,128)} %fusion.35.q_ref.k_ref.v_ref, f32[512,1280]{1,0:T(8,128)} %fusion.35.q_ref.k_ref.v_ref, f32[512,1280]{1,0:T(8,128)} %fusion.35.q_ref.k_ref.v_ref, f32[8,128]{1,0:T(8,128)} %maximum_maximum_fusion.gain_ref, ...), custom_call_target="tpu_custom_call" | custom-call | tf_op jit(solution)/shard_map/attend_forward/pallas_call | solution.py:79
  93.9 24.8 %all-gather.8.cloned.1.call-done.refs_4_ = bf16[4096,512]{1,0:T(8,128)(2,1)} async-done(((bf16[512,512]{1,0:T(8,128)(2,1)}), bf16[4096,512]{1,0:T(8,128)(2,1)}) %all-gather.8.cloned.1.call-update) | async-done | bytes 4194320 | tf_op jit(solution)/shard_map/all_gather | solution.py:687
  118.7 20.9 %collective-permute-done.4.refs_2_ = bf16[512,1024]{1,0:T(8,128)(2,1)} collective-permute-done((bf16[512,1024]{1,0:T(8,128)(2,1)}, bf16[512,1024]{1,0:T(8,128)(2,1)}, u32[]{:S(2)}, u32[]{:S(2)}) %collective-permute-start.4) | collective-permute-done | bytes 1048608 | tf_op jit(solution)/shard_map/ppermute | solution.py:680
  186.2 30.3 %all-gather.10.cloned.1.call-done = bf16[1024,2048]{1,0:T(8,128)(2,1)} async-done(((bf16[128,2048]{1,0:T(8,128)(2,1)}), bf16[1024,2048]{1,0:T(8,128)(2,1)}) %all-gather.10.cloned.1.call-update) | async-done | bytes 4194320 | tf_op jit(solution)/shard_map/all_gather | solution.py:687
  232.6 23.7 %collective-permute-done.9.x_ref.refs_1_ = bf16[272,2048]{1,0:T(8,128)(2,1)} collective-permute-done((bf16[272,2048]{1,0:T(8,128)(2,1)}, bf16[272,2048]{1,0:T(8,128)(2,1)}, u32[]{:S(2)}, u32[]{:S(2)}) %collective-permute-start.9) | collective-permute-done | bytes 1114144 | tf_op jit(solution)/shard_map/ppermute | solution.py:680
  256.3 12.6 %expert_piece.5 = (bf16[272,2048]{1,0:T(8,128)(2,1)}, bf16[272,2176]{1,0:T(8,128)(2,1)}, bf16[272,768]{1,0:T(8,128)(2,1)}, bf16[272,2048]{1,0:T(8,128)(2,1)}, bf...) custom-call(s32[1]{0:T(128)} %bitcast.10.me_ref, bf16[272,2048]{1,0:T(8,128)(2,1)} %collective-permute-done.9.x_ref.refs_1_, ...), custom_call_target="tpu_custom_call" | custom-call | tf_op jit(solution)/shard_map/expert_piece/pallas_call | solution.py:221
  270.2 11.2 %collective-permute-done.12.x_ref.refs_2_ = bf16[272,2048]{1,0:T(8,128)(2,1)} collective-permute-done((bf16[272,2048]{1,0:T(8,128)(2,1)}, bf16[272,2048]{1,0:T(8,128)(2,1)}, u32[]{:S(2)}, u32[]{:S(2)}) %collective-permute-start.12) | collective-permute-done | bytes 1114144 | tf_op jit(solution)/shard_map/ppermute | solution.py:680
  281.4 12.4 %expert_piece.6 = (bf16[272,2048]{1,0:T(8,128)(2,1)}, bf16[272,2176]{1,0:T(8,128)(2,1)}, bf16[272,768]{1,0:T(8,128)(2,1)}, bf16[272,2048]{1,0:T(8,128)(2,1)}, bf...) custom-call(s32[1]{0:T(128)} %bitcast.10.me_ref, bf16[272,2048]{1,0:T(8,128)(2,1)} %collective-permute-done.12.x_ref.refs_2_, ...), custom_call_target="tpu_custom_call" | custom-call | tf_op jit(solution)/shard_map/expert_piece/pallas_call | solution.py:221
  294.4 12.6 %expert_piece.7 = (bf16[272,2048]{1,0:T(8,128)(2,1)}, bf16[272,2176]{1,0:T(8,128)(2,1)}, bf16[272,768]{1,0:T(8,128)(2,1)}, bf16[272,2048]{1,0:T(8,128)(2,1)}, bf...) custom-call(s32[1]{0:T(128)} %bitcast.10.me_ref, bf16[272,2048]{1,0:T(8,128)(2,1)} %collective-permute-done.15.x_ref.refs_3_, ...), custom_call_target="tpu_custom_call" | custom-call | tf_op jit(solution)/shard_map/expert_piece/pallas_call | solution.py:221
  315.3 12.4 %expert_piece.4 = (bf16[272,2048]{1,0:T(8,128)(2,1)}, bf16[272,2176]{1,0:T(8,128)(2,1)}, bf16[272,768]{1,0:T(8,128)(2,1)}, bf16[272,2048]{1,0:T(8,128)(2,1)}, bf...) custom-call(s32[1]{0:T(128)} %bitcast.10.me_ref, bf16[272,2048]{1,0:T(8,128)(2,1)} %convolution_convert_fusion.7.x_ref.refs_0_, ...), custom_call_target="tpu_custom_call" | custom-call | tf_op jit(solution)/shard_map/expert_piece/pallas_call | solution.py:221
  327.8 13.9 %collective-permute-done.19.refs_2_ = bf16[272,2176]{1,0:T(8,128)(2,1)S(1)} collective-permute-done((bf16[272,2176]{1,0:T(8,128)(2,1)}, bf16[272,2176]{1,0:T(8,128)(2,1)S(1)}, u32[]{:S(2)}, u32[]{:S(2)}) %collective-permute-start.19) | collective-permute-done | bytes 1183776 | tf_op jit(solution)/shard_map/ppermute | solution.py:680
  343.1 12.1 %shard_map.264 = bf16[1024,2176]{1,0:T(8,128)(2,1)} custom-call(bf16[1024,1088]{1,0:T(8,128)(2,1)} %get-tuple-element.63.place_ref, bf16[272,2176]{1,0:T(8,128)(2,1)} %get-tuple-element.73.refs_0_, bf16[272,2176]{1,0:T(8,128)(2,1)} %copy-done.8, bf16[272,2176]{1,0:T(8,128)(2,1)} %copy-done.10, bf16[272,2176]{1,0:T(8,128)(2,1)} %copy-done.11), custom_call_target="tpu_custom_call" | custom-call | tf_op jit(solution)/shard_map/pallas_call | solution.py:301
  357.0 62.5 %reduce-scatter.7.cloned.1.call-done.back_ref = bf16[128,2176]{1,0:T(8,128)(2,1)} async-done(((bf16[1024,2176]{1,0:T(8,128)(2,1)}), bf16[128,2176]{1,0:T(8,128)(2,1)}) %reduce-scatter.7.cloned.1.call-update) | async-done | bytes 557072 | tf_op jit(solution)/shard_map/reduce_scatter | solution.py:690
  427.6 10.9 %collective-permute-done.23.refs_7_ = bf16[128,2048]{1,0:T(8,128)(2,1)S(1)} collective-permute-done((bf16[128,2048]{1,0:T(8,128)(2,1)}, bf16[128,2048]{1,0:T(8,128)(2,1)S(1)}, u32[]{:S(2)}, u32[]{:S(2)}) %collective-permute-start.23) | collective-permute-done | bytes 524320 | tf_op jit(solution)/shard_map/ppermute | solution.py:680
  438.5 10.8 %collective-permute-done.22.refs_6_ = bf16[128,2048]{1,0:T(8,128)(2,1)S(1)} collective-permute-done((bf16[128,2048]{1,0:T(8,128)(2,1)}, bf16[128,2048]{1,0:T(8,128)(2,1)S(1)}, u32[]{:S(2)}, u32[]{:S(2)}) %collective-permute-start.22) | collective-permute-done | bytes 524320 | tf_op jit(solution)/shard_map/ppermute | solution.py:680
  450.9 11.4 %out_grads.1 = bf16[4096,512]{1,0:T(8,128)(2,1)} custom-call(s32[1]{0:T(128)} %bitcast.c_ref, bf16[512,1024]{1,0:T(8,128)(2,1)} %get-tuple-element.61.refs_0_.mix_ref, bf16[512,1024]{1,0:T(8,128)(2,1)} %collective-permute-done.3.refs_1_, bf16[512,1024]{1,0:T(8,128)(2,1)} %collective-permute-done.4.refs_2_, bf16[512,1024]{1,0:T(8,128)(2,1)} %collective-permute-done.5.refs_3_, ...), custom_call_target="tpu_custom_call" | custom-call | tf_op jit(solution)/shard_map/out_grads/pallas_call | solution.py:514
  473.4 16.7 %attend_backward.1 = (bf16[512,1024]{1,0:T(8,128)(2,1)}, bf16[512,256]{1,0:T(8,128)(2,1)}, f32[8,128]{1,0:T(8,128)}) custom-call(f32[512,1280]{1,0:T(8,128)} %fusion.35.q_ref.k_ref.v_ref, f32[512,1280]{1,0:T(8,128)} %fusion.35.q_ref.k_ref.v_ref, f32[512,1280]{1,0:T(8,128)} %fusion.35.q_ref.k_ref.v_ref, bf16[512,1024]{1,0:T(8,128)(2,1)} %fusion.11.dm_ref, ...), custom_call_target="tpu_custom_call" | custom-call | tf_op jit(solution)/shard_map/attend_backward/pallas_call | solution.py:148
  514.7 23.9 %collective-permute-done.11.refs_1_ = bf16[272,2048]{1,0:T(8,128)(2,1)S(1)} collective-permute-done((bf16[272,2048]{1,0:T(8,128)(2,1)S(1)}, bf16[272,2048]{1,0:T(8,128)(2,1)S(1)}, u32[]{:S(2)}, u32[]{:S(2)}) %collective-permute-start.11) | collective-permute-done | bytes 1114144 | tf_op jit(solution)/shard_map/ppermute | solution.py:680
  538.7 24.6 %collective-permute-done.14.refs_2_ = bf16[272,2048]{1,0:T(8,128)(2,1)S(1)} collective-permute-done((bf16[272,2048]{1,0:T(8,128)(2,1)}, bf16[272,2048]{1,0:T(8,128)(2,1)S(1)}, u32[]{:S(2)}, u32[]{:S(2)}) %collective-permute-start.14) | collective-permute-done | bytes 1114144 | tf_op jit(solution)/shard_map/ppermute | solution.py:680
  564.6 11.1 %shard_map.263 = bf16[1024,2048]{1,0:T(8,128)(2,1)} custom-call(bf16[1024,1088]{1,0:T(8,128)(2,1)} %get-tuple-element.63.place_ref, bf16[272,2048]{1,0:T(8,128)(2,1)} %get-tuple-element.66.refs_0_, bf16[272,2048]{1,0:T(8,128)(2,1)} %copy-done.12, bf16[272,2048]{1,0:T(8,128)(2,1)} %copy-done.13, bf16[272,2048]{1,0:T(8,128)(2,1)} %copy-done.14), custom_call_target="tpu_custom_call" | custom-call | tf_op jit(solution)/shard_map/pallas_call | solution.py:301
  617.4 19.1 %expert_grads.1 = (f32[2048,768]{1,0:T(8,128)}, f32[2048,768]{1,0:T(8,128)}, f32[768,2048]{1,0:T(8,128)}) custom-call(bf16[272,2048]{1,0:T(8,128)(2,1)} %convolution_convert_fusion.7.x_ref.refs_0_, bf16[272,2048]{1,0:T(8,128)(2,1)} %collective-permute-done.9.x_ref.refs_1_, bf16[272,2048]{1,0:T(8,128)(2,1)} %collective-permute-done.12.x_ref.refs_2_, ...), custom_call_target="tpu_custom_call" | custom-call | tf_op jit(solution)/shard_map/expert_grads/pallas_call | solution.py:269
  642.6 13.0 %collective-permute-done.32.refs_2_ = bf16[512,512]{1,0:T(8,128)(2,1)} collective-permute-done((bf16[512,512]{1,0:T(8,128)(2,1)}, bf16[512,512]{1,0:T(8,128)(2,1)}, u32[]{:S(2)}, u32[]{:S(2)}) %collective-permute-start.32) | collective-permute-done | bytes 524320 | tf_op jit(solution)/shard_map/ppermute | solution.py:680
  (276 shorter events, 222.8 us)
Async XLA Ops:
  7.2 63.7 %all-gather.6.cloned.1.call-start = ((), (), s32[]{:S(2)}) async-start(), calls=%async_computation.4 | async-start | bytes 5898240 | tf_op jit(solution)/shard_map/all_gather | solution.py:687
  10.3 108.4 %all-gather.8.cloned.1.call-start = ((), (), s32[]{:S(2)}) async-start(), calls=%async_computation.5 | async-start | bytes 4718592 | tf_op jit(solution)/shard_map/all_gather | solution.py:687
  11.3 161.4 %all-gather.12.cloned.1.call-start = ((), (), s32[]{:S(2)}) async-start(), calls=%async_computation.7 | async-start | bytes 5013504 | tf_op jit(solution)/shard_map/all_gather | solution.py:687
  13.0 203.5 %all-gather.10.cloned.1.call-start = ((), (), s32[]{:S(2)}) async-start(), calls=%async_computation.6 | async-start | bytes 4718592 | tf_op jit(solution)/shard_map/all_gather | solution.py:687
  91.9 47.8 %collective-permute-start.4 = (bf16[512,1024]{1,0:T(8,128)(2,1)}, bf16[512,1024]{1,0:T(8,128)(2,1)}, u32[]{:S(2)}, u32[]{:S(2)}) collective-permute-start(bf16[512,1024]{1,0:T(8,128)(2,1)} %get-tuple-element.61.refs_0_.mix_ref), channel_id=1, source_target_pairs={{0,16},{8,24},{16,0},{24,8},{1,17},{9,25},{17,1},{25,9},{2,18},{10... | collective-permute-start | bytes 3145736 | tf_op jit(solution)/shard_map/ppermute | solution.py:680
  93.3 46.3 %collective-permute-start.5 = (bf16[512,1024]{1,0:T(8,128)(2,1)}, bf16[512,1024]{1,0:T(8,128)(2,1)}, u32[]{:S(2)}, u32[]{:S(2)}) collective-permute-start(bf16[512,1024]{1,0:T(8,128)(2,1)} %get-tuple-element.61.refs_0_.mix_ref), channel_id=1, source_target_pairs={{0,24},{8,16},{16,8},{24,0},{1,25},{9,17},{17,9},{25,1},{2,26},{10... | collective-permute-start | bytes 3145736 | tf_op jit(solution)/shard_map/ppermute | solution.py:680
  159.9 259.5 %reduce-scatter.7.cloned.1.call-start = ((), (), s32[]{:S(2)}) async-start(), calls=%async_computation.9 | async-start | bytes 5013504 | tf_op jit(solution)/shard_map/reduce_scatter | solution.py:690
  177.7 51.4 %collective-permute-start.10 = (bf16[272,2176]{1,0:T(8,128)(2,1)}, bf16[272,2176]{1,0:T(8,128)(2,1)S(1)}, u32[]{:S(2)}, u32[]{:S(2)}) collective-permute-start(bf16[272,2176]{1,0:T(8,128)(2,1)} %convolution_convert_fusion.2), channel_id=1, source_target_pairs={{0,8},{8,0},{16,24},{24,16},{1,9},{9,1},{17,25},{25,17},{2,10},{10... | collective-permute-start | bytes 3551240 | tf_op jit(solution)/shard_map/ppermute | solution.py:680
  181.6 88.6 %collective-permute-start.13 = (bf16[272,2176]{1,0:T(8,128)(2,1)}, bf16[272,2176]{1,0:T(8,128)(2,1)}, u32[]{:S(2)}, u32[]{:S(2)}) collective-permute-start(bf16[272,2176]{1,0:T(8,128)(2,1)} %convolution_convert_fusion.1), channel_id=1, source_target_pairs={{0,16},{8,24},{16,0},{24,8},{1,17},{9,25},{17,1},{25,9},{2,18},{10... | collective-permute-start | bytes 3551240 | tf_op jit(solution)/shard_map/ppermute | solution.py:680
  185.1 109.3 %collective-permute-start.16 = (bf16[272,2176]{1,0:T(8,128)(2,1)}, bf16[272,2176]{1,0:T(8,128)(2,1)}, u32[]{:S(2)}, u32[]{:S(2)}) collective-permute-start(bf16[272,2176]{1,0:T(8,128)(2,1)} %convolution_convert_fusion), channel_id=1, source_target_pairs={{0,24},{8,16},{16,8},{24,0},{1,25},{9,17},{17,9},{25,1},{2,26},{10... | collective-permute-start | bytes 3551240 | tf_op jit(solution)/shard_map/ppermute | solution.py:680
  225.3 56.1 %collective-permute-start.12 = (bf16[272,2048]{1,0:T(8,128)(2,1)}, bf16[272,2048]{1,0:T(8,128)(2,1)}, u32[]{:S(2)}, u32[]{:S(2)}) collective-permute-start(bf16[272,2048]{1,0:T(8,128)(2,1)} %convolution_convert_fusion.5), channel_id=1, source_target_pairs={{0,16},{8,24},{16,0},{24,8},{1,17},{9,25},{17,1},{25,9},{2,18},{10... | collective-permute-start | bytes 3342344 | tf_op jit(solution)/shard_map/ppermute | solution.py:680
  229.1 65.3 %collective-permute-start.15 = (bf16[272,2048]{1,0:T(8,128)(2,1)}, bf16[272,2048]{1,0:T(8,128)(2,1)}, u32[]{:S(2)}, u32[]{:S(2)}) collective-permute-start(bf16[272,2048]{1,0:T(8,128)(2,1)} %convolution_convert_fusion.4), channel_id=1, source_target_pairs={{0,24},{8,16},{16,8},{24,0},{1,25},{9,17},{17,9},{25,1},{2,26},{10... | collective-permute-start | bytes 3342344 | tf_op jit(solution)/shard_map/ppermute | solution.py:680
  268.8 59.0 %collective-permute-start.18 = (bf16[272,2176]{1,0:T(8,128)(2,1)}, bf16[272,2176]{1,0:T(8,128)(2,1)S(1)}, u32[]{:S(2)}, u32[]{:S(2)}) collective-permute-start(bf16[272,2176]{1,0:T(8,128)(2,1)} %get-tuple-element.74), channel_id=1, source_target_pairs={{0,8},{8,0},{16,24},{24,16},{1,9},{9,1},{17,25},{25,17},{2,10},{10... | collective-permute-start | bytes 3551240 | tf_op jit(solution)/shard_map/ppermute | solution.py:680
  293.8 47.9 %collective-permute-start.19 = (bf16[272,2176]{1,0:T(8,128)(2,1)}, bf16[272,2176]{1,0:T(8,128)(2,1)S(1)}, u32[]{:S(2)}, u32[]{:S(2)}) collective-permute-start(bf16[272,2176]{1,0:T(8,128)(2,1)} %get-tuple-element.75), channel_id=1, source_target_pairs={{0,16},{8,24},{16,0},{24,8},{1,17},{9,25},{17,1},{25,9},{2,18},{10... | collective-permute-start | bytes 3551240 | tf_op jit(solution)/shard_map/ppermute | solution.py:680
  355.3 112.6 %all-gather.14.cloned.1.call-start = ((), (), s32[]{:S(2)}) async-start(), calls=%async_computation.10 | async-start | bytes 4718592 | tf_op jit(solution)/shard_map/all_gather | solution.py:687
  356.9 225.2 %reduce-scatter.11.cloned.1.call-start = ((), (), s32[]{:S(2)}) async-start(), calls=%async_computation.12 | async-start | bytes 4718592 | tf_op jit(solution)/shard_map/reduce_scatter | solution.py:690
  462.3 123.3 %reduce-scatter.9.cloned.1.call-start = ((), (), s32[]{:S(2)}) async-start(), calls=%async_computation.11 | async-start | bytes 6488064 | tf_op jit(solution)/shard_map/reduce_scatter | solution.py:690
  510.0 126.9 %reduce-scatter.5.cloned.1.call-start = ((), (), s32[]{:S(2)}) async-start(), calls=%async_computation.8 | async-start | bytes 4718592 | tf_op jit(solution)/shard_map/reduce_scatter | solution.py:690
  512.7 50.6 %collective-permute-start.14 = (bf16[272,2048]{1,0:T(8,128)(2,1)}, bf16[272,2048]{1,0:T(8,128)(2,1)S(1)}, u32[]{:S(2)}, u32[]{:S(2)}) collective-permute-start(bf16[272,2048]{1,0:T(8,128)(2,1)} %get-tuple-element.70), channel_id=1, source_target_pairs={{0,16},{8,24},{16,0},{24,8},{1,17},{9,25},{17,1},{25,9},{2,18},{10... | collective-permute-start | bytes 3342344 | tf_op jit(solution)/shard_map/ppermute | solution.py:680
  514.2 49.1 %collective-permute-start.17 = (bf16[272,2048]{1,0:T(8,128)(2,1)}, bf16[272,2048]{1,0:T(8,128)(2,1)S(1)}, u32[]{:S(2)}, u32[]{:S(2)}) collective-permute-start(bf16[272,2048]{1,0:T(8,128)(2,1)} %get-tuple-element.72), channel_id=1, source_target_pairs={{0,24},{8,16},{16,8},{24,0},{1,25},{9,17},{17,9},{25,1},{2,26},{10... | collective-permute-start | bytes 3342344 | tf_op jit(solution)/shard_map/ppermute | solution.py:680
  585.6 75.6 %collective-permute-start.28 = (bf16[256,1408]{1,0:T(8,128)(2,1)}, bf16[256,1408]{1,0:T(8,128)(2,1)S(1)}, u32[]{:S(2)}, u32[]{:S(2)}) collective-permute-start(bf16[256,1408]{1,0:T(8,128)(2,1)} %reduce-scatter.9.cloned.1.call-done.refs_0_), channel_id=1, source_target_pairs={{0,8},{8,0},{16,24},{24,16},{1,9},{9,1},{17,25},{25,17},{2,10},{10... | collective-permute-start | bytes 2162696 | tf_op jit(solution)/shard_map/ppermute | solution.py:680
  593.4 67.9 %collective-permute-start.29 = (bf16[256,1408]{1,0:T(8,128)(2,1)}, bf16[256,1408]{1,0:T(8,128)(2,1)S(1)}, u32[]{:S(2)}, u32[]{:S(2)}) collective-permute-start(bf16[256,1408]{1,0:T(8,128)(2,1)} %reduce-scatter.9.cloned.1.call-done.refs_0_), channel_id=1, source_target_pairs={{0,16},{8,24},{16,0},{24,8},{1,17},{9,25},{17,1},{25,9},{2,18},{10... | collective-permute-start | bytes 2162696 | tf_op jit(solution)/shard_map/ppermute | solution.py:680
  603.4 57.9 %collective-permute-start.30 = (bf16[256,1408]{1,0:T(8,128)(2,1)}, bf16[256,1408]{1,0:T(8,128)(2,1)}, u32[]{:S(2)}, u32[]{:S(2)}) collective-permute-start(bf16[256,1408]{1,0:T(8,128)(2,1)} %reduce-scatter.9.cloned.1.call-done.refs_0_), channel_id=1, source_target_pairs={{0,24},{8,16},{16,8},{24,0},{1,25},{9,17},{17,9},{25,1},{2,26},{10... | collective-permute-start | bytes 2162696 | tf_op jit(solution)/shard_map/ppermute | solution.py:680
  607.4 48.2 %collective-permute-start.32 = (bf16[512,512]{1,0:T(8,128)(2,1)}, bf16[512,512]{1,0:T(8,128)(2,1)}, u32[]{:S(2)}, u32[]{:S(2)}) collective-permute-start(bf16[512,512]{1,0:T(8,128)(2,1)} %reduce-scatter.11.cloned.1.call-done.refs_0_), channel_id=1, source_target_pairs={{0,16},{8,24},{16,0},{24,8},{1,17},{9,25},{17,1},{25,9},{2,18},{10... | collective-permute-start | bytes 1572872 | tf_op jit(solution)/shard_map/ppermute | solution.py:680
  (72 other events, 817.1 us)
Sparse Core Ops, SparseCore 0:
  10.5 60.4 all-gather.5
  73.1 45.5 all-gather.7
  120.9 47.8 all-gather.11
  170.9 45.6 all-gather.9
  355.4 64.0 reduce-scatter.6
  420.9 46.8 all-gather.13
  470.7 48.7 reduce-scatter.10
  522.4 63.2 reduce-scatter.8
  588.5 48.3 reduce-scatter.4

commit v2 on v1

--- a/solution.py
+++ b/solution.py
@@ -286,11 +286,11 @@
     )(*xs, *dgs, *dus, *hids, *deos)
 
 
-def combine(place, parts):
+def combine(place, parts, lo, hi, block=512):
     n = len(parts)
     m = place.shape[0]
-    r, d = parts[0].shape
-    block = 256
+    r = parts[0].shape[0]
+    first = lo // block
 
     def kernel(place_ref, *refs):
         v, out_ref, v_s = refs[:n], refs[n], refs[n + 1]
@@ -300,11 +300,11 @@
 
     return pl.pallas_call(
         kernel,
-        grid=(pl.cdiv(d, block),),
+        grid=(pl.cdiv(hi - lo, block),),
         in_specs=[pl.BlockSpec(place.shape, lambda j: (0, 0))]
-        + [pl.BlockSpec((r, block), lambda j: (0, j))] * n,
+        + [pl.BlockSpec((r, block), lambda j: (0, first + j))] * n,
         out_specs=pl.BlockSpec((m, block), lambda j: (0, j)),
-        out_shape=jax.ShapeDtypeStruct((m, d), BF16),
+        out_shape=jax.ShapeDtypeStruct((m, hi - lo), BF16),
         scratch_shapes=[pltpu.VMEM((n * r, block), BF16)],
         compiler_params=params(),
     )(place, *parts)
@@ -487,15 +487,42 @@
     )(c, *parts, w_cols)
 
 
-def out_grads(mixes, d_parts, c, block=256):
+def turn_mixes(mixes, block=512):
     n = len(mixes)
     t, k = mixes[0].shape
+    nb = k // block
+
+    def kernel(*refs):
+        i = pl.program_id(0)
+        for e in range(n):
+
+            @pl.when(i == e)
+            def _():
+                refs[n][...] = refs[e][...].T
+
+    def pick(e):
+        return pl.BlockSpec((t, block), lambda i, j: (0, jnp.where(i < e, 0, jnp.where(i > e, nb - 1, j))))
+
+    return pl.pallas_call(
+        kernel,
+        grid=(n, nb),
+        in_specs=[pick(e) for e in range(n)],
+        out_specs=pl.BlockSpec((block, t), lambda i, j: (i * nb + j, 0)),
+        out_shape=jax.ShapeDtypeStruct((n * k, t), BF16),
+        compiler_params=params(),
+        name="turn_mixes",
+    )(*mixes)
+
+
+def out_grads(mix_t, d_parts, c, block=512):
+    n = len(d_parts)
+    k, t = mix_t.shape[0] // n, mix_t.shape[1]
     rows, d_model = d_parts[0].shape
     w = d_model // n
     nb = k // block
 
-    def kernel(c_ref, *refs):
-        mix, dp, out_ref, d_s = refs[:n], refs[n : 2 * n], refs[2 * n], refs[2 * n + 1]
+    def kernel(c_ref, m_ref, *refs):
+        dp, out_ref, d_s = refs[:n], refs[n], refs[n + 1]
         i, j = pl.program_id(0), pl.program_id(1)
 
         @pl.when((i == 0) & (j == 0))
@@ -504,19 +531,14 @@
                 for b in range(n):
                     d_s[e, b * rows : (b + 1) * rows, :] = dp[b ^ e][...]
 
-        for e in range(n):
-
-            @pl.when(i == e)
-            def _():
-                m = mix[e][:, pl.ds(pl.multiple_of(j * block, block), block)]
-                out_ref[...] = dot(m.T, d_s[e]).astype(BF16)
+        out_ref[...] = dot(m_ref[...], d_s[i]).astype(BF16)
 
     return pl.pallas_call(
         kernel,
         grid_spec=pltpu.PrefetchScalarGridSpec(
             num_scalar_prefetch=1,
             grid=(n, nb),
-            in_specs=[pl.BlockSpec((t, k), lambda i, j, c_ref: (0, 0))] * n
+            in_specs=[pl.BlockSpec((block, t), lambda i, j, c_ref: (i * nb + j, 0))]
             + [pl.BlockSpec((rows, w), lambda i, j, c_ref: (0, c_ref[0]))] * n,
             out_specs=pl.BlockSpec((block, w), lambda i, j, c_ref: ((c_ref[0] ^ i) * nb + j, 0)),
             scratch_shapes=[pltpu.VMEM((n, t, w), BF16)],
@@ -524,7 +546,7 @@
         out_shape=jax.ShapeDtypeStruct((n * k, w), BF16),
         compiler_params=params(),
         name="out_grads",
-    )(c, *mixes, *d_parts)
+    )(c, mix_t, *d_parts)
 
 
 def residual(x, parts, gain, c):
@@ -768,6 +790,7 @@
     qkv = dot(h1, w_qkv, 1, 0)
     mix, totals = attend_forward(qkv, hc, head_gains, cosine, sine, pos_col, pos_row)
     mixes = gather_ctx(mix)
+    mix_t = turn_mixes(mixes)
     attn_cols = out_proj(mixes, w_out_cols, c_vec).reshape(C, T, dc)
     attn_out = exchange_ctx([attn_cols[d] for d in range(C)])
     r1, h2 = residual(x_own, attn_out, gain_moe.reshape(1, D), c_vec)
@@ -793,7 +816,7 @@
         )
     mixed_rows, back_rows, hidden, d_expert_out, d_gate, d_up = (list(v) for v in zip(*done))
     back_in = exchange_ctx(back_rows)
-    back_sum = sum_shard(combine(place, back_in))
+    back_sum = sum_shard(combine(place, back_in, 0, D + back_extra, 768))
     mixed_in = exchange_ctx(mixed_rows)
     grad_gate, grad_up, grad_down = expert_grads(expert_in, d_gate, d_up, hidden, d_expert_out)
 
@@ -801,7 +824,7 @@
         back_sum, r1, h2, out_cot[0], hits_wide, router_wide, gain_moe.reshape(1, D), E
     )
     d_attn_parts = gather_ctx(d_attn_own)
-    grad_out_piece = sum_shard(out_grads(mixes, d_attn_parts, c_vec))
+    grad_out_piece = sum_shard(out_grads(mix_t, d_attn_parts, c_vec))
     d_attn = jnp.concatenate(d_attn_parts, axis=0)
     d_mix = dot(d_attn, w_out_rows, 1, 1).astype(BF16)
     d_q, d_kv, gain_grads = attend_backward(
@@ -834,7 +857,8 @@
     d_h1_in = exchange_ctx([d_h1_parts[d] for d in range(C)])
     grad_in = input_back(x_own, d_h1_in, d_r1, gain_attn.reshape(1, D))[None]
 
-    mixture = sum_shard(combine(place, mixed_in)).astype(F32)
+    halves = [sum_shard(combine(place, mixed_in, i * D // 2, (i + 1) * D // 2)) for i in range(2)]
+    mixture = jnp.concatenate(halves, axis=1).astype(F32)
     block_out = (r1 + mixture).astype(BF16)[None]
 
     out_parts = gather_ctx(grad_out_piece)

time: 689 us -> 695 us (level)
    ppermute x33, waiting for transfers between devices: 182 us -> 161 us  [exchange_ctx(): out.append(lax.ppermute(parts[d], 'ctx', [(i, i ^ d) for i in range(C)]))]
    reduce_scatter x4 -> x5, waiting for transfers between devices: 65.8 us -> 85.9 us  [sum_shard(): return lax.psum_scatter(v, 'shard', scatter_dimension=0, tiled=True)]
    pallas_call x2 -> x4, Pallas kernels: 23.2 us -> 30.9 us  [the longest x3 22.7 us: combine(): pl.pallas_call(kernel, grid=(pl.cdiv(hi - lo, block),), in_specs=[pl.Bloc...]
  transfers between devices with their start and end apart: 43 -> 44, of which waited for: 23 -> 21; matrix products, arithmetic and copies ran while one was open for 12% -> 12% of each run, Pallas kernels for 24% -> 25%
where the time goes in v2:
time: 695 us; the launch traced here: 685 us
  waiting for transfers between devices  330 us (47%)
  Pallas kernels  183 us (26%)
  matrix products  47.7 us (7%)
  starting transfers between devices  42 us (6%)
  local copies, waits for them, and re-layouts  33.9 us (5%)
  other arithmetic  17.1 us (2%)
  blocking collectives  16 us (2%)
  between operations  14.9 us (2%)
    ppermute x33, waiting for transfers between devices, exchange_ctx(): out.append(lax.ppermute(parts[d], 'ctx', [(i, i ^ d) for i in range(C)]))  161 us
    reduce_scatter x5, waiting for transfers between devices, sum_shard(): return lax.psum_scatter(v, 'shard', scatter_dimension=0, tiled=True)  85.9 us
    all_gather x5, waiting for transfers between devices, gather_shard(): return lax.all_gather(v, 'shard', axis=0, tiled=True)  82.9 us
    pallas_call x4, Pallas kernels, expert_piece(): pl.pallas_call(kernel, in_specs=[pl.BlockSpec(memory_space=pltpu.SMEM)] +...  50 us
    dot_general x12, matrix products, dot(): lax.dot_general(a, b, (((ca,), (cb,)), ((), ())), preferred_element_type=...  47.7 us
    ppermute x33, starting transfers between devices, exchange_ctx(): out.append(lax.ppermute(parts[d], 'ctx', [(i, i ^ d) for i in range(C)]))  40.9 us
    pallas_call x3, Pallas kernels, combine(): pl.pallas_call(kernel, grid=(pl.cdiv(hi - lo, block),), in_specs=[pl.Bloc...  22.7 us
    pallas_call x1, Pallas kernels, expert_grads(): pl.pallas_call(kernel, grid=(d // block,), in_specs=[part] * n + [whole]...  19.1 us
  transfers between devices with their start and end apart: 44, of which 21 were waited for; matrix products, arithmetic and copies ran while one was open for 12% of the time, Pallas kernels for 25%

profile of v2, /device:TPU:0, one launch (start us, length us, event | category | flops | bytes accessed | tf_op | source)
XLA Modules:
  0.0 685.0 jit_solution(13798008604378808759)
XLA Ops:
  18.6 16.0 %all_gather.18 = bf16[1024,128]{1,0:T(8,128)(2,1)S(1)} all-gather(bf16[128,128]{1,0:T(8,128)(2,1)S(1)} %concatenate.34), channel_id=1, replica_groups=mesh['ctx'=4,'shard'=8] {'shard'}, dimensions={0}, use_global_device_ids=true | all-gather | bytes 294912 | tf_op jit(solution)/shard_map/all_gather | solution.py:709
  48.9 22.1 %all-gather.6.cloned.1.call-done = bf16[2048,1280]{1,0:T(8,128)(2,1)} async-done(((bf16[256,1280]{1,0:T(8,128)(2,1)}), bf16[2048,1280]{1,0:T(8,128)(2,1)}) %all-gather.6.cloned.1.call-update) | async-done | bytes 5242896 | tf_op jit(solution)/shard_map/all_gather | solution.py:709
  78.4 12.0 %attend_forward.1 = (bf16[512,1024]{1,0:T(8,128)(2,1)}, f32[512,128]{1,0:T(8,128)}) custom-call(f32[512,1280]{1,0:T(8,128)} %fusion.35.q_ref.k_ref.v_ref, f32[512,1280]{1,0:T(8,128)} %fusion.35.q_ref.k_ref.v_ref, f32[512,1280]{1,0:T(8,128)} %fusion.35.q_ref.k_ref.v_ref, f32[8,128]{1,0:T(8,128)} %maximum_maximum_fusion.gain_ref, ...), custom_call_target="tpu_custom_call" | custom-call | tf_op jit(solution)/shard_map/attend_forward/pallas_call | solution.py:79
  93.9 24.8 %all-gather.8.cloned.1.call-done.refs_4_ = bf16[4096,512]{1,0:T(8,128)(2,1)} async-done(((bf16[512,512]{1,0:T(8,128)(2,1)}), bf16[4096,512]{1,0:T(8,128)(2,1)}) %all-gather.8.cloned.1.call-update) | async-done | bytes 4194320 | tf_op jit(solution)/shard_map/all_gather | solution.py:709
  118.7 20.9 %collective-permute-done.4.refs_2_ = bf16[512,1024]{1,0:T(8,128)(2,1)} collective-permute-done((bf16[512,1024]{1,0:T(8,128)(2,1)}, bf16[512,1024]{1,0:T(8,128)(2,1)}, u32[]{:S(2)}, u32[]{:S(2)}) %collective-permute-start.4) | collective-permute-done | bytes 1048608 | tf_op jit(solution)/shard_map/ppermute | solution.py:702
  186.2 30.3 %all-gather.10.cloned.1.call-done = bf16[1024,2048]{1,0:T(8,128)(2,1)} async-done(((bf16[128,2048]{1,0:T(8,128)(2,1)}), bf16[1024,2048]{1,0:T(8,128)(2,1)}) %all-gather.10.cloned.1.call-update) | async-done | bytes 4194320 | tf_op jit(solution)/shard_map/all_gather | solution.py:709
  232.5 23.7 %collective-permute-done.9.x_ref.refs_1_ = bf16[272,2048]{1,0:T(8,128)(2,1)} collective-permute-done((bf16[272,2048]{1,0:T(8,128)(2,1)}, bf16[272,2048]{1,0:T(8,128)(2,1)}, u32[]{:S(2)}, u32[]{:S(2)}) %collective-permute-start.9) | collective-permute-done | bytes 1114144 | tf_op jit(solution)/shard_map/ppermute | solution.py:702
  256.2 12.6 %expert_piece.5 = (bf16[272,2048]{1,0:T(8,128)(2,1)}, bf16[272,2176]{1,0:T(8,128)(2,1)}, bf16[272,768]{1,0:T(8,128)(2,1)}, bf16[272,2048]{1,0:T(8,128)(2,1)}, bf...) custom-call(s32[1]{0:T(128)} %bitcast.10.me_ref, bf16[272,2048]{1,0:T(8,128)(2,1)} %collective-permute-done.9.x_ref.refs_1_, ...), custom_call_target="tpu_custom_call" | custom-call | tf_op jit(solution)/shard_map/expert_piece/pallas_call | solution.py:221
  270.2 11.2 %collective-permute-done.12.x_ref.refs_2_ = bf16[272,2048]{1,0:T(8,128)(2,1)} collective-permute-done((bf16[272,2048]{1,0:T(8,128)(2,1)}, bf16[272,2048]{1,0:T(8,128)(2,1)}, u32[]{:S(2)}, u32[]{:S(2)}) %collective-permute-start.12) | collective-permute-done | bytes 1114144 | tf_op jit(solution)/shard_map/ppermute | solution.py:702
  281.3 12.4 %expert_piece.6 = (bf16[272,2048]{1,0:T(8,128)(2,1)}, bf16[272,2176]{1,0:T(8,128)(2,1)}, bf16[272,768]{1,0:T(8,128)(2,1)}, bf16[272,2048]{1,0:T(8,128)(2,1)}, bf...) custom-call(s32[1]{0:T(128)} %bitcast.10.me_ref, bf16[272,2048]{1,0:T(8,128)(2,1)} %collective-permute-done.12.x_ref.refs_2_, ...), custom_call_target="tpu_custom_call" | custom-call | tf_op jit(solution)/shard_map/expert_piece/pallas_call | solution.py:221
  294.4 12.6 %expert_piece.7 = (bf16[272,2048]{1,0:T(8,128)(2,1)}, bf16[272,2176]{1,0:T(8,128)(2,1)}, bf16[272,768]{1,0:T(8,128)(2,1)}, bf16[272,2048]{1,0:T(8,128)(2,1)}, bf...) custom-call(s32[1]{0:T(128)} %bitcast.10.me_ref, bf16[272,2048]{1,0:T(8,128)(2,1)} %collective-permute-done.15.x_ref.refs_3_, ...), custom_call_target="tpu_custom_call" | custom-call | tf_op jit(solution)/shard_map/expert_piece/pallas_call | solution.py:221
  315.3 12.4 %expert_piece.4 = (bf16[272,2048]{1,0:T(8,128)(2,1)}, bf16[272,2176]{1,0:T(8,128)(2,1)}, bf16[272,768]{1,0:T(8,128)(2,1)}, bf16[272,2048]{1,0:T(8,128)(2,1)}, bf...) custom-call(s32[1]{0:T(128)} %bitcast.10.me_ref, bf16[272,2048]{1,0:T(8,128)(2,1)} %convolution_convert_fusion.7.x_ref.refs_0_, ...), custom_call_target="tpu_custom_call" | custom-call | tf_op jit(solution)/shard_map/expert_piece/pallas_call | solution.py:221
  327.8 13.8 %collective-permute-done.19.refs_2_ = bf16[272,2176]{1,0:T(8,128)(2,1)S(1)} collective-permute-done((bf16[272,2176]{1,0:T(8,128)(2,1)}, bf16[272,2176]{1,0:T(8,128)(2,1)S(1)}, u32[]{:S(2)}, u32[]{:S(2)}) %collective-permute-start.19) | collective-permute-done | bytes 1183776 | tf_op jit(solution)/shard_map/ppermute | solution.py:702
  343.0 10.0 %shard_map.265 = bf16[1024,2176]{1,0:T(8,128)(2,1)} custom-call(bf16[1024,1088]{1,0:T(8,128)(2,1)} %get-tuple-element.63.place_ref, bf16[272,2176]{1,0:T(8,128)(2,1)} %get-tuple-element.73.refs_0_, bf16[272,2176]{1,0:T(8,128)(2,1)} %copy-done.11, bf16[272,2176]{1,0:T(8,128)(2,1)} %copy-done.13, bf16[272,2176]{1,0:T(8,128)(2,1)} %copy-done.14), custom_call_target="tpu_custom_call" | custom-call | tf_op jit(solution)/shard_map/pallas_call | solution.py:301
  354.7 62.6 %reduce-scatter.10.cloned.1.call-done.back_ref = bf16[128,2176]{1,0:T(8,128)(2,1)} async-done(((bf16[1024,2176]{1,0:T(8,128)(2,1)}), bf16[128,2176]{1,0:T(8,128)(2,1)}) %reduce-scatter.10.cloned.1.call-update) | async-done | bytes 557072 | tf_op jit(solution)/shard_map/reduce_scatter | solution.py:712
  436.3 10.8 %collective-permute-done.22.refs_2_ = bf16[128,2048]{1,0:T(8,128)(2,1)S(1)} collective-permute-done((bf16[128,2048]{1,0:T(8,128)(2,1)}, bf16[128,2048]{1,0:T(8,128)(2,1)S(1)}, u32[]{:S(2)}, u32[]{:S(2)}) %collective-permute-start.22) | collective-permute-done | bytes 524320 | tf_op jit(solution)/shard_map/ppermute | solution.py:702
  471.2 16.7 %attend_backward.1 = (bf16[512,1024]{1,0:T(8,128)(2,1)}, bf16[512,256]{1,0:T(8,128)(2,1)}, f32[8,128]{1,0:T(8,128)}) custom-call(f32[512,1280]{1,0:T(8,128)} %fusion.35.q_ref.k_ref.v_ref, f32[512,1280]{1,0:T(8,128)} %fusion.35.q_ref.k_ref.v_ref, f32[512,1280]{1,0:T(8,128)} %fusion.35.q_ref.k_ref.v_ref, bf16[512,1024]{1,0:T(8,128)(2,1)} %fusion.11.dm_ref, ...), custom_call_target="tpu_custom_call" | custom-call | tf_op jit(solution)/shard_map/attend_backward/pallas_call | solution.py:148
  498.9 8.8 %weight_grads.1 = bf16[2048,1408]{1,0:T(8,128)(2,1)} custom-call(bf16[512,2048]{1,0:T(8,128)(2,1)} %norm_rows.1.h_ref, bf16[512,1024]{1,0:T(8,128)(2,1)} %get-tuple-element.80.q_ref, bf16[512,256]{1,0:T(8,128)(2,1)} %get-tuple-element.81.kv_ref, bf16[2048,128]{1,0:T(8,128)(2,1)} %add_convert_fusion.small_ref), custom_call_target="tpu_custom_call" | custom-call | tf_op jit(solution)/shard_map/weight_grads/pallas_call | solution.py:365
  512.4 23.9 %collective-permute-done.11.refs_1_ = bf16[272,2048]{1,0:T(8,128)(2,1)S(1)} collective-permute-done((bf16[272,2048]{1,0:T(8,128)(2,1)S(1)}, bf16[272,2048]{1,0:T(8,128)(2,1)S(1)}, u32[]{:S(2)}, u32[]{:S(2)}) %collective-permute-start.11) | collective-permute-done | bytes 1114144 | tf_op jit(solution)/shard_map/ppermute | solution.py:702
  536.4 24.6 %collective-permute-done.14.refs_2_ = bf16[272,2048]{1,0:T(8,128)(2,1)S(1)} collective-permute-done((bf16[272,2048]{1,0:T(8,128)(2,1)}, bf16[272,2048]{1,0:T(8,128)(2,1)S(1)}, u32[]{:S(2)}, u32[]{:S(2)}) %collective-permute-start.14) | collective-permute-done | bytes 1114144 | tf_op jit(solution)/shard_map/ppermute | solution.py:702
  594.3 8.5 %collective-permute-done.26.refs_2_ = bf16[128,2048]{1,0:T(8,128)(2,1)S(1)} collective-permute-done((bf16[128,2048]{1,0:T(8,128)(2,1)}, bf16[128,2048]{1,0:T(8,128)(2,1)S(1)}, u32[]{:S(2)}, u32[]{:S(2)}) %collective-permute-start.26) | collective-permute-done | bytes 524320 | tf_op jit(solution)/shard_map/ppermute | solution.py:702
  606.8 8.5 %collective-permute-done.31.refs_1_ = bf16[512,512]{1,0:T(8,128)(2,1)S(1)} collective-permute-done((bf16[512,512]{1,0:T(8,128)(2,1)}, bf16[512,512]{1,0:T(8,128)(2,1)S(1)}, u32[]{:S(2)}, u32[]{:S(2)}) %collective-permute-start.31) | collective-permute-done | bytes 524320 | tf_op jit(solution)/shard_map/ppermute | solution.py:702
  616.8 19.1 %expert_grads.1 = (f32[2048,768]{1,0:T(8,128)}, f32[2048,768]{1,0:T(8,128)}, f32[768,2048]{1,0:T(8,128)}) custom-call(bf16[272,2048]{1,0:T(8,128)(2,1)} %convolution_convert_fusion.7.x_ref.refs_0_, bf16[272,2048]{1,0:T(8,128)(2,1)} %collective-permute-done.9.x_ref.refs_1_, bf16[272,2048]{1,0:T(8,128)(2,1)} %collective-permute-done.12.x_ref.refs_2_, ...), custom_call_target="tpu_custom_call" | custom-call | tf_op jit(solution)/shard_map/expert_grads/pallas_call | solution.py:269
  635.9 22.0 %reduce-scatter.6.cloned.1.call-done = bf16[128,1024]{1,0:T(8,128)(2,1)} async-done(((bf16[1024,1024]{1,0:T(8,128)(2,1)}), bf16[128,1024]{1,0:T(8,128)(2,1)}) %reduce-scatter.6.cloned.1.call-update) | async-done | bytes 262160 | tf_op jit(solution)/shard_map/reduce_scatter | solution.py:712
  (281 shorter events, 229.7 us)
Async XLA Ops:
  7.2 63.7 %all-gather.6.cloned.1.call-start = ((), (), s32[]{:S(2)}) async-start(), calls=%async_computation.5 | async-start | bytes 5898240 | tf_op jit(solution)/shard_map/all_gather | solution.py:709
  10.3 108.4 %all-gather.8.cloned.1.call-start = ((), (), s32[]{:S(2)}) async-start(), calls=%async_computation.6 | async-start | bytes 4718592 | tf_op jit(solution)/shard_map/all_gather | solution.py:709
  11.3 161.3 %all-gather.12.cloned.1.call-start = ((), (), s32[]{:S(2)}) async-start(), calls=%async_computation.8 | async-start | bytes 5013504 | tf_op jit(solution)/shard_map/all_gather | solution.py:709
  13.0 203.5 %all-gather.10.cloned.1.call-start = ((), (), s32[]{:S(2)}) async-start(), calls=%async_computation.7 | async-start | bytes 4718592 | tf_op jit(solution)/shard_map/all_gather | solution.py:709
  159.9 257.3 %reduce-scatter.10.cloned.1.call-start = ((), (), s32[]{:S(2)}) async-start(), calls=%async_computation.11 | async-start | bytes 5013504 | tf_op jit(solution)/shard_map/reduce_scatter | solution.py:712
  177.7 51.3 %collective-permute-start.10 = (bf16[272,2176]{1,0:T(8,128)(2,1)}, bf16[272,2176]{1,0:T(8,128)(2,1)S(1)}, u32[]{:S(2)}, u32[]{:S(2)}) collective-permute-start(bf16[272,2176]{1,0:T(8,128)(2,1)} %convolution_convert_fusion.2), channel_id=1, source_target_pairs={{0,8},{8,0},{16,24},{24,16},{1,9},{9,1},{17,25},{25,17},{2,10},{10... | collective-permute-start | bytes 3551240 | tf_op jit(solution)/shard_map/ppermute | solution.py:702
  181.5 88.6 %collective-permute-start.13 = (bf16[272,2176]{1,0:T(8,128)(2,1)}, bf16[272,2176]{1,0:T(8,128)(2,1)}, u32[]{:S(2)}, u32[]{:S(2)}) collective-permute-start(bf16[272,2176]{1,0:T(8,128)(2,1)} %convolution_convert_fusion.1), channel_id=1, source_target_pairs={{0,16},{8,24},{16,0},{24,8},{1,17},{9,25},{17,1},{25,9},{2,18},{10... | collective-permute-start | bytes 3551240 | tf_op jit(solution)/shard_map/ppermute | solution.py:702
  185.1 109.3 %collective-permute-start.16 = (bf16[272,2176]{1,0:T(8,128)(2,1)}, bf16[272,2176]{1,0:T(8,128)(2,1)}, u32[]{:S(2)}, u32[]{:S(2)}) collective-permute-start(bf16[272,2176]{1,0:T(8,128)(2,1)} %convolution_convert_fusion), channel_id=1, source_target_pairs={{0,24},{8,16},{16,8},{24,0},{1,25},{9,17},{17,9},{25,1},{2,26},{10... | collective-permute-start | bytes 3551240 | tf_op jit(solution)/shard_map/ppermute | solution.py:702
  225.2 56.2 %collective-permute-start.12 = (bf16[272,2048]{1,0:T(8,128)(2,1)}, bf16[272,2048]{1,0:T(8,128)(2,1)}, u32[]{:S(2)}, u32[]{:S(2)}) collective-permute-start(bf16[272,2048]{1,0:T(8,128)(2,1)} %convolution_convert_fusion.5), channel_id=1, source_target_pairs={{0,16},{8,24},{16,0},{24,8},{1,17},{9,25},{17,1},{25,9},{2,18},{10... | collective-permute-start | bytes 3342344 | tf_op jit(solution)/shard_map/ppermute | solution.py:702
  229.0 65.3 %collective-permute-start.15 = (bf16[272,2048]{1,0:T(8,128)(2,1)}, bf16[272,2048]{1,0:T(8,128)(2,1)}, u32[]{:S(2)}, u32[]{:S(2)}) collective-permute-start(bf16[272,2048]{1,0:T(8,128)(2,1)} %convolution_convert_fusion.4), channel_id=1, source_target_pairs={{0,24},{8,16},{16,8},{24,0},{1,25},{9,17},{17,9},{25,1},{2,26},{10... | collective-permute-start | bytes 3342344 | tf_op jit(solution)/shard_map/ppermute | solution.py:702
  268.8 58.9 %collective-permute-start.18 = (bf16[272,2176]{1,0:T(8,128)(2,1)}, bf16[272,2176]{1,0:T(8,128)(2,1)S(1)}, u32[]{:S(2)}, u32[]{:S(2)}) collective-permute-start(bf16[272,2176]{1,0:T(8,128)(2,1)} %get-tuple-element.74), channel_id=1, source_target_pairs={{0,8},{8,0},{16,24},{24,16},{1,9},{9,1},{17,25},{25,17},{2,10},{10... | collective-permute-start | bytes 3551240 | tf_op jit(solution)/shard_map/ppermute | solution.py:702
  293.7 47.8 %collective-permute-start.19 = (bf16[272,2176]{1,0:T(8,128)(2,1)}, bf16[272,2176]{1,0:T(8,128)(2,1)S(1)}, u32[]{:S(2)}, u32[]{:S(2)}) collective-permute-start(bf16[272,2176]{1,0:T(8,128)(2,1)} %get-tuple-element.75), channel_id=1, source_target_pairs={{0,16},{8,24},{16,0},{24,8},{1,17},{9,25},{17,1},{25,9},{2,18},{10... | collective-permute-start | bytes 3551240 | tf_op jit(solution)/shard_map/ppermute | solution.py:702
  353.0 112.6 %all-gather.14.cloned.1.call-start = ((), (), s32[]{:S(2)}) async-start(), calls=%async_computation.12 | async-start | bytes 4718592 | tf_op jit(solution)/shard_map/all_gather | solution.py:709
  354.6 226.9 %reduce-scatter.14.cloned.1.call-start = ((), (), s32[]{:S(2)}) async-start(), calls=%async_computation.14 | async-start | bytes 4718592 | tf_op jit(solution)/shard_map/reduce_scatter | solution.py:712
  457.1 126.3 %reduce-scatter.12.cloned.1.call-start = ((), (), s32[]{:S(2)}) async-start(), calls=%async_computation.13 | async-start | bytes 6488064 | tf_op jit(solution)/shard_map/reduce_scatter | solution.py:712
  507.7 128.2 %reduce-scatter.8.cloned.1.call-start = ((), (), s32[]{:S(2)}) async-start(), calls=%async_computation.10 | async-start | bytes 2359296 | tf_op jit(solution)/shard_map/reduce_scatter | solution.py:712
  510.4 50.6 %collective-permute-start.14 = (bf16[272,2048]{1,0:T(8,128)(2,1)}, bf16[272,2048]{1,0:T(8,128)(2,1)S(1)}, u32[]{:S(2)}, u32[]{:S(2)}) collective-permute-start(bf16[272,2048]{1,0:T(8,128)(2,1)} %get-tuple-element.70), channel_id=1, source_target_pairs={{0,16},{8,24},{16,0},{24,8},{1,17},{9,25},{17,1},{25,9},{2,18},{10... | collective-permute-start | bytes 3342344 | tf_op jit(solution)/shard_map/ppermute | solution.py:702
  511.9 49.1 %collective-permute-start.17 = (bf16[272,2048]{1,0:T(8,128)(2,1)}, bf16[272,2048]{1,0:T(8,128)(2,1)S(1)}, u32[]{:S(2)}, u32[]{:S(2)}) collective-permute-start(bf16[272,2048]{1,0:T(8,128)(2,1)} %get-tuple-element.72), channel_id=1, source_target_pairs={{0,24},{8,16},{16,8},{24,0},{1,25},{9,17},{17,9},{25,1},{2,26},{10... | collective-permute-start | bytes 3342344 | tf_op jit(solution)/shard_map/ppermute | solution.py:702
  568.6 89.3 %reduce-scatter.6.cloned.1.call-start = ((), (), s32[]{:S(2)}) async-start(), calls=%async_computation.9 | async-start | bytes 2359296 | tf_op jit(solution)/shard_map/reduce_scatter | solution.py:712
  583.4 84.1 %collective-permute-start.28 = (bf16[256,1408]{1,0:T(8,128)(2,1)}, bf16[256,1408]{1,0:T(8,128)(2,1)S(1)}, u32[]{:S(2)}, u32[]{:S(2)}) collective-permute-start(bf16[256,1408]{1,0:T(8,128)(2,1)} %reduce-scatter.12.cloned.1.call-done.refs_0_), channel_id=1, source_target_pairs={{0,8},{8,0},{16,24},{24,16},{1,9},{9,1},{17,25},{25,17},{2,10},{10... | collective-permute-start | bytes 2162696 | tf_op jit(solution)/shard_map/ppermute | solution.py:702
  592.8 74.7 %collective-permute-start.29 = (bf16[256,1408]{1,0:T(8,128)(2,1)}, bf16[256,1408]{1,0:T(8,128)(2,1)S(1)}, u32[]{:S(2)}, u32[]{:S(2)}) collective-permute-start(bf16[256,1408]{1,0:T(8,128)(2,1)} %reduce-scatter.12.cloned.1.call-done.refs_0_), channel_id=1, source_target_pairs={{0,16},{8,24},{16,0},{24,8},{1,17},{9,25},{17,1},{25,9},{2,18},{10... | collective-permute-start | bytes 2162696 | tf_op jit(solution)/shard_map/ppermute | solution.py:702
  602.8 64.8 %collective-permute-start.30 = (bf16[256,1408]{1,0:T(8,128)(2,1)}, bf16[256,1408]{1,0:T(8,128)(2,1)}, u32[]{:S(2)}, u32[]{:S(2)}) collective-permute-start(bf16[256,1408]{1,0:T(8,128)(2,1)} %reduce-scatter.12.cloned.1.call-done.refs_0_), channel_id=1, source_target_pairs={{0,24},{8,16},{16,8},{24,0},{1,25},{9,17},{17,9},{25,1},{2,26},{10... | collective-permute-start | bytes 2162696 | tf_op jit(solution)/shard_map/ppermute | solution.py:702
  606.8 56.8 %collective-permute-start.32 = (bf16[512,512]{1,0:T(8,128)(2,1)}, bf16[512,512]{1,0:T(8,128)(2,1)}, u32[]{:S(2)}, u32[]{:S(2)}) collective-permute-start(bf16[512,512]{1,0:T(8,128)(2,1)} %reduce-scatter.14.cloned.1.call-done.refs_0_), channel_id=1, source_target_pairs={{0,16},{8,24},{16,0},{24,8},{1,17},{9,25},{17,1},{25,9},{2,18},{10... | collective-permute-start | bytes 1572872 | tf_op jit(solution)/shard_map/ppermute | solution.py:702
  615.3 48.3 %collective-permute-start.33 = (bf16[512,512]{1,0:T(8,128)(2,1)}, bf16[512,512]{1,0:T(8,128)(2,1)}, u32[]{:S(2)}, u32[]{:S(2)}) collective-permute-start(bf16[512,512]{1,0:T(8,128)(2,1)} %reduce-scatter.14.cloned.1.call-done.refs_0_), channel_id=1, source_target_pairs={{0,24},{8,16},{16,8},{24,0},{1,25},{9,17},{17,9},{25,1},{2,26},{10... | collective-permute-start | bytes 1572872 | tf_op jit(solution)/shard_map/ppermute | solution.py:702
  (73 other events, 902.5 us)
Sparse Core Ops, SparseCore 0:
  10.5 60.4 all-gather.5
  73.1 45.5 all-gather.7
  120.9 47.8 all-gather.11
  170.9 45.6 all-gather.9
  353.1 64.0 reduce-scatter.9
  418.7 46.8 all-gather.13
  468.5 48.7 reduce-scatter.13
  520.1 63.2 reduce-scatter.11
  586.3 34.5 reduce-scatter.7
  623.0 34.8 reduce-scatter.5

commit v3 on v2

--- a/solution.py
+++ b/solution.py
@@ -96,7 +96,7 @@
         ],
         scratch_shapes=[pltpu.VMEM((n, hs), BF16), pltpu.VMEM((n, 2 * hs), BF16), pltpu.VMEM((n, n), F32)],
         compiler_params=params(),
-        name="attend_forward",
+        name="attend",
     )(qkv, qkv, qkv, gains, cosine, sine, pos_col, pos_row)
 
 
@@ -175,7 +175,7 @@
             pltpu.VMEM((n, n), F32),
         ],
         compiler_params=params(),
-        name="attend_backward",
+        name="unattend",
     )(qkv, qkv, qkv, d_mix, mix, totals, gains, cosine, sine, pos_col, pos_row)
 
 
@@ -282,7 +282,7 @@
             pltpu.VMEM((f, n * r), BF16),
         ],
         compiler_params=params(),
-        name="expert_grads",
+        name="exgrads",
     )(*xs, *dgs, *dus, *hids, *deos)
 
 
@@ -374,7 +374,7 @@
         out_specs=pl.BlockSpec((block, qc + kc + sc), lambda j: (j, 0)),
         out_shape=jax.ShapeDtypeStruct((d, qc + kc + sc), BF16),
         compiler_params=params(),
-        name="weight_grads",
+        name="wgrads",
     )(h1, d_q, d_kv, small)
 
 
@@ -394,8 +394,36 @@
         out_specs=vm,
         out_shape=jax.ShapeDtypeStruct((rows, n * w), F32),
         compiler_params=params(),
-        name="assemble_columns",
+        name="columns",
     )(c, *parts)
+
+
+def pack(w_query, w_key, w_value, at, qc):
+    ws = w_query.shape[0]
+    hs = HEAD_SIZE
+
+    def kernel(at_ref, q_ref, k_ref, v_ref, out_ref):
+        out_ref[:, :qc] = q_ref[...]
+        out_ref[:, qc : qc + hs] = k_ref[...]
+        out_ref[:, qc + hs :] = v_ref[...]
+
+    head_spec = pl.BlockSpec((ws, hs), lambda j, at_ref: (0, at_ref[1]))
+    return pl.pallas_call(
+        kernel,
+        grid_spec=pltpu.PrefetchScalarGridSpec(
+            num_scalar_prefetch=1,
+            grid=(1,),
+            in_specs=[
+                pl.BlockSpec((ws, qc), lambda j, at_ref: (0, at_ref[0])),
+                head_spec,
+                head_spec,
+            ],
+            out_specs=pl.BlockSpec((ws, qc + 2 * hs), lambda j, at_ref: (0, 0)),
+        ),
+        out_shape=jax.ShapeDtypeStruct((ws, qc + 2 * hs), BF16),
+        compiler_params=params(),
+        name="pack",
+    )(at, w_query, w_key, w_value)
 
 
 def plan(targets, rows, block=LANES):
@@ -510,7 +538,7 @@
         out_specs=pl.BlockSpec((block, t), lambda i, j: (i * nb + j, 0)),
         out_shape=jax.ShapeDtypeStruct((n * k, t), BF16),
         compiler_params=params(),
-        name="turn_mixes",
+        name="turn",
     )(*mixes)
 
 
@@ -643,7 +671,7 @@
         out_specs=vm,
         out_shape=jax.ShapeDtypeStruct(x.shape, F32),
         compiler_params=params(),
-        name="input_back",
+        name="inback",
     )(x, d_r1, gain, *parts)
 
 
@@ -711,15 +739,8 @@
     def sum_shard(v):
         return lax.psum_scatter(v, "shard", scatter_dimension=0, tiled=True)
 
-    kv = c // share
-    packed = jnp.concatenate(
-        [
-            lax.dynamic_slice_in_dim(w_query, c * qc, qc, 1),
-            lax.dynamic_slice_in_dim(w_key, kv * HEAD_SIZE, HEAD_SIZE, 1),
-            lax.dynamic_slice_in_dim(w_value, kv * HEAD_SIZE, HEAD_SIZE, 1),
-        ],
-        axis=1,
-    )
+    at = jnp.stack([c, c // share]).astype(jnp.int32)
+    packed = pack(w_query, w_key, w_value, at, qc)
     w_qkv = gather_shard(packed)
     hits = (
         (routes[0][:, :, None] == jnp.arange(E, dtype=jnp.int32)[None, None, :])
@@ -754,8 +775,11 @@
         axis=0,
     )
 
-    spread = [((p % C) * S + p // C, p) for p in range(E)]
-    piece = lax.ppermute(lax.dynamic_slice_in_dim(w_out, c * po, po, 0), ("ctx", "shard"), spread)
+    pieces = []
+    for i in range(C):
+        pairs = [(p // S * S + p // C, p) for p in range(E) if p % C == i]
+        pieces.append(lax.ppermute(w_out[i * po : (i + 1) * po], ("ctx", "shard"), pairs))
+    piece = sum(pieces[1:], pieces[0])
     w_out_rows = gather_shard(piece)
     dc = D // C
     w_out_cols = gather_shard(lax.dynamic_slice_in_dim(w_out, c * dc, dc, 1))
@@ -810,7 +834,7 @@
     me_vec = me.astype(jnp.int32).reshape(1)
     back_extra = round_up(2 * E, LANES)
     done = [None] * C
-    for d in [0, C - 1] + list(range(1, C - 1)):
+    for d in [0] + list(range(C - 1, 0, -1)):
         done[d] = expert_piece(
             expert_in[d], cot_in[d], router_wide, wg, wu, wd, me_vec, E, back_extra
         )

time: 695 us -> 712 us (1.024)
  starting transfers between devices: 42 us -> 53.7 us
  waiting for transfers between devices: 330 us -> 338 us
    ppermute x1 -> x4, waiting for transfers between devices: 0.01 us -> 39.8 us  [layer(): lax.ppermute(w_out[i * po:(i + 1) * po], ('ctx', 'shard'), pairs)]
    reduce_scatter x5, waiting for transfers between devices: 85.9 us -> 57.1 us  [sum_shard(): return lax.psum_scatter(v, 'shard', scatter_dimension=0, tiled=True)]
    unnamed x113 -> x115, local copies, waits for them, and re-layouts: 13.1 us -> 16.6 us
  transfers between devices with their start and end apart: 44 -> 47, of which waited for: 21 -> 23; matrix products, arithmetic and copies ran while one was open for 12% -> 10% of each run, Pallas kernels for 25% -> 24%
where the time goes in v3:
time: 712 us; the launch traced here: 702 us
  waiting for transfers between devices  338 us (47%)
  Pallas kernels  186 us (26%)
  starting transfers between devices  53.7 us (8%)
  matrix products  46.4 us (7%)
  local copies, waits for them, and re-layouts  33 us (5%)
  blocking collectives  16 us (2%)
  between operations  15 us (2%)
  other arithmetic  14.5 us (2%)
    ppermute x33, waiting for transfers between devices, exchange_ctx(): out.append(lax.ppermute(parts[d], 'ctx', [(i, i ^ d) for i in range(C)]))  156 us
    all_gather x5, waiting for transfers between devices, gather_shard(): return lax.all_gather(v, 'shard', axis=0, tiled=True)  84.4 us
    reduce_scatter x5, waiting for transfers between devices, sum_shard(): return lax.psum_scatter(v, 'shard', scatter_dimension=0, tiled=True)  57.1 us
    pallas_call x4, Pallas kernels, expert_piece(): pl.pallas_call(kernel, in_specs=[pl.BlockSpec(memory_space=pltpu.SMEM)] +...  50 us
    dot_general x12, matrix products, dot(): lax.dot_general(a, b, (((ca,), (cb,)), ((), ())), preferred_element_type=...  46.4 us
    ppermute x33, starting transfers between devices, exchange_ctx(): out.append(lax.ppermute(parts[d], 'ctx', [(i, i ^ d) for i in range(C)]))  46.1 us
    ppermute x4, waiting for transfers between devices, layer(): lax.ppermute(w_out[i * po:(i + 1) * po], ('ctx', 'shard'), pairs)  39.8 us
    pallas_call x3, Pallas kernels, combine(): pl.pallas_call(kernel, grid=(pl.cdiv(hi - lo, block),), in_specs=[pl.Bloc...  22.7 us
  transfers between devices with their start and end apart: 47, of which 23 were waited for; matrix products, arithmetic and copies ran while one was open for 10% of the time, Pallas kernels for 24%

profile of v3, /device:TPU:0, one launch (start us, length us, event | category | flops | bytes accessed | tf_op | source)
XLA Modules:
  0.0 702.1 jit_solution(4837004761166626823)
XLA Ops:
  19.5 16.0 %all_gather.18 = bf16[1024,128]{1,0:T(8,128)(2,1)S(1)} all-gather(bf16[128,128]{1,0:T(8,128)(2,1)S(1)} %concatenate.31), channel_id=1, replica_groups=mesh['ctx'=4,'shard'=8] {'shard'}, dimensions={0}, use_global_device_ids=true | all-gather | bytes 294912 | tf_op jit(solution)/shard_map/all_gather | solution.py:737
  49.5 21.9 %all-gather.6.cloned.1.call-done = bf16[2048,1280]{1,0:T(8,128)(2,1)} async-done(((bf16[256,1280]{1,0:T(8,128)(2,1)}), bf16[2048,1280]{1,0:T(8,128)(2,1)}) %all-gather.6.cloned.1.call-update) | async-done | bytes 5242896 | tf_op jit(solution)/shard_map/all_gather | solution.py:737
  78.9 12.0 %attend.1 = (bf16[512,1024]{1,0:T(8,128)(2,1)}, f32[512,128]{1,0:T(8,128)}) custom-call(f32[512,1280]{1,0:T(8,128)} %fusion.36.q_ref.k_ref.v_ref, f32[512,1280]{1,0:T(8,128)} %fusion.36.q_ref.k_ref.v_ref, f32[512,1280]{1,0:T(8,128)} %fusion.36.q_ref.k_ref.v_ref, f32[8,128]{1,0:T(8,128)} %maximum_maximum_fusion.gain_ref, ...), custom_call_target="tpu_custom_call" | custom-call | tf_op jit(solution)/shard_map/attend/pallas_call | solution.py:79
  94.4 24.7 %all-gather.8.cloned.1.call-done.refs_4_ = bf16[4096,512]{1,0:T(8,128)(2,1)} async-done(((bf16[512,512]{1,0:T(8,128)(2,1)}), bf16[4096,512]{1,0:T(8,128)(2,1)}) %all-gather.8.cloned.1.call-update) | async-done | bytes 4194320 | tf_op jit(solution)/shard_map/all_gather | solution.py:737
  119.1 20.9 %collective-permute-done.4.refs_2_ = bf16[512,1024]{1,0:T(8,128)(2,1)S(1)} collective-permute-done((bf16[512,1024]{1,0:T(8,128)(2,1)}, bf16[512,1024]{1,0:T(8,128)(2,1)S(1)}, u32[]{:S(2)}, u32[]{:S(2)}) %collective-permute-start.4) | collective-permute-done | bytes 1048608 | tf_op jit(solution)/shard_map/ppermute | solution.py:730
  185.6 30.9 %all-gather.10.cloned.1.call-done = bf16[1024,2048]{1,0:T(8,128)(2,1)} async-done(((bf16[128,2048]{1,0:T(8,128)(2,1)}), bf16[1024,2048]{1,0:T(8,128)(2,1)}) %all-gather.10.cloned.1.call-update) | async-done | bytes 4194320 | tf_op jit(solution)/shard_map/all_gather | solution.py:737
  230.7 24.8 %collective-permute-done.9.x_ref.refs_1_ = bf16[272,2048]{1,0:T(8,128)(2,1)S(1)} collective-permute-done((bf16[272,2048]{1,0:T(8,128)(2,1)}, bf16[272,2048]{1,0:T(8,128)(2,1)S(1)}, u32[]{:S(2)}, u32[]{:S(2)}) %collective-permute-start.9) | collective-permute-done | bytes 1114144 | tf_op jit(solution)/shard_map/ppermute | solution.py:730
  256.5 12.6 %expert_piece.5 = (bf16[272,2048]{1,0:T(8,128)(2,1)}, bf16[272,2176]{1,0:T(8,128)(2,1)}, bf16[272,768]{1,0:T(8,128)(2,1)}, bf16[272,2048]{1,0:T(8,128)(2,1)}, bf...) custom-call(s32[1]{0:T(128)} %bitcast.10.me_ref, bf16[272,2048]{1,0:T(8,128)(2,1)} %copy-done.6, ...), custom_call_target="tpu_custom_call" | custom-call | tf_op jit(solution)/shard_map/expert_piece/pallas_call | solution.py:221
  270.6 9.7 %collective-permute-done.12.x_ref.refs_2_ = bf16[272,2048]{1,0:T(8,128)(2,1)S(1)} collective-permute-done((bf16[272,2048]{1,0:T(8,128)(2,1)}, bf16[272,2048]{1,0:T(8,128)(2,1)S(1)}, u32[]{:S(2)}, u32[]{:S(2)}) %collective-permute-start.12) | collective-permute-done | bytes 1114144 | tf_op jit(solution)/shard_map/ppermute | solution.py:730
  281.3 12.4 %expert_piece.6 = (bf16[272,2048]{1,0:T(8,128)(2,1)}, bf16[272,2176]{1,0:T(8,128)(2,1)}, bf16[272,768]{1,0:T(8,128)(2,1)}, bf16[272,2048]{1,0:T(8,128)(2,1)}, bf...) custom-call(s32[1]{0:T(128)} %bitcast.10.me_ref, bf16[272,2048]{1,0:T(8,128)(2,1)} %copy-done.7, ...), custom_call_target="tpu_custom_call" | custom-call | tf_op jit(solution)/shard_map/expert_piece/pallas_call | solution.py:221
  294.5 12.6 %expert_piece.7 = (bf16[272,2048]{1,0:T(8,128)(2,1)}, bf16[272,2176]{1,0:T(8,128)(2,1)}, bf16[272,768]{1,0:T(8,128)(2,1)}, bf16[272,2048]{1,0:T(8,128)(2,1)}, bf...) custom-call(s32[1]{0:T(128)} %bitcast.10.me_ref, bf16[272,2048]{1,0:T(8,128)(2,1)} %collective-permute-done.15.x_ref.refs_3_, ...), custom_call_target="tpu_custom_call" | custom-call | tf_op jit(solution)/shard_map/expert_piece/pallas_call | solution.py:221
  315.8 12.4 %expert_piece.4 = (bf16[272,2048]{1,0:T(8,128)(2,1)}, bf16[272,2176]{1,0:T(8,128)(2,1)}, bf16[272,768]{1,0:T(8,128)(2,1)}, bf16[272,2048]{1,0:T(8,128)(2,1)}, bf...) custom-call(s32[1]{0:T(128)} %bitcast.10.me_ref, bf16[272,2048]{1,0:T(8,128)(2,1)} %convolution_convert_fusion.7.x_ref.refs_0_, ...), custom_call_target="tpu_custom_call" | custom-call | tf_op jit(solution)/shard_map/expert_piece/pallas_call | solution.py:221
  328.2 14.3 %collective-permute-done.19.refs_2_ = bf16[272,2176]{1,0:T(8,128)(2,1)S(1)} collective-permute-done((bf16[272,2176]{1,0:T(8,128)(2,1)}, bf16[272,2176]{1,0:T(8,128)(2,1)S(1)}, u32[]{:S(2)}, u32[]{:S(2)}) %collective-permute-start.19) | collective-permute-done | bytes 1183776 | tf_op jit(solution)/shard_map/ppermute | solution.py:730
  344.1 10.0 %shard_map.265 = bf16[1024,2176]{1,0:T(8,128)(2,1)} custom-call(bf16[1024,1088]{1,0:T(8,128)(2,1)} %get-tuple-element.63.place_ref, bf16[272,2176]{1,0:T(8,128)(2,1)} %get-tuple-element.73.refs_0_, bf16[272,2176]{1,0:T(8,128)(2,1)} %copy-done.19, bf16[272,2176]{1,0:T(8,128)(2,1)} %copy-done.20, bf16[272,2176]{1,0:T(8,128)(2,1)} %copy-done.21), custom_call_target="tpu_custom_call" | custom-call | tf_op jit(solution)/shard_map/pallas_call | solution.py:301
  363.1 17.4 %collective-permute-done.27 = bf16[128,2048]{1,0:T(8,128)(2,1)S(1)} collective-permute-done((bf16[128,2048]{1,0:T(8,128)(2,1)S(1)}, bf16[128,2048]{1,0:T(8,128)(2,1)S(1)}, u32[]{:S(2)}, u32[]{:S(2)}) %collective-permute-start.27) | collective-permute-done | bytes 524320 | tf_op jit(solution)/shard_map/ppermute | solution.py:781
  380.4 22.5 %collective-permute-done.26 = bf16[128,2048]{1,0:T(8,128)(2,1)S(1)} collective-permute-done((bf16[128,2048]{1,0:T(8,128)(2,1)S(1)}, bf16[128,2048]{1,0:T(8,128)(2,1)S(1)}, u32[]{:S(2)}, u32[]{:S(2)}) %collective-permute-start.26) | collective-permute-done | bytes 524320 | tf_op jit(solution)/shard_map/ppermute | solution.py:781
  403.9 26.5 %reduce-scatter.10.cloned.1.call-done.back_ref = bf16[128,2176]{1,0:T(8,128)(2,1)} async-done(((bf16[1024,2176]{1,0:T(8,128)(2,1)}), bf16[128,2176]{1,0:T(8,128)(2,1)}) %reduce-scatter.10.cloned.1.call-update) | async-done | bytes 557072 | tf_op jit(solution)/shard_map/reduce_scatter | solution.py:740
  487.9 16.7 %unattend.1 = (bf16[512,1024]{1,0:T(8,128)(2,1)}, bf16[512,256]{1,0:T(8,128)(2,1)}, f32[8,128]{1,0:T(8,128)}) custom-call(f32[512,1280]{1,0:T(8,128)} %fusion.36.q_ref.k_ref.v_ref, f32[512,1280]{1,0:T(8,128)} %fusion.36.q_ref.k_ref.v_ref, f32[512,1280]{1,0:T(8,128)} %fusion.36.q_ref.k_ref.v_ref, bf16[512,1024]{1,0:T(8,128)(2,1)} %fusion.11.dm_ref, ...), custom_call_target="tpu_custom_call" | custom-call | tf_op jit(solution)/shard_map/unattend/pallas_call | solution.py:148
  514.2 8.8 %wgrads.1 = bf16[2048,1408]{1,0:T(8,128)(2,1)} custom-call(bf16[512,2048]{1,0:T(8,128)(2,1)} %norm_rows.1.h_ref, bf16[512,1024]{1,0:T(8,128)(2,1)} %get-tuple-element.80.q_ref, bf16[512,256]{1,0:T(8,128)(2,1)} %get-tuple-element.81.kv_ref, bf16[2048,128]{1,0:T(8,128)(2,1)} %add_convert_fusion.small_ref), custom_call_target="tpu_custom_call" | custom-call | tf_op jit(solution)/shard_map/wgrads/pallas_call | solution.py:365
  526.6 24.2 %collective-permute-done.11.refs_1_ = bf16[272,2048]{1,0:T(8,128)(2,1)S(1)} collective-permute-done((bf16[272,2048]{1,0:T(8,128)(2,1)}, bf16[272,2048]{1,0:T(8,128)(2,1)S(1)}, u32[]{:S(2)}, u32[]{:S(2)}) %collective-permute-start.11) | collective-permute-done | bytes 1114144 | tf_op jit(solution)/shard_map/ppermute | solution.py:730
  550.8 24.3 %collective-permute-done.14.refs_2_ = bf16[272,2048]{1,0:T(8,128)(2,1)S(1)} collective-permute-done((bf16[272,2048]{1,0:T(8,128)(2,1)}, bf16[272,2048]{1,0:T(8,128)(2,1)S(1)}, u32[]{:S(2)}, u32[]{:S(2)}) %collective-permute-start.14) | collective-permute-done | bytes 1114144 | tf_op jit(solution)/shard_map/ppermute | solution.py:730
  618.7 9.2 %collective-permute-done.34.refs_1_ = bf16[512,512]{1,0:T(8,128)(2,1)} collective-permute-done((bf16[512,512]{1,0:T(8,128)(2,1)}, bf16[512,512]{1,0:T(8,128)(2,1)}, u32[]{:S(2)}, u32[]{:S(2)}) %collective-permute-start.34) | collective-permute-done | bytes 524320 | tf_op jit(solution)/shard_map/ppermute | solution.py:730
  629.5 19.1 %exgrads.1 = (f32[2048,768]{1,0:T(8,128)}, f32[2048,768]{1,0:T(8,128)}, f32[768,2048]{1,0:T(8,128)}) custom-call(bf16[272,2048]{1,0:T(8,128)(2,1)} %convolution_convert_fusion.7.x_ref.refs_0_, bf16[272,2048]{1,0:T(8,128)(2,1)} %copy-done.6, bf16[272,2048]{1,0:T(8,128)(2,1)} %copy-done.7, bf16[272,2048]{1,0:T(8,128)(2,1)} %collective-permute-done.15.x_ref.refs_3_, ...), custom_call_target="tpu_custom_call" | custom-call | tf_op jit(solution)/shard_map/exgrads/pallas_call | solution.py:269
  648.6 25.6 %reduce-scatter.6.cloned.1.call-done = bf16[128,1024]{1,0:T(8,128)(2,1)} async-done(((bf16[1024,1024]{1,0:T(8,128)(2,1)}), bf16[128,1024]{1,0:T(8,128)(2,1)}) %reduce-scatter.6.cloned.1.call-update) | async-done | bytes 262160 | tf_op jit(solution)/shard_map/reduce_scatter | solution.py:740
  (289 shorter events, 257.7 us)
Async XLA Ops:
  7.2 64.2 %all-gather.6.cloned.1.call-start = ((), (), s32[]{:S(2)}) async-start(), calls=%async_computation.5 | async-start | bytes 5898240 | tf_op jit(solution)/shard_map/all_gather | solution.py:737
  10.7 108.4 %all-gather.8.cloned.1.call-start = ((), (), s32[]{:S(2)}) async-start(), calls=%async_computation.6 | async-start | bytes 4718592 | tf_op jit(solution)/shard_map/all_gather | solution.py:737
  12.7 159.3 %all-gather.12.cloned.1.call-start = ((), (), s32[]{:S(2)}) async-start(), calls=%async_computation.8 | async-start | bytes 5013504 | tf_op jit(solution)/shard_map/all_gather | solution.py:737
  13.9 202.7 %all-gather.10.cloned.1.call-start = ((), (), s32[]{:S(2)}) async-start(), calls=%async_computation.7 | async-start | bytes 4718592 | tf_op jit(solution)/shard_map/all_gather | solution.py:737
  161.2 269.1 %reduce-scatter.10.cloned.1.call-start = ((), (), s32[]{:S(2)}) async-start(), calls=%async_computation.11 | async-start | bytes 5013504 | tf_op jit(solution)/shard_map/reduce_scatter | solution.py:740
  177.1 51.6 %collective-permute-start.10 = (bf16[272,2176]{1,0:T(8,128)(2,1)}, bf16[272,2176]{1,0:T(8,128)(2,1)}, u32[]{:S(2)}, u32[]{:S(2)}) collective-permute-start(bf16[272,2176]{1,0:T(8,128)(2,1)} %convolution_convert_fusion.2), channel_id=1, source_target_pairs={{0,8},{8,0},{16,24},{24,16},{1,9},{9,1},{17,25},{25,17},{2,10},{10... | collective-permute-start | bytes 3551240 | tf_op jit(solution)/shard_map/ppermute | solution.py:730
  181.1 89.5 %collective-permute-start.13 = (bf16[272,2176]{1,0:T(8,128)(2,1)}, bf16[272,2176]{1,0:T(8,128)(2,1)}, u32[]{:S(2)}, u32[]{:S(2)}) collective-permute-start(bf16[272,2176]{1,0:T(8,128)(2,1)} %convolution_convert_fusion.1), channel_id=1, source_target_pairs={{0,16},{8,24},{16,0},{24,8},{1,17},{9,25},{17,1},{25,9},{2,18},{10... | collective-permute-start | bytes 3551240 | tf_op jit(solution)/shard_map/ppermute | solution.py:730
  184.5 110.0 %collective-permute-start.16 = (bf16[272,2176]{1,0:T(8,128)(2,1)}, bf16[272,2176]{1,0:T(8,128)(2,1)}, u32[]{:S(2)}, u32[]{:S(2)}) collective-permute-start(bf16[272,2176]{1,0:T(8,128)(2,1)} %convolution_convert_fusion), channel_id=1, source_target_pairs={{0,24},{8,16},{16,8},{24,0},{1,25},{9,17},{17,9},{25,1},{2,26},{10... | collective-permute-start | bytes 3551240 | tf_op jit(solution)/shard_map/ppermute | solution.py:730
  224.8 55.4 %collective-permute-start.12 = (bf16[272,2048]{1,0:T(8,128)(2,1)}, bf16[272,2048]{1,0:T(8,128)(2,1)S(1)}, u32[]{:S(2)}, u32[]{:S(2)}) collective-permute-start(bf16[272,2048]{1,0:T(8,128)(2,1)} %convolution_convert_fusion.5), channel_id=1, source_target_pairs={{0,16},{8,24},{16,0},{24,8},{1,17},{9,25},{17,1},{25,9},{2,18},{10... | collective-permute-start | bytes 3342344 | tf_op jit(solution)/shard_map/ppermute | solution.py:730
  228.7 65.8 %collective-permute-start.15 = (bf16[272,2048]{1,0:T(8,128)(2,1)}, bf16[272,2048]{1,0:T(8,128)(2,1)}, u32[]{:S(2)}, u32[]{:S(2)}) collective-permute-start(bf16[272,2048]{1,0:T(8,128)(2,1)} %convolution_convert_fusion.4), channel_id=1, source_target_pairs={{0,24},{8,16},{16,8},{24,0},{1,25},{9,17},{17,9},{25,1},{2,26},{10... | collective-permute-start | bytes 3342344 | tf_op jit(solution)/shard_map/ppermute | solution.py:730
  269.1 59.1 %collective-permute-start.18 = (bf16[272,2176]{1,0:T(8,128)(2,1)}, bf16[272,2176]{1,0:T(8,128)(2,1)S(1)}, u32[]{:S(2)}, u32[]{:S(2)}) collective-permute-start(bf16[272,2176]{1,0:T(8,128)(2,1)} %get-tuple-element.74), channel_id=1, source_target_pairs={{0,8},{8,0},{16,24},{24,16},{1,9},{9,1},{17,25},{25,17},{2,10},{10... | collective-permute-start | bytes 3551240 | tf_op jit(solution)/shard_map/ppermute | solution.py:730
  293.7 48.9 %collective-permute-start.19 = (bf16[272,2176]{1,0:T(8,128)(2,1)}, bf16[272,2176]{1,0:T(8,128)(2,1)S(1)}, u32[]{:S(2)}, u32[]{:S(2)}) collective-permute-start(bf16[272,2176]{1,0:T(8,128)(2,1)} %get-tuple-element.75), channel_id=1, source_target_pairs={{0,16},{8,24},{16,0},{24,8},{1,17},{9,25},{17,1},{25,9},{2,18},{10... | collective-permute-start | bytes 3551240 | tf_op jit(solution)/shard_map/ppermute | solution.py:730
  354.0 128.0 %all-gather.14.cloned.1.call-start = ((), (), s32[]{:S(2)}) async-start(), calls=%async_computation.12 | async-start | bytes 4718592 | tf_op jit(solution)/shard_map/all_gather | solution.py:737
  403.8 190.2 %reduce-scatter.14.cloned.1.call-start = ((), (), s32[]{:S(2)}) async-start(), calls=%async_computation.14 | async-start | bytes 4718592 | tf_op jit(solution)/shard_map/reduce_scatter | solution.py:740
  473.3 126.5 %reduce-scatter.12.cloned.1.call-start = ((), (), s32[]{:S(2)}) async-start(), calls=%async_computation.13 | async-start | bytes 6488064 | tf_op jit(solution)/shard_map/reduce_scatter | solution.py:740
  523.0 125.5 %reduce-scatter.8.cloned.1.call-start = ((), (), s32[]{:S(2)}) async-start(), calls=%async_computation.10 | async-start | bytes 2359296 | tf_op jit(solution)/shard_map/reduce_scatter | solution.py:740
  524.6 50.5 %collective-permute-start.14 = (bf16[272,2048]{1,0:T(8,128)(2,1)}, bf16[272,2048]{1,0:T(8,128)(2,1)S(1)}, u32[]{:S(2)}, u32[]{:S(2)}) collective-permute-start(bf16[272,2048]{1,0:T(8,128)(2,1)} %get-tuple-element.70), channel_id=1, source_target_pairs={{0,16},{8,24},{16,0},{24,8},{1,17},{9,25},{17,1},{25,9},{2,18},{10... | collective-permute-start | bytes 3342344 | tf_op jit(solution)/shard_map/ppermute | solution.py:730
  526.1 49.1 %collective-permute-start.17 = (bf16[272,2048]{1,0:T(8,128)(2,1)}, bf16[272,2048]{1,0:T(8,128)(2,1)S(1)}, u32[]{:S(2)}, u32[]{:S(2)}) collective-permute-start(bf16[272,2048]{1,0:T(8,128)(2,1)} %get-tuple-element.72), channel_id=1, source_target_pairs={{0,24},{8,16},{16,8},{24,0},{1,25},{9,17},{17,9},{25,1},{2,26},{10... | collective-permute-start | bytes 3342344 | tf_op jit(solution)/shard_map/ppermute | solution.py:730
  582.7 91.5 %reduce-scatter.6.cloned.1.call-start = ((), (), s32[]{:S(2)}) async-start(), calls=%async_computation.9 | async-start | bytes 2359296 | tf_op jit(solution)/shard_map/reduce_scatter | solution.py:740
  599.8 83.9 %collective-permute-start.31 = (bf16[256,1408]{1,0:T(8,128)(2,1)}, bf16[256,1408]{1,0:T(8,128)(2,1)S(1)}, u32[]{:S(2)}, u32[]{:S(2)}) collective-permute-start(bf16[256,1408]{1,0:T(8,128)(2,1)} %reduce-scatter.12.cloned.1.call-done.refs_0_), channel_id=1, source_target_pairs={{0,8},{8,0},{16,24},{24,16},{1,9},{9,1},{17,25},{25,17},{2,10},{10... | collective-permute-start | bytes 2162696 | tf_op jit(solution)/shard_map/ppermute | solution.py:730
  605.3 78.4 %collective-permute-start.32 = (bf16[256,1408]{1,0:T(8,128)(2,1)}, bf16[256,1408]{1,0:T(8,128)(2,1)S(1)}, u32[]{:S(2)}, u32[]{:S(2)}) collective-permute-start(bf16[256,1408]{1,0:T(8,128)(2,1)} %reduce-scatter.12.cloned.1.call-done.refs_0_), channel_id=1, source_target_pairs={{0,16},{8,24},{16,0},{24,8},{1,17},{9,25},{17,1},{25,9},{2,18},{10... | collective-permute-start | bytes 2162696 | tf_op jit(solution)/shard_map/ppermute | solution.py:730
  615.3 68.5 %collective-permute-start.33 = (bf16[256,1408]{1,0:T(8,128)(2,1)}, bf16[256,1408]{1,0:T(8,128)(2,1)S(1)}, u32[]{:S(2)}, u32[]{:S(2)}) collective-permute-start(bf16[256,1408]{1,0:T(8,128)(2,1)} %reduce-scatter.12.cloned.1.call-done.refs_0_), channel_id=1, source_target_pairs={{0,24},{8,16},{16,8},{24,0},{1,25},{9,17},{17,9},{25,1},{2,26},{10... | collective-permute-start | bytes 2162696 | tf_op jit(solution)/shard_map/ppermute | solution.py:730
  618.7 61.2 %collective-permute-start.35 = (bf16[512,512]{1,0:T(8,128)(2,1)}, bf16[512,512]{1,0:T(8,128)(2,1)}, u32[]{:S(2)}, u32[]{:S(2)}) collective-permute-start(bf16[512,512]{1,0:T(8,128)(2,1)} %reduce-scatter.14.cloned.1.call-done.refs_0_), channel_id=1, source_target_pairs={{0,16},{8,24},{16,0},{24,8},{1,17},{9,25},{17,1},{25,9},{2,18},{10... | collective-permute-start | bytes 1572872 | tf_op jit(solution)/shard_map/ppermute | solution.py:730
  628.0 52.0 %collective-permute-start.36 = (bf16[512,512]{1,0:T(8,128)(2,1)}, bf16[512,512]{1,0:T(8,128)(2,1)}, u32[]{:S(2)}, u32[]{:S(2)}) collective-permute-start(bf16[512,512]{1,0:T(8,128)(2,1)} %reduce-scatter.14.cloned.1.call-done.refs_0_), channel_id=1, source_target_pairs={{0,24},{8,16},{16,8},{24,0},{1,25},{9,17},{17,9},{25,1},{2,26},{10... | collective-permute-start | bytes 1572872 | tf_op jit(solution)/shard_map/ppermute | solution.py:730
  (77 other events, 1042.4 us)
Sparse Core Ops, SparseCore 0:
  10.8 60.5 all-gather.5
  73.6 45.4 all-gather.7
  121.3 47.8 all-gather.11
  170.6 45.8 all-gather.9
  354.2 76.1 reduce-scatter.9
  431.8 50.1 all-gather.13
  484.9 48.7 reduce-scatter.13
  536.5 63.2 reduce-scatter.11
  602.7 34.7 reduce-scatter.7
  639.6 34.5 reduce-scatter.5

commit v4 on v3

--- a/solution.py
+++ b/solution.py
@@ -175,7 +175,7 @@
             pltpu.VMEM((n, n), F32),
         ],
         compiler_params=params(),
-        name="unattend",
+        name="detend",
     )(qkv, qkv, qkv, d_mix, mix, totals, gains, cosine, sine, pos_col, pos_row)
 
 
@@ -231,7 +231,7 @@
             jax.ShapeDtypeStruct((r, f), BF16),
         ],
         compiler_params=params(),
-        name="expert_piece",
+        name="piece",
     )(me, x, cot, router, wg, wu, wd)
 
 
@@ -398,6 +398,31 @@
     )(c, *parts)
 
 
+def gather_rows(picks, pieces, block=768):
+    n, k = len(picks), len(pieces)
+    rows, m = picks[0].shape
+    t, d = pieces[0].shape
+
+    def kernel(*refs):
+        pick, piece, out, v_s = refs[:n], refs[n : n + k], refs[n + k : -1], refs[-1]
+        for j in range(k):
+            v_s[j * t : (j + 1) * t, :] = piece[j][...]
+        for i in range(n):
+            out[i][...] = dot(pick[i][...], v_s[...]).astype(BF16)
+
+    return pl.pallas_call(
+        kernel,
+        grid=(pl.cdiv(d, block),),
+        in_specs=[pl.BlockSpec((rows, m), lambda j: (0, 0))] * n
+        + [pl.BlockSpec((t, block), lambda j: (0, j))] * k,
+        out_specs=[pl.BlockSpec((rows, block), lambda j: (0, j))] * n,
+        out_shape=[jax.ShapeDtypeStruct((rows, d), BF16)] * n,
+        scratch_shapes=[pltpu.VMEM((m, block), BF16)],
+        compiler_params=params(),
+        name="grab",
+    )(*picks, *pieces)
+
+
 def pack(w_query, w_key, w_value, at, qc):
     ws = w_query.shape[0]
     hs = HEAD_SIZE
@@ -426,13 +451,15 @@
     )(at, w_query, w_key, w_value)
 
 
-def plan(targets, rows, block=LANES):
+def plan(targets, rows, placed, block=LANES):
     n, m = targets.shape
 
     def kernel(row_ref, col_ref, *outs):
         ids = lax.broadcasted_iota(jnp.int32, (rows, block), 0)
         for d in range(n):
             outs[d][...] = jnp.where(row_ref[d : d + 1, :] == ids, 1.0, 0.0).astype(BF16)
+        if not placed:
+            return
         ids = lax.broadcasted_iota(jnp.int32, (block, n * rows), 1)
         hot = col_ref[:, 0:1] == ids
         for d in range(1, n):
@@ -447,11 +474,10 @@
             pl.BlockSpec((block, n), lambda j: (j, 0)),
         ],
         out_specs=[pl.BlockSpec((rows, block), lambda j: (0, j))] * n
-        + [pl.BlockSpec((block, n * rows), lambda j: (j, 0))],
+        + [pl.BlockSpec((block, n * rows), lambda j: (j, 0))] * placed,
         out_shape=[jax.ShapeDtypeStruct((rows, m), BF16)] * n
-        + [jax.ShapeDtypeStruct((m, n * rows), BF16)],
-        compiler_params=params(),
-        name="plan",
+        + [jax.ShapeDtypeStruct((m, n * rows), BF16)] * placed,
+        compiler_params=params(),
     )(targets, targets.T)
 
 
@@ -511,7 +537,7 @@
         ),
         out_shape=jax.ShapeDtypeStruct((t, w), BF16),
         compiler_params=params(),
-        name="out_proj",
+        name="oproj",
     )(c, *parts, w_cols)
 
 
@@ -596,7 +622,7 @@
         out_specs=[vm] * 2,
         out_shape=[jax.ShapeDtypeStruct(x.shape, F32), jax.ShapeDtypeStruct(x.shape, BF16)],
         compiler_params=params(),
-        name="residual",
+        name="resid",
     )(c, x, gain, *parts)
 
 
@@ -650,7 +676,7 @@
             jax.ShapeDtypeStruct((1, d), F32),
         ],
         compiler_params=params(),
-        name="turn_back",
+        name="tback",
     )(back_sum, r1, h2, cot, hits, router, gain)
 
 
@@ -787,7 +813,13 @@
     extra = round_up(E, LANES)
     hits_wide = jnp.pad(hits, ((0, 0), (0, extra - E)))
     cot_own = jnp.concatenate([out_cot[0], hits_wide], axis=1)
-    cot_column = gather_shard(cot_own)
+
+    def hop_shard(v, d):
+        return lax.ppermute(v, "shard", [(i, i ^ d) for i in range(S)])
+
+    far = [cot_own] + [hop_shard(cot_own, d) for d in range(2, S, 2)]
+    near = [hop_shard(v, 1) for v in far]
+    cot_pieces = [v for both in zip(far, near) for v in both]
     router_wide = jnp.pad(router, ((0, 0), (0, extra - E)))
 
     pairs_here = jnp.stack([block_pairs[c ^ d] for d in range(C)])
@@ -808,7 +840,9 @@
     target = jnp.where(
         hit > 0.5, jnp.arange(S, dtype=jnp.int32)[None, :, None] * cap + slot, -E * cap
     )
-    *picks, place = plan(target.reshape(C, M), rows)
+    *picks, place = plan(target.reshape(C, M), rows, 1)
+    near_target = [lax.dynamic_index_in_dim(target, s ^ j, 1, False) for j in range(S)]
+    near_picks = plan(jnp.concatenate(near_target, axis=1), rows, 0)
 
     h1 = norm_rows(x_parts, gain_attn.reshape(1, D))
     qkv = dot(h1, w_qkv, 1, 0)
@@ -821,14 +855,14 @@
 
     h2_column = gather_shard(h2)
 
-    def dispatch(v):
-        sent = [None] * C
-        for d in [C - 1] + list(range(1, C - 1)) + [0]:
-            sent[d] = dot(picks[d], v, 1, 0).astype(BF16)
-        return exchange_ctx(sent)
-
-    cot_in = dispatch(cot_column)
-    expert_in = dispatch(h2_column)
+    cot_rows = [None] * C
+    for d in list(range(C - 1, -1, -1)):
+        cot_rows[d] = gather_rows([near_picks[d]], cot_pieces)[0]
+    cot_in = exchange_ctx(cot_rows)
+    h2_rows = [None] * C
+    for d in [C - 1] + list(range(1, C - 1)) + [0]:
+        h2_rows[d] = dot(picks[d], h2_column, 1, 0).astype(BF16)
+    expert_in = exchange_ctx(h2_rows)
 
     wg, wu, wd = expert_gate[0], expert_up[0], expert_down[0]
     me_vec = me.astype(jnp.int32).reshape(1)

time: 712 us -> 810 us (1.14)
  waiting for transfers between devices: 338 us -> 388 us
  starting transfers between devices: 53.7 us -> 82.8 us
  Pallas kernels: 186 us -> 211 us
  matrix products: 46.4 us -> 34.6 us
    ppermute x0 -> x7, waiting for transfers between devices: none -> 57.9 us  [hop_shard(): return lax.ppermute(v, 'shard', [(i, i ^ d) for i in range(S)])]
    ppermute x33, waiting for transfers between devices: 156 us -> 192 us  [exchange_ctx(): out.append(lax.ppermute(parts[d], 'ctx', [(i, i ^ d) for i in range(C)]))]
    all_gather x5 -> x4, waiting for transfers between devices: 84.4 us -> 52.9 us  [gather_shard(): return lax.all_gather(v, 'shard', axis=0, tiled=True)]
    pallas_call x0 -> x4, Pallas kernels: none -> 21.1 us  [gather_rows(): pl.pallas_call(kernel, grid=(pl.cdiv(d, block),), in_specs=[pl.BlockSpec(...]
    ppermute x4, starting transfers between devices: 7.17 us -> 23.1 us  [layer(): lax.ppermute(w_out[i * po:(i + 1) * po], ('ctx', 'shard'), pairs)]
    dot_general x12 -> x8, matrix products: 46.4 us -> 34.6 us  [dot(): lax.dot_general(a, b, (((ca,), (cb,)), ((), ())), preferred_element_type=...]
    reduce_scatter x5, waiting for transfers between devices: 57.1 us -> 45.9 us  [sum_shard(): return lax.psum_scatter(v, 'shard', scatter_dimension=0, tiled=True)]
    unnamed x115 -> x136, local copies, waits for them, and re-layouts: 16.6 us -> 17.9 us
  transfers between devices with their start and end apart: 47 -> 53, of which waited for: 23 -> 25; matrix products, arithmetic and copies ran while one was open for 10% -> 8% of each run, Pallas kernels for 24% -> 23%
where the time goes in v4:
time: 810 us; the launch traced here: 800 us
  waiting for transfers between devices  388 us (48%)
  Pallas kernels  211 us (26%)
  starting transfers between devices  82.8 us (10%)
  local copies, waits for them, and re-layouts  37 us (5%)
  matrix products  34.6 us (4%)
  blocking collectives  16.3 us (2%)
  other arithmetic  16 us (2%)
  between operations  15 us (2%)
    ppermute x33, waiting for transfers between devices, exchange_ctx(): out.append(lax.ppermute(parts[d], 'ctx', [(i, i ^ d) for i in range(C)]))  192 us
    ppermute x7, waiting for transfers between devices, hop_shard(): return lax.ppermute(v, 'shard', [(i, i ^ d) for i in range(S)])  57.9 us
    ppermute x33, starting transfers between devices, exchange_ctx(): out.append(lax.ppermute(parts[d], 'ctx', [(i, i ^ d) for i in range(C)]))  53.4 us
    all_gather x4, waiting for transfers between devices, gather_shard(): return lax.all_gather(v, 'shard', axis=0, tiled=True)  52.9 us
    pallas_call x4, Pallas kernels, expert_piece(): pl.pallas_call(kernel, in_specs=[pl.BlockSpec(memory_space=pltpu.SMEM)] +...  49.8 us
    reduce_scatter x5, waiting for transfers between devices, sum_shard(): return lax.psum_scatter(v, 'shard', scatter_dimension=0, tiled=True)  45.9 us
    ppermute x4, waiting for transfers between devices, layer(): lax.ppermute(w_out[i * po:(i + 1) * po], ('ctx', 'shard'), pairs)  38.7 us
    dot_general x8, matrix products, dot(): lax.dot_general(a, b, (((ca,), (cb,)), ((), ())), preferred_element_type=...  34.6 us
  transfers between devices with their start and end apart: 53, of which 25 were waited for; matrix products, arithmetic and copies ran while one was open for 8% of the time, Pallas kernels for 23%

profile of v4, /device:TPU:0, one launch (start us, length us, event | category | flops | bytes accessed | tf_op | source)
XLA Modules:
  0.0 800.5 jit_solution(3866447027758431753)
XLA Ops:
  18.4 16.3 %all_gather.15 = bf16[1024,128]{1,0:T(8,128)(2,1)S(1)} all-gather(bf16[128,128]{1,0:T(8,128)(2,1)S(1)} %concatenate.34), channel_id=1, replica_groups=mesh['ctx'=4,'shard'=8] {'shard'}, dimensions={0}, use_global_device_ids=true | all-gather | bytes 294912 | tf_op jit(solution)/shard_map/all_gather | solution.py:763
  48.0 23.0 %all-gather.5.cloned.1.call-done = bf16[2048,1280]{1,0:T(8,128)(2,1)} async-done(((bf16[256,1280]{1,0:T(8,128)(2,1)}), bf16[2048,1280]{1,0:T(8,128)(2,1)}) %all-gather.5.cloned.1.call-update) | async-done | bytes 5242896 | tf_op jit(solution)/shard_map/all_gather | solution.py:763
  78.5 12.0 %attend.1 = (bf16[512,1024]{1,0:T(8,128)(2,1)}, f32[512,128]{1,0:T(8,128)}) custom-call(f32[512,1280]{1,0:T(8,128)} %fusion.36.q_ref.k_ref.v_ref, f32[512,1280]{1,0:T(8,128)} %fusion.36.q_ref.k_ref.v_ref, f32[512,1280]{1,0:T(8,128)} %fusion.36.q_ref.k_ref.v_ref, f32[8,128]{1,0:T(8,128)} %maximum_maximum_fusion.gain_ref, ...), custom_call_target="tpu_custom_call" | custom-call | tf_op jit(solution)/shard_map/attend/pallas_call | solution.py:79
  93.9 25.2 %all-gather.7.cloned.1.call-done.refs_4_ = bf16[4096,512]{1,0:T(8,128)(2,1)} async-done(((bf16[512,512]{1,0:T(8,128)(2,1)}), bf16[4096,512]{1,0:T(8,128)(2,1)}) %all-gather.7.cloned.1.call-update) | async-done | bytes 4194320 | tf_op jit(solution)/shard_map/all_gather | solution.py:763
  119.1 20.5 %collective-permute-done.4.refs_2_ = bf16[512,1024]{1,0:T(8,128)(2,1)S(1)} collective-permute-done((bf16[512,1024]{1,0:T(8,128)(2,1)}, bf16[512,1024]{1,0:T(8,128)(2,1)S(1)}, u32[]{:S(2)}, u32[]{:S(2)}) %collective-permute-start.4) | collective-permute-done | bytes 1048608 | tf_op jit(solution)/shard_map/ppermute | solution.py:756
  171.6 36.5 %collective-permute-done.10.refs_3_ = bf16[128,2176]{1,0:T(8,128)(2,1)S(1)} collective-permute-done((bf16[128,2176]{1,0:T(8,128)(2,1)S(1)}, bf16[128,2176]{1,0:T(8,128)(2,1)S(1)}, u32[]{:S(2)}, u32[]{:S(2)}) %collective-permute-start.10) | collective-permute-done | bytes 557088 | tf_op jit(solution)/shard_map/ppermute | solution.py:818
  208.5 21.4 %collective-permute-done.14.refs_7_ = bf16[128,2176]{1,0:T(8,128)(2,1)S(1)} collective-permute-done((bf16[128,2176]{1,0:T(8,128)(2,1)S(1)}, bf16[128,2176]{1,0:T(8,128)(2,1)S(1)}, u32[]{:S(2)}, u32[]{:S(2)}) %collective-permute-start.14) | collective-permute-done | bytes 557088 | tf_op jit(solution)/shard_map/ppermute | solution.py:818
  281.8 46.4 %collective-permute-done.16.x_ref.refs_1_ = bf16[272,2048]{1,0:T(8,128)(2,1)S(1)} collective-permute-done((bf16[272,2048]{1,0:T(8,128)(2,1)}, bf16[272,2048]{1,0:T(8,128)(2,1)S(1)}, u32[]{:S(2)}, u32[]{:S(2)}) %collective-permute-start.16) | collective-permute-done | bytes 1114144 | tf_op jit(solution)/shard_map/ppermute | solution.py:756
  329.3 12.4 %piece.5 = (bf16[272,2048]{1,0:T(8,128)(2,1)}, bf16[272,2176]{1,0:T(8,128)(2,1)}, bf16[272,768]{1,0:T(8,128)(2,1)}, bf16[272,2048]{1,0:T(8,128)(2,1)}, bf16[272,...) custom-call(s32[1]{0:T(128)} %bitcast.10.me_ref, bf16[272,2048]{1,0:T(8,128)(2,1)} %copy-done.14, ...), custom_call_target="tpu_custom_call" | custom-call | tf_op jit(solution)/shard_map/piece/pallas_call | solution.py:221
  343.4 14.9 %collective-permute-done.19.x_ref.refs_2_ = bf16[272,2048]{1,0:T(8,128)(2,1)S(1)} collective-permute-done((bf16[272,2048]{1,0:T(8,128)(2,1)}, bf16[272,2048]{1,0:T(8,128)(2,1)S(1)}, u32[]{:S(2)}, u32[]{:S(2)}) %collective-permute-start.19) | collective-permute-done | bytes 1114144 | tf_op jit(solution)/shard_map/ppermute | solution.py:756
  359.3 12.6 %piece.6 = (bf16[272,2048]{1,0:T(8,128)(2,1)}, bf16[272,2176]{1,0:T(8,128)(2,1)}, bf16[272,768]{1,0:T(8,128)(2,1)}, bf16[272,2048]{1,0:T(8,128)(2,1)}, bf16[272,...) custom-call(s32[1]{0:T(128)} %bitcast.10.me_ref, bf16[272,2048]{1,0:T(8,128)(2,1)} %copy-done.15, ...), custom_call_target="tpu_custom_call" | custom-call | tf_op jit(solution)/shard_map/piece/pallas_call | solution.py:221
  372.2 12.4 %piece.7 = (bf16[272,2048]{1,0:T(8,128)(2,1)}, bf16[272,2176]{1,0:T(8,128)(2,1)}, bf16[272,768]{1,0:T(8,128)(2,1)}, bf16[272,2048]{1,0:T(8,128)(2,1)}, bf16[272,...) custom-call(s32[1]{0:T(128)} %bitcast.10.me_ref, bf16[272,2048]{1,0:T(8,128)(2,1)} %collective-permute-done.22.x_ref.refs_3_, ...), custom_call_target="tpu_custom_call" | custom-call | tf_op jit(solution)/shard_map/piece/pallas_call | solution.py:221
  396.1 12.4 %piece.4 = (bf16[272,2048]{1,0:T(8,128)(2,1)}, bf16[272,2176]{1,0:T(8,128)(2,1)}, bf16[272,768]{1,0:T(8,128)(2,1)}, bf16[272,2048]{1,0:T(8,128)(2,1)}, bf16[272,...) custom-call(s32[1]{0:T(128)} %bitcast.10.me_ref, bf16[272,2048]{1,0:T(8,128)(2,1)} %convolution_convert_fusion.3.x_ref.refs_0_, ...), custom_call_target="tpu_custom_call" | custom-call | tf_op jit(solution)/shard_map/piece/pallas_call | solution.py:221
  408.5 16.3 %collective-permute-done.26.refs_2_ = bf16[272,2176]{1,0:T(8,128)(2,1)S(1)} collective-permute-done((bf16[272,2176]{1,0:T(8,128)(2,1)}, bf16[272,2176]{1,0:T(8,128)(2,1)S(1)}, u32[]{:S(2)}, u32[]{:S(2)}) %collective-permute-start.26) | collective-permute-done | bytes 1183776 | tf_op jit(solution)/shard_map/ppermute | solution.py:756
  438.1 17.1 %collective-permute-start.34 = (bf16[128,2048]{1,0:T(8,128)(2,1)S(1)}, bf16[128,2048]{1,0:T(8,128)(2,1)S(1)}, u32[]{:S(2)}, u32[]{:S(2)}) collective-permute-start(bf16[128,2048]{1,0:T(8,128)(2,1)S(1)} %get-tuple-element.188), channel_id=1, source_target_pairs={{0,3},{1,7},{10,11},{11,15},{20,19},{21,23},{30,27},{31,31}} | collective-permute-start | bytes 1572872 | tf_op jit(solution)/shard_map/ppermute | solution.py:807
  461.2 16.2 %collective-permute-done.34 = bf16[128,2048]{1,0:T(8,128)(2,1)S(1)} collective-permute-done((bf16[128,2048]{1,0:T(8,128)(2,1)S(1)}, bf16[128,2048]{1,0:T(8,128)(2,1)S(1)}, u32[]{:S(2)}, u32[]{:S(2)}) %collective-permute-start.34) | collective-permute-done | bytes 524320 | tf_op jit(solution)/shard_map/ppermute | solution.py:807
  477.4 22.5 %collective-permute-done.33 = bf16[128,2048]{1,0:T(8,128)(2,1)S(1)} collective-permute-done((bf16[128,2048]{1,0:T(8,128)(2,1)S(1)}, bf16[128,2048]{1,0:T(8,128)(2,1)S(1)}, u32[]{:S(2)}, u32[]{:S(2)}) %collective-permute-start.33) | collective-permute-done | bytes 524320 | tf_op jit(solution)/shard_map/ppermute | solution.py:807
  500.9 20.8 %reduce-scatter.10.cloned.1.call-done.back_ref = bf16[128,2176]{1,0:T(8,128)(2,1)} async-done(((bf16[1024,2176]{1,0:T(8,128)(2,1)}), bf16[128,2176]{1,0:T(8,128)(2,1)}) %reduce-scatter.10.cloned.1.call-update) | async-done | bytes 557072 | tf_op jit(solution)/shard_map/reduce_scatter | solution.py:766
  526.3 14.8 %collective-permute-start.30 = (bf16[128,2048]{1,0:T(8,128)(2,1)}, bf16[128,2048]{1,0:T(8,128)(2,1)S(1)}, u32[]{:S(2)}, u32[]{:S(2)}) collective-permute-start(bf16[128,2048]{1,0:T(8,128)(2,1)} %get-tuple-element.86.refs_0_), channel_id=1, source_target_pairs={{0,24},{8,16},{16,8},{24,0},{1,25},{9,17},{17,9},{25,1},{2,26},{10... | collective-permute-start | bytes 1572872 | tf_op jit(solution)/shard_map/ppermute | solution.py:756
  586.2 16.7 %detend.1 = (bf16[512,1024]{1,0:T(8,128)(2,1)}, bf16[512,256]{1,0:T(8,128)(2,1)}, f32[8,128]{1,0:T(8,128)}) custom-call(f32[512,1280]{1,0:T(8,128)} %fusion.36.q_ref.k_ref.v_ref, f32[512,1280]{1,0:T(8,128)} %fusion.36.q_ref.k_ref.v_ref, f32[512,1280]{1,0:T(8,128)} %fusion.36.q_ref.k_ref.v_ref, bf16[512,1024]{1,0:T(8,128)(2,1)} %fusion.11.dm_ref, ...), custom_call_target="tpu_custom_call" | custom-call | tf_op jit(solution)/shard_map/detend/pallas_call | solution.py:148
  626.1 24.2 %collective-permute-done.18.refs_1_ = bf16[272,2048]{1,0:T(8,128)(2,1)S(1)} collective-permute-done((bf16[272,2048]{1,0:T(8,128)(2,1)}, bf16[272,2048]{1,0:T(8,128)(2,1)S(1)}, u32[]{:S(2)}, u32[]{:S(2)}) %collective-permute-start.18) | collective-permute-done | bytes 1114144 | tf_op jit(solution)/shard_map/ppermute | solution.py:756
  650.3 24.4 %collective-permute-done.21.refs_2_ = bf16[272,2048]{1,0:T(8,128)(2,1)S(1)} collective-permute-done((bf16[272,2048]{1,0:T(8,128)(2,1)}, bf16[272,2048]{1,0:T(8,128)(2,1)S(1)}, u32[]{:S(2)}, u32[]{:S(2)}) %collective-permute-start.21) | collective-permute-done | bytes 1114144 | tf_op jit(solution)/shard_map/ppermute | solution.py:756
  730.7 19.0 %exgrads.1 = (f32[2048,768]{1,0:T(8,128)}, f32[2048,768]{1,0:T(8,128)}, f32[768,2048]{1,0:T(8,128)}) custom-call(bf16[272,2048]{1,0:T(8,128)(2,1)} %convolution_convert_fusion.3.x_ref.refs_0_, bf16[272,2048]{1,0:T(8,128)(2,1)} %copy-done.14, bf16[272,2048]{1,0:T(8,128)(2,1)} %copy-done.15, bf16[272,2048]{1,0:T(8,128)(2,1)} %collective-permute-done.22.x_ref.refs_3_, ...), custom_call_target="tpu_custom_call" | custom-call | tf_op jit(solution)/shard_map/exgrads/pallas_call | solution.py:269
  749.7 22.9 %reduce-scatter.6.cloned.1.call-done = bf16[128,1024]{1,0:T(8,128)(2,1)} async-done(((bf16[1024,1024]{1,0:T(8,128)(2,1)}), bf16[128,1024]{1,0:T(8,128)(2,1)}) %reduce-scatter.6.cloned.1.call-update) | async-done | bytes 262160 | tf_op jit(solution)/shard_map/reduce_scatter | solution.py:766
  (326 shorter events, 304.7 us)
Async XLA Ops:
  7.2 63.8 %all-gather.5.cloned.1.call-start = ((), (), s32[]{:S(2)}) async-start(), calls=%async_computation.5 | async-start | bytes 5898240 | tf_op jit(solution)/shard_map/all_gather | solution.py:763
  10.7 108.4 %all-gather.7.cloned.1.call-start = ((), (), s32[]{:S(2)}) async-start(), calls=%async_computation.6 | async-start | bytes 4718592 | tf_op jit(solution)/shard_map/all_gather | solution.py:763
  12.6 251.1 %all-gather.9.cloned.1.call-start = ((), (), s32[]{:S(2)}) async-start(), calls=%async_computation.7 | async-start | bytes 4718592 | tf_op jit(solution)/shard_map/all_gather | solution.py:763
  160.7 361.0 %reduce-scatter.10.cloned.1.call-start = ((), (), s32[]{:S(2)}) async-start(), calls=%async_computation.10 | async-start | bytes 5013504 | tf_op jit(solution)/shard_map/reduce_scatter | solution.py:766
  161.2 82.4 %collective-permute-start.9 = (bf16[128,2176]{1,0:T(8,128)(2,1)S(1)}, bf16[128,2176]{1,0:T(8,128)(2,1)S(1)}, u32[]{:S(2)}, u32[]{:S(2)}) collective-permute-start(bf16[128,2176]{1,0:T(8,128)(2,1)S(1)} %pad_maximum_fusion.1.refs_1_), channel_id=1, source_target_pairs={{0,1},{1,0},{2,3},{3,2},{4,5},{5,4},{6,7},{7,6},{8,9},{9,8},{10,11... | collective-permute-start | bytes 1671176 | tf_op jit(solution)/shard_map/ppermute | solution.py:818
  163.2 66.8 %collective-permute-start.14 = (bf16[128,2176]{1,0:T(8,128)(2,1)S(1)}, bf16[128,2176]{1,0:T(8,128)(2,1)S(1)}, u32[]{:S(2)}, u32[]{:S(2)}) collective-permute-start(bf16[128,2176]{1,0:T(8,128)(2,1)S(1)} %pad_maximum_fusion.1.refs_1_), channel_id=1, source_target_pairs={{0,6},{1,7},{2,4},{3,5},{4,2},{5,3},{6,0},{7,1},{8,14},{9,15},{10,... | collective-permute-start | bytes 1671176 | tf_op jit(solution)/shard_map/ppermute | solution.py:818
  256.7 86.7 %collective-permute-start.20 = (bf16[272,2176]{1,0:T(8,128)(2,1)}, bf16[272,2176]{1,0:T(8,128)(2,1)}, u32[]{:S(2)}, u32[]{:S(2)}) collective-permute-start(bf16[272,2176]{1,0:T(8,128)(2,1)} %grab.6), channel_id=1, source_target_pairs={{0,16},{8,24},{16,0},{24,8},{1,17},{9,25},{17,1},{25,9},{2,18},{10... | collective-permute-start | bytes 3551240 | tf_op jit(solution)/shard_map/ppermute | solution.py:756
  262.3 109.9 %collective-permute-start.23 = (bf16[272,2176]{1,0:T(8,128)(2,1)}, bf16[272,2176]{1,0:T(8,128)(2,1)}, u32[]{:S(2)}, u32[]{:S(2)}) collective-permute-start(bf16[272,2176]{1,0:T(8,128)(2,1)} %grab.7), channel_id=1, source_target_pairs={{0,24},{8,16},{16,8},{24,0},{1,25},{9,17},{17,9},{25,1},{2,26},{10... | collective-permute-start | bytes 3551240 | tf_op jit(solution)/shard_map/ppermute | solution.py:756
  268.4 59.8 %collective-permute-start.16 = (bf16[272,2048]{1,0:T(8,128)(2,1)}, bf16[272,2048]{1,0:T(8,128)(2,1)S(1)}, u32[]{:S(2)}, u32[]{:S(2)}) collective-permute-start(bf16[272,2048]{1,0:T(8,128)(2,1)} %convolution_convert_fusion.2), channel_id=1, source_target_pairs={{0,8},{8,0},{16,24},{24,16},{1,9},{9,1},{17,25},{25,17},{2,10},{10... | collective-permute-start | bytes 3342344 | tf_op jit(solution)/shard_map/ppermute | solution.py:756
  272.5 85.8 %collective-permute-start.19 = (bf16[272,2048]{1,0:T(8,128)(2,1)}, bf16[272,2048]{1,0:T(8,128)(2,1)S(1)}, u32[]{:S(2)}, u32[]{:S(2)}) collective-permute-start(bf16[272,2048]{1,0:T(8,128)(2,1)} %convolution_convert_fusion.1), channel_id=1, source_target_pairs={{0,16},{8,24},{16,0},{24,8},{1,17},{9,25},{17,1},{25,9},{2,18},{10... | collective-permute-start | bytes 3342344 | tf_op jit(solution)/shard_map/ppermute | solution.py:756
  279.1 93.1 %collective-permute-start.22 = (bf16[272,2048]{1,0:T(8,128)(2,1)}, bf16[272,2048]{1,0:T(8,128)(2,1)}, u32[]{:S(2)}, u32[]{:S(2)}) collective-permute-start(bf16[272,2048]{1,0:T(8,128)(2,1)} %convolution_convert_fusion), channel_id=1, source_target_pairs={{0,24},{8,16},{16,8},{24,0},{1,25},{9,17},{17,9},{25,1},{2,26},{10... | collective-permute-start | bytes 3342344 | tf_op jit(solution)/shard_map/ppermute | solution.py:756
  341.7 66.8 %collective-permute-start.25 = (bf16[272,2176]{1,0:T(8,128)(2,1)}, bf16[272,2176]{1,0:T(8,128)(2,1)S(1)}, u32[]{:S(2)}, u32[]{:S(2)}) collective-permute-start(bf16[272,2176]{1,0:T(8,128)(2,1)} %get-tuple-element.82), channel_id=1, source_target_pairs={{0,8},{8,0},{16,24},{24,16},{1,9},{9,1},{17,25},{25,17},{2,10},{10... | collective-permute-start | bytes 3551240 | tf_op jit(solution)/shard_map/ppermute | solution.py:756
  371.9 53.0 %collective-permute-start.26 = (bf16[272,2176]{1,0:T(8,128)(2,1)}, bf16[272,2176]{1,0:T(8,128)(2,1)S(1)}, u32[]{:S(2)}, u32[]{:S(2)}) collective-permute-start(bf16[272,2176]{1,0:T(8,128)(2,1)} %get-tuple-element.83), channel_id=1, source_target_pairs={{0,16},{8,24},{16,0},{24,8},{1,17},{9,25},{17,1},{25,9},{2,18},{10... | collective-permute-start | bytes 3551240 | tf_op jit(solution)/shard_map/ppermute | solution.py:756
  436.2 144.3 %all-gather.11.cloned.1.call-start = ((), (), s32[]{:S(2)}) async-start(), calls=%async_computation.11 | async-start | bytes 4718592 | tf_op jit(solution)/shard_map/all_gather | solution.py:763
  500.8 194.4 %reduce-scatter.14.cloned.1.call-start = ((), (), s32[]{:S(2)}) async-start(), calls=%async_computation.13 | async-start | bytes 4718592 | tf_op jit(solution)/shard_map/reduce_scatter | solution.py:766
  573.0 125.2 %reduce-scatter.12.cloned.1.call-start = ((), (), s32[]{:S(2)}) async-start(), calls=%async_computation.12 | async-start | bytes 6488064 | tf_op jit(solution)/shard_map/reduce_scatter | solution.py:766
  622.5 127.2 %reduce-scatter.8.cloned.1.call-start = ((), (), s32[]{:S(2)}) async-start(), calls=%async_computation.9 | async-start | bytes 2359296 | tf_op jit(solution)/shard_map/reduce_scatter | solution.py:766
  624.1 50.6 %collective-permute-start.21 = (bf16[272,2048]{1,0:T(8,128)(2,1)}, bf16[272,2048]{1,0:T(8,128)(2,1)S(1)}, u32[]{:S(2)}, u32[]{:S(2)}) collective-permute-start(bf16[272,2048]{1,0:T(8,128)(2,1)} %get-tuple-element.77), channel_id=1, source_target_pairs={{0,16},{8,24},{16,0},{24,8},{1,17},{9,25},{17,1},{25,9},{2,18},{10... | collective-permute-start | bytes 3342344 | tf_op jit(solution)/shard_map/ppermute | solution.py:756
  682.3 90.3 %reduce-scatter.6.cloned.1.call-start = ((), (), s32[]{:S(2)}) async-start(), calls=%async_computation.8 | async-start | bytes 2359296 | tf_op jit(solution)/shard_map/reduce_scatter | solution.py:766
  698.2 84.0 %collective-permute-start.38 = (bf16[256,1408]{1,0:T(8,128)(2,1)}, bf16[256,1408]{1,0:T(8,128)(2,1)S(1)}, u32[]{:S(2)}, u32[]{:S(2)}) collective-permute-start(bf16[256,1408]{1,0:T(8,128)(2,1)} %reduce-scatter.12.cloned.1.call-done.refs_0_), channel_id=1, source_target_pairs={{0,8},{8,0},{16,24},{24,16},{1,9},{9,1},{17,25},{25,17},{2,10},{10... | collective-permute-start | bytes 2162696 | tf_op jit(solution)/shard_map/ppermute | solution.py:756
  706.5 75.6 %collective-permute-start.39 = (bf16[256,1408]{1,0:T(8,128)(2,1)}, bf16[256,1408]{1,0:T(8,128)(2,1)S(1)}, u32[]{:S(2)}, u32[]{:S(2)}) collective-permute-start(bf16[256,1408]{1,0:T(8,128)(2,1)} %reduce-scatter.12.cloned.1.call-done.refs_0_), channel_id=1, source_target_pairs={{0,16},{8,24},{16,0},{24,8},{1,17},{9,25},{17,1},{25,9},{2,18},{10... | collective-permute-start | bytes 2162696 | tf_op jit(solution)/shard_map/ppermute | solution.py:756
  716.3 65.9 %collective-permute-start.40 = (bf16[256,1408]{1,0:T(8,128)(2,1)}, bf16[256,1408]{1,0:T(8,128)(2,1)S(1)}, u32[]{:S(2)}, u32[]{:S(2)}) collective-permute-start(bf16[256,1408]{1,0:T(8,128)(2,1)} %reduce-scatter.12.cloned.1.call-done.refs_0_), channel_id=1, source_target_pairs={{0,24},{8,16},{16,8},{24,0},{1,25},{9,17},{17,9},{25,1},{2,26},{10... | collective-permute-start | bytes 2162696 | tf_op jit(solution)/shard_map/ppermute | solution.py:756
  720.1 58.3 %collective-permute-start.42 = (bf16[512,512]{1,0:T(8,128)(2,1)}, bf16[512,512]{1,0:T(8,128)(2,1)}, u32[]{:S(2)}, u32[]{:S(2)}) collective-permute-start(bf16[512,512]{1,0:T(8,128)(2,1)} %reduce-scatter.14.cloned.1.call-done.refs_0_), channel_id=1, source_target_pairs={{0,16},{8,24},{16,0},{24,8},{1,17},{9,25},{17,1},{25,9},{2,18},{10... | collective-permute-start | bytes 1572872 | tf_op jit(solution)/shard_map/ppermute | solution.py:756
  729.1 49.2 %collective-permute-start.43 = (bf16[512,512]{1,0:T(8,128)(2,1)}, bf16[512,512]{1,0:T(8,128)(2,1)}, u32[]{:S(2)}, u32[]{:S(2)}) collective-permute-start(bf16[512,512]{1,0:T(8,128)(2,1)} %reduce-scatter.14.cloned.1.call-done.refs_0_), channel_id=1, source_target_pairs={{0,24},{8,16},{16,8},{24,0},{1,25},{9,17},{17,9},{25,1},{2,26},{10... | collective-permute-start | bytes 1572872 | tf_op jit(solution)/shard_map/ppermute | solution.py:756
  (90 other events, 1561.3 us)
Sparse Core Ops, SparseCore 0:
  10.8 60.1 all-gather.4
  73.1 45.9 all-gather.6
  160.8 86.1 all-gather.8
  436.4 85.2 reduce-scatter.9
  523.1 57.4 all-gather.10
  583.3 48.7 reduce-scatter.13
  634.9 63.2 reduce-scatter.11
  701.0 34.7 reduce-scatter.7
  738.1 34.5 reduce-scatter.5
